TPU v7x, 32 devices: a whole 2x2x4 slice. The times are simulated.
32 devices in a mesh: depth: 8 (over z, y), batch: 4 (over x, core).
Axes of the slice: x: 2, y: 2, z: 4, core: 2. Of those that a mesh axis runs over, the one named last changes fastest.
Arguments:
- iterate: float32 [8, 8, 16, 16, 256], P('depth', 'batch'), may hold values from -70 to 70
- weights: bfloat16 [32, 3, 3, 256, 256], P('depth'), may hold values from -0.125 to 0.125
- norm_scale: float32 [32, 256], P('depth'), may hold values from 0.5 to 2
- norm_shift: float32 [32, 256], P('depth'), may hold values from -3 to 3
Outputs:
- block_ends: float32 [8, 8, 16, 16, 256], P('depth', 'batch')
All inputs are finite; a program needn't handle non-finite values.
Results may differ from a plain program's by a relative error of at most 0.0018.
Values sent between devices are 32-bit elements; how exact they have to be, the bound alone decides.
No kernel may reach another device: no remote copies, remote signals or barrier semaphores. Data moves between devices by JAX's collectives and lax.ppermute only.
A program may use at most 64 MiB of HBM per device.

v0:
```python
import functools
import jax
import jax.numpy as jnp
from jax import lax
from jax.experimental import pallas as pl
from jax.experimental.pallas import tpu as pltpu
from jax.sharding import PartitionSpec as P

fine_step = 0.125
coarse_step = 0.5
epsilon = 1e-05
layers_of_block = 4
vmem_bytes = 16 << 20


whole = pl.BlockSpec(memory_space=pltpu.VMEM)
in_place = pl.BlockSpec(memory_space=pltpu.HBM)


def call(
    body, operands, outs, scratch=(), specs=None, out_specs=None, aliases=None,
    flops=0, moved=0,
):
    return pl.pallas_call(
        body,
        out_shape=outs,
        in_specs=[whole] * len(operands) if specs is None else specs,
        out_specs=jax.tree.map(lambda _: whole, outs) if out_specs is None else out_specs,
        scratch_shapes=list(scratch),
        input_output_aliases=aliases or {},
        compiler_params=pltpu.CompilerParams(vmem_limit_bytes=vmem_bytes),
        cost_estimate=pl.CostEstimate(flops=flops, bytes_accessed=moved, transcendentals=0),
    )(*operands)


def f32(*shape):
    return jax.ShapeDtypeStruct(shape, jnp.float32)


def lay_out(activated, taps, width, above=True, below=True):
    entries, channels = activated.shape
    column = lax.broadcasted_iota(jnp.int32, (entries, 1), 0) % width
    before = jnp.where(column == 0, 0.0, pltpu.roll(activated, 1, 0))
    after = jnp.where(column == width - 1, 0.0, pltpu.roll(activated, entries - 1, 0))
    edge = jnp.zeros((width, 3 * channels), jnp.bfloat16)
    start = width if above else 0
    if above:
        taps[0:width] = edge
    if below:
        taps[start + entries : start + entries + width] = edge
    for place, values in enumerate((before, activated, after)):
        taps[start : start + entries, place * channels : (place + 1) * channels] = values.astype(
            jnp.bfloat16
        )


def convolved(taps, kernel, width, entries):
    total = jnp.dot(taps[0:entries], kernel(0), preferred_element_type=jnp.float32)
    for row in (1, 2):
        total += jnp.dot(
            taps[row * width : row * width + entries],
            kernel(row),
            preferred_element_type=jnp.float32,
        )
    return total


def both_sums(values):
    return jnp.concatenate(
        [jnp.sum(values, axis=0, keepdims=True), jnp.sum(values * values, axis=0, keepdims=True)],
        axis=0,
    )


def spans(cuts, rows):
    edges = (0, *cuts, rows)
    return list(zip(edges, edges[1:]))


def sums_kernel(state, sums):
    samples, rows, width, channels = state.shape
    total = jnp.zeros((2, channels), jnp.float32)
    for i in range(samples):
        total += both_sums(state[i].reshape(rows * width, channels))
    sums[...] = total


def copy_kernel(*refs):
    refs[-1][...] = refs[0][...]


def statistics(totals, entries):
    center = totals[0:1] * (1.0 / entries)
    return center, lax.rsqrt(totals[1:2] * (1.0 / entries) - center * center + epsilon)


def layer_kernel(number, parts, batch_entries, kind, cut, *refs):
    state, weights, gains, offsets = refs[:4]
    totals = refs[4 : 4 + parts]
    refs = refs[4 + parts :]
    position = lax.axis_index("depth")
    if kind == "first":
        initial, initial_totals = refs[0], refs[1 : 1 + lax.axis_size("batch")]
        outs, taps = refs[1 + len(initial_totals) : -1], refs[-1]
    elif kind == "last":
        coarse_begin, terms = refs[:2]
        outs, taps = refs[2:-1], refs[-1]
    else:
        outs, taps = refs[:-1], refs[-1]
    samples, rows, width, channels = state.shape
    entries = rows * width

    def load(i):
        values = state[i]
        if kind == "first":
            values = jnp.where(position == 0, initial[i], values)
        return values.reshape(entries, channels)

    def added(pieces):
        summed = pieces[0][...]
        for piece in pieces[1:]:
            summed = summed + piece[...]
        return summed

    summed = added(totals)
    if kind == "first":
        summed = jnp.where(position == 0, added(initial_totals), summed)
    center, inverse = statistics(summed, batch_entries)
    scale = gains[number : number + 1] * inverse
    offset = offsets[number : number + 1]
    for i in range(samples):
        lay_out(jnp.maximum((load(i) - center) * scale + offset, 0.0), taps.at[i], width)
    total = jnp.zeros((2, channels), jnp.float32)
    for i in range(samples):
        change = convolved(taps.at[i], lambda row: weights[number, row], width, entries)
        values = load(i)
        made = values + fine_step * change
        if kind == "last":
            begun = coarse_begin[i].reshape(entries, channels)
            forcing = made - begun
            outs[0][i] = (begun + forcing).reshape(rows, width, channels)
            outs[1][i] = forcing
        else:
            outs[0][i] = made.reshape(rows, width, channels)
            total += both_sums(made)
            if kind == "first":
                outs[2][i] = (values + coarse_step * change).reshape(rows, width, channels)
    if kind == "last":
        half = samples // 2
        other = (1 - position % 2) * half
        for i in range(half):
            sent = jnp.where(
                position == 1, outs[0][other + i].reshape(entries, channels), outs[1][other + i]
            )
            for (low, high), out in zip(spans(cut, rows), outs[2:]):
                size = (high - low) * width
                out[i * size : (i + 1) * size] = sent[low * width : high * width]
        outs[2][half * cut[0] * width :] = terms[...]
    else:
        outs[1][...] = total
    if kind == "first":
        outs[3][...] = jnp.concatenate(
            [center, scale, offset, jnp.zeros((5, channels), jnp.float32)], axis=0
        )


def layer(number, state, weights, gains, offsets, totals, batch_entries, kind, extra=(), cut=None):
    samples, rows, width, channels = state.shape
    entries = rows * width
    half = samples // 2
    if kind == "last":
        outs = (
            f32(*state.shape),
            f32(samples, entries, channels),
            *(
                f32(half * (high - low) * width + (8 if low == 0 else 0), channels)
                for low, high in spans(cut, rows)
            ),
        )
    else:
        outs = (f32(*state.shape), f32(2, channels))
        if kind == "first":
            outs += (f32(*state.shape), f32(8, channels))
    return call(
        functools.partial(layer_kernel, number, len(totals), batch_entries, kind, cut),
        (state, weights, gains, offsets, *totals, *extra),
        outs,
        [pltpu.VMEM((samples, entries + 2 * width, 3 * channels), jnp.bfloat16)],
        flops=2 * samples * entries * 9 * channels * channels,
        moved=4 * samples * entries * channels,
    )


def widen_kernel(part, weights, after, out, held, done):
    piece = out.shape[0] // 3
    at = pl.multiple_of((lax.axis_index("batch") % 2) * 2 * piece + part * piece, piece)
    copy = pltpu.make_async_copy(weights.at[0, :, pl.ds(at, piece)], held, done)
    copy.start()
    copy.wait()
    for row in range(3):
        out[row * piece : (row + 1) * piece] = held[row].astype(jnp.float32)


def widen(part, weights, after):
    inner, channels = weights.shape[2:]
    piece = inner // 4
    return call(
        functools.partial(widen_kernel, part),
        (weights, after),
        f32(3 * piece, channels),
        [pltpu.VMEM((3, piece, channels), jnp.bfloat16), pltpu.SemaphoreType.DMA],
        specs=[in_place, whole],
        moved=3 * piece * channels * 6,
    )


def gather_kernel(weights, near_upper, near_lower, far_upper, far_lower, out):
    parity, core = lax.axis_index("depth") % 2, lax.axis_index("batch") % 2
    piece = near_upper.shape[0] // 3
    out[parity] = weights[0]
    for part, pieces in enumerate(((near_upper, far_upper), (near_lower, far_lower))):
        for owner, source in ((core, pieces[0]), (1 - core, pieces[1])):
            at = pl.multiple_of(owner * 2 * piece + part * piece, piece)
            for row in range(3):
                values = source[row * piece : (row + 1) * piece]
                out[1 - parity, row, pl.ds(at, piece)] = values.astype(jnp.bfloat16)


def relay_kernel(low, high, received, early, out):
    half, rows, width, channels = out.shape
    entries = rows * width
    odd = lax.axis_index("depth") % 2 == 1
    for i in range(half):
        passed = received[i * entries : (i + 1) * entries].reshape(rows, width, channels)
        out[i] = jnp.where(odd, early[half + i, low:high], passed)


def pair_kernel(turn, piece, cuts, start_cuts, kept, out_cuts, last, *refs):
    refs, taps = list(refs[:-1]), refs[-1]
    take = lambda count: [refs.pop(0) for _ in range(count)]
    pieces = len(cuts) + 1
    is_last = piece is None or piece == pieces - 1
    if piece is None:
        incoming, halo = take(pieces), []
    elif piece == 0:
        incoming, halo = take(1), []
    else:
        incoming, halo = take(2), take(1)
    exchange = take(pieces if piece is None else piece + 1)
    forcing, terms, kernels = take(3)
    take(1 + len(kept))
    gives = {low_high: ref for low_high, ref in zip(kept, refs[len(refs) - len(kept) :])}
    own = refs[len(refs) - len(kept) - 1]
    made = refs[: len(refs) - len(kept) - 1]
    half, height, width, channels = own.shape
    position = lax.axis_index("depth")
    parity = position % 2

    def flat(values):
        return values.reshape(-1, channels)

    def joined(values):
        return values[0] if len(values) == 1 else jnp.concatenate(values, axis=0)

    def forced(stage, i, low, high):
        here = forcing[parity * half + i, low * width : high * width]
        there = []
        for (first, end), ref in zip(spans(start_cuts, height), exchange):
            a, b = max(low, first), min(high, end)
            if a < b:
                base = i * (end - first) - first
                there.append(ref[(base + a) * width : (base + b) * width])
        return jnp.where(parity == stage, here, joined(there))

    def mapped(stage, i, values, begin, low, high):
        base = half * start_cuts[0] * width
        center, scale, offset = (
            jnp.where(parity == stage, terms[n : n + 1], exchange[0][base + n : base + n + 1])
            for n in range(3)
        )
        lay_out(
            jnp.maximum((values - center) * scale + offset, 0.0),
            taps.at[i, stage],
            width,
            low == 0,
            high == height,
        )
        change = convolved(
            taps.at[i, stage], lambda row: kernels[stage, row], width, (high - low) * width
        )
        kept_values = values[(low - begin) * width : (high - begin) * width]
        return kept_values + coarse_step * change + forced(stage, i, low, high)

    def put(i, low, values, is_own):
        high = low + values.shape[0] // width
        values = values.reshape(high - low, width, channels)
        if is_own:
            own[i, low:high] = values
            return
        for (first, end), ref in gives.items():
            a, b = max(low, first), min(high, end)
            if a < b:
                ref[i, a - first : b - first] = values[a - low : b - low]

    @pl.when(position // 2 == turn)
    def _():
        for i in range(half):
            if halo:
                cut = cuts[piece - 1]
                low = (cut - 1, cut - 2)
                values = joined([flat(incoming[0][i, -2:]), flat(incoming[1][i])])
                begin = (cut - 2, cut - 3)
            else:
                low, begin = (0, 0), (0, 0)
                values = joined([flat(part[i]) for part in incoming])
            high = (height, height) if is_last else (cuts[piece] - 1, cuts[piece] - 2)
            first = mapped(0, i, values, begin[0], low[0], high[0])
            values = joined([flat(halo[0][i, -2:]), first]) if halo else first
            second = mapped(1, i, values, begin[1], low[1], high[1])
            outs = list(made)
            if not is_last:
                outs.pop(0)[i] = first.reshape(-1, width, channels)
            if not last:
                for a, b in spans(out_cuts, height) if piece is None else [(low[1], high[1])]:
                    at = slice((a - low[1]) * width, (b - low[1]) * width)
                    outs.pop(0)[i] = second[at].reshape(-1, width, channels)

            @pl.when(parity == 0)
            def _():
                put(i, low[0], first, True)
                put(i, low[1], second, False)

            @pl.when(parity == 1)
            def _():
                put(i, low[0], first, False)
                put(i, low[1], second, True)


def pair(turn, piece, cuts, start_cuts, out_cuts, last, incoming, exchange, shared, own, gives):
    half, height, width, channels = own.shape
    pieces = len(cuts) + 1
    is_last = piece is None or piece == pieces - 1
    rows = lambda low, high: f32(half, high - low, width, channels)
    made = []
    if not is_last:
        low = cuts[piece - 1] - 1 if piece else 0
        made.append(rows(low, cuts[piece] - 1))
    if not last:
        if piece is None:
            made += [rows(*span) for span in spans(out_cuts, height)]
        else:
            made.append(rows(*spans(out_cuts, height)[piece]))
    kept = tuple(gives)
    carried = (own, *gives.values())
    operands = (*incoming, *exchange, *shared, *carried)
    count = len(operands) - len(carried)
    entries = half * height * width // pieces
    outs = call(
        functools.partial(pair_kernel, turn, piece, cuts, start_cuts, kept, out_cuts, last),
        operands,
        tuple(made) + tuple(f32(*part.shape) for part in carried),
        [pltpu.VMEM((half, 2, (height + 2) * width, 3 * channels), jnp.bfloat16)],
        aliases={count + n: len(made) + n for n in range(len(carried))},
        flops=4 * entries * 9 * channels * channels,
        moved=8 * entries * channels,
    )
    rest = outs[len(made) :]
    return outs[: len(made)], rest[0], dict(zip(kept, rest[1:]))


def finish_own_kernel(early, own, out, done):
    half = own.shape[0]
    position = lax.axis_index("depth")

    @pl.when(position < 2)
    def _():
        copy = pltpu.make_async_copy(early, out, done)
        copy.start()
        copy.wait()

    @pl.when(position >= 2)
    def _():
        copy = pltpu.make_async_copy(own, out.at[pl.ds((position % 2) * half, half)], done)
        copy.start()
        copy.wait()


def finish_kernel(cuts, *refs):
    pieces, out, done = refs[: len(cuts) + 1], refs[-2], refs[-1]
    half = pieces[0].shape[0]
    position = lax.axis_index("depth")

    @pl.when(position >= 2)
    def _():
        there = pl.ds((1 - position % 2) * half, half)
        copies = [
            pltpu.make_async_copy(piece, out.at[there, low:high], done.at[n])
            for n, (piece, (low, high)) in enumerate(zip(pieces, spans(cuts, out.shape[1])))
        ]
        for copy in copies:
            copy.start()
        for copy in copies:
            copy.wait()


def turns_of(count, height):
    start = (height // 2, height * 7 // 8)
    plan, cuts = [], start
    for _ in range(count):
        split = cuts[0] >= 3
        plan.append((cuts, split, tuple(cut - 2 for cut in cuts) if split else start))
        cuts = plan[-1][2]
    return start, plan


def steps(iterate, weights, norm_scale, norm_shift):
    initial = iterate[0]
    samples, rows, width, channels = initial.shape
    half = samples // 2
    devices = lax.axis_size("depth")
    group = lax.axis_size("batch")
    batch_entries = samples * rows * width * group
    weights = weights.reshape(layers_of_block, 3, 3 * channels, channels)
    run = functools.partial(layer, batch_entries=batch_entries)

    def gathered(sums, mark=False, ready=()):
        others = [
            lax.ppermute(sums, "batch", [(i, i ^ m) for i in range(group)])
            for m in range(1, group)
        ]
        if mark:
            sums = call(copy_kernel, (sums, *ready), f32(*sums.shape))
        return (sums, *others)

    partners = [(i, i ^ 1) for i in range(devices)]
    cores = [(i, i ^ 1) for i in range(group)]
    onward = [(i, i + 1) for i in range(devices - 1)]

    sums = call(sums_kernel, (initial,), f32(2, channels), moved=initial.size * 4)
    first_totals = gathered(sums, True, (weights, norm_scale, norm_shift))
    norms = (weights, norm_scale, norm_shift)
    current, totals = initial, first_totals
    for number in range(layers_of_block):
        current, sums = run(number, current, *norms, totals, kind="plain")
        if number == 0:
            near_upper = lax.ppermute(widen(0, weights, sums), "depth", partners)
        totals = gathered(sums, number == 0)
    arrived = lax.ppermute(current, "depth", onward)
    arrived_totals = lax.ppermute(sum(totals[1:], totals[0]), "depth", onward)

    start, plan = turns_of(devices // 2 - 1, rows)
    current, sums, coarse_begin, terms = run(
        0, arrived, *norms, (arrived_totals,), kind="first", extra=(initial, *first_totals)
    )
    near_lower = lax.ppermute(widen(1, weights, sums), "depth", partners)
    far_upper = lax.ppermute(near_upper, "batch", cores)
    for number in range(1, layers_of_block - 1):
        totals = gathered(sums, number == 1)
        current, sums = run(number, current, *norms, totals, kind="plain")
    far_lower = lax.ppermute(near_lower, "batch", cores)
    early, forcing, *sent = run(
        layers_of_block - 1,
        current,
        *norms,
        gathered(sums, True),
        kind="last",
        extra=(coarse_begin, terms),
        cut=start,
    )
    kernels = call(
        gather_kernel,
        (weights, near_upper, near_lower, far_upper, far_lower),
        jax.ShapeDtypeStruct((2, 3, 3 * channels, channels), jnp.bfloat16),
        moved=9 * channels * channels * 8,
    )

    exchange = [lax.ppermute(part, "depth", partners) for part in sent]
    passed = [
        call(
            functools.partial(relay_kernel, low, high),
            (part, early),
            f32(half, high - low, width, channels),
            moved=half * (high - low) * width * channels * 8,
        )
        for part, (low, high) in zip(exchange, spans(start, rows))
    ]
    own = jnp.zeros((half, rows, width, channels), jnp.float32)
    gives = {
        (low, high): jnp.zeros((half, high - low, width, channels), jnp.float32)
        for low, high in spans(plan[-1][2], rows)
    }
    back_spans = list(gives)
    back = []
    shared = (forcing, terms, kernels)
    for turn, (cuts, split, out_cuts) in enumerate(plan, 1):
        across = {2 * turn - 2: 2 * turn, 2 * turn - 1: 2 * turn + 1}
        across.update({b: a for a, b in across.items()})
        route = [(i, across.get(i, i ^ 1)) for i in range(devices)]
        arriving = [lax.ppermute(part, "depth", route) for part in passed]
        last = turn == len(plan)
        if not split:
            passed, own, gives = pair(
                turn, None, cuts, start, out_cuts, last, arriving, exchange, shared, own, gives
            )
            continue
        passed, halo = [], ()
        for n in range(len(cuts) + 1):
            incoming = (*arriving[max(n - 1, 0) : n + 1], *halo)
            now = {span: gives[span] for span in back_spans[n : n + 2]} if last else gives
            made, own, now = pair(
                turn,
                n,
                cuts,
                start,
                out_cuts,
                last,
                incoming,
                exchange[: n + 1],
                shared,
                own,
                now,
            )
            gives = {**gives, **now}
            halo = tuple(made[:1]) if n < len(cuts) else ()
            if last:
                back.append(lax.ppermute(gives[back_spans[n]], "depth", partners))
            else:
                passed.append(made[-1])
    if not back:
        back = [lax.ppermute(part, "depth", partners) for part in gives.values()]
    out = call(
        finish_own_kernel,
        (early, own),
        f32(*initial.shape),
        [pltpu.SemaphoreType.DMA],
        out_specs=in_place,
        moved=initial.size * 8,
    )
    out = call(
        functools.partial(finish_kernel, plan[-1][2]),
        (*back, out),
        f32(*initial.shape),
        [pltpu.SemaphoreType.DMA((len(back),))],
        specs=[whole] * len(back) + [in_place],
        out_specs=in_place,
        aliases={len(back): 0},
        moved=initial.size * 4,
    )
    return out[None]


def solution(mesh):
    return jax.shard_map(
        steps,
        mesh=mesh,
        in_specs=(
            P("depth", "batch", None, None, None),
            P("depth", None, None, None, None),
            P("depth", None),
            P("depth", None),
        ),
        out_specs=P("depth", "batch", None, None, None),
        check_vma=False,
    )
```

profile of v0, /device:TPU:24, one launch (start us, length us, event | category | flops | bytes accessed | tf_op | source)
XLA Modules:
  0.0 120.9 jit_solution(7662833167876272210)
XLA Ops:
  0.0 1.0 copy-done.2
  1.2 1.6 %collective-permute-start.1 = (f32[2,256]{1,0:T(2,128)S(1)}, f32[2,256]{1,0:T(2,128)S(1)}, u32[]{:S(2)}, u32[]{:S(2)}) collective-permute-start(f32[2,256]{1,0:T(2,128)S(1)} %shard_map.46.refs_0_), channel_id=1, source_target_pairs={{0,2},{1,3},{2,0},{3,1},{4,6},{5,7},{6,4},{7,5},{8,10},{9,11},{10,... | collective-permute-start | bytes 6152 | tf_op jit(solution)/shard_map/ppermute | solution.py:428
  3.0 2.3 %copy-done = bf16[4,3,3,256,256]{4,3,2,1,0:T(8,128)(2,1)S(1)} copy-done((bf16[4,3,3,256,256]{4,3,2,1,0:T(8,128)(2,1)S(1)}, bf16[4,3,3,256,256]{4,3,2,1,0:T(8,128)(2,1)}, u32[]{:S(2)}) %copy-start) | copy-done | bytes 4718616
  6.8 2.3 %copy-done.1 = bf16[4,3,3,256,256]{4,3,2,1,0:T(8,128)(2,1)S(1)} copy-done((bf16[4,3,3,256,256]{4,3,2,1,0:T(8,128)(2,1)S(1)}, bf16[4,3,3,256,256]{4,3,2,1,0:T(8,128)(2,1)}, u32[]{:S(2)}) %copy-start.1) | copy-done | bytes 4718616
  9.1 0.9 shard_map.48
  10.4 1.5 %collective-permute-start.4 = (f32[2,256]{1,0:T(2,128)S(1)}, f32[2,256]{1,0:T(2,128)S(1)}, u32[]{:S(2)}, u32[]{:S(2)}) collective-permute-start(f32[2,256]{1,0:T(2,128)S(1)} %get-tuple-element.71.refs_0_.after), channel_id=1, source_target_pairs={{0,2},{1,3},{2,0},{3,1},{4,6},{5,7},{6,4},{7,5},{8,10},{9,11},{10,... | collective-permute-start | bytes 6152 | tf_op jit(solution)/shard_map/ppermute | solution.py:428
  11.9 2.1 %collective-permute-done.4.refs_6_ = f32[2,256]{1,0:T(2,128)S(1)} collective-permute-done((f32[2,256]{1,0:T(2,128)S(1)}, f32[2,256]{1,0:T(2,128)S(1)}, u32[]{:S(2)}, u32[]{:S(2)}) %collective-permute-start.4) | collective-permute-done | bytes 2080 | tf_op jit(solution)/shard_map/ppermute | solution.py:428
  14.0 0.9 collective-permute-done.5.refs_7_
  14.9 0.9 shard_map.50
  16.5 1.2 collective-permute-start.8
  17.7 1.9 %collective-permute-done.7.refs_6_ = f32[2,256]{1,0:T(2,128)S(1)} collective-permute-done((f32[2,256]{1,0:T(2,128)S(1)}, f32[2,256]{1,0:T(2,128)S(1)}, u32[]{:S(2)}, u32[]{:S(2)}) %collective-permute-start.7) | collective-permute-done | bytes 2080 | tf_op jit(solution)/shard_map/ppermute | solution.py:428
  19.5 0.9 shard_map.51
  20.4 1.5 %collective-permute-start.10 = (f32[2,256]{1,0:T(2,128)S(1)}, f32[2,256]{1,0:T(2,128)S(1)}, u32[]{:S(2)}, u32[]{:S(2)}) collective-permute-start(f32[2,256]{1,0:T(2,128)S(1)} %get-tuple-element.75.refs_4_), channel_id=1, source_target_pairs={{0,2},{1,3},{2,0},{3,1},{4,6},{5,7},{6,4},{7,5},{8,10},{9,11},{10,... | collective-permute-start | bytes 6152 | tf_op jit(solution)/shard_map/ppermute | solution.py:428
  22.6 1.4 %collective-permute-done.10.refs_6_ = f32[2,256]{1,0:T(2,128)S(1)} collective-permute-done((f32[2,256]{1,0:T(2,128)S(1)}, f32[2,256]{1,0:T(2,128)S(1)}, u32[]{:S(2)}, u32[]{:S(2)}) %collective-permute-start.10) | collective-permute-done | bytes 2080 | tf_op jit(solution)/shard_map/ppermute | solution.py:428
  24.0 0.9 collective-permute-done.11.refs_7_
  24.9 0.9 shard_map.52
  25.8 3.4 %collective-permute-start.12 = (f32[2,16,16,256]{3,2,1,0:T(8,128)S(1)}, f32[2,16,16,256]{3,2,1,0:T(8,128)S(1)}, u32[]{:S(2)}, u32[]{:S(2)}) collective-permute-start(f32[2,16,16,256]{3,2,1,0:T(8,128)S(1)} %get-tuple-element.76), channel_id=1, source_target_pairs={{0,4},{4,8},{8,12},{12,16},{16,20},{20,24},{24,28},{1,5},{5,9},{9,... | collective-permute-start | bytes 1572872 | tf_op jit(solution)/shard_map/ppermute | solution.py:448
  29.9 1.2 collective-permute-start.15
  31.1 1.8 %collective-permute-done.14 = f32[2,256]{1,0:T(2,128)S(1)} collective-permute-done((f32[2,256]{1,0:T(2,128)S(1)}, f32[2,256]{1,0:T(2,128)S(1)}, u32[]{:S(2)}, u32[]{:S(2)}) %collective-permute-start.14) | collective-permute-done | bytes 2080 | tf_op jit(solution)/shard_map/ppermute | solution.py:428
  33.0 1.9 %collective-permute-start.16 = (f32[2,256]{1,0:T(2,128)S(1)}, f32[2,256]{1,0:T(2,128)S(1)}, u32[]{:S(2)}, u32[]{:S(2)}) collective-permute-start(f32[2,256]{1,0:T(2,128)S(1)} %add_add_fusion), channel_id=1, source_target_pairs={{0,4},{4,8},{8,12},{12,16},{16,20},{20,24},{24,28},{1,5},{5,9},{9,... | collective-permute-start | bytes 6152 | tf_op jit(solution)/shard_map/ppermute | solution.py:449
  35.1 7.6 %collective-permute-done.16.refs_4_ = f32[2,256]{1,0:T(2,128)S(1)} collective-permute-done((f32[2,256]{1,0:T(2,128)S(1)}, f32[2,256]{1,0:T(2,128)S(1)}, u32[]{:S(2)}, u32[]{:S(2)}) %collective-permute-start.16) | collective-permute-done | bytes 2080 | tf_op jit(solution)/shard_map/ppermute | solution.py:449
  42.7 0.9 shard_map.53
  43.7 1.4 %collective-permute-start.29 = (f32[576,256]{1,0:T(8,128)S(1)}, f32[576,256]{1,0:T(8,128)S(1)}, u32[]{:S(2)}, u32[]{:S(2)}) collective-permute-start(f32[576,256]{1,0:T(8,128)S(1)} %shard_map.61), channel_id=1, source_target_pairs={{0,4},{4,0},{8,12},{12,8},{16,20},{20,16},{24,28},{28,24},{1,5},{5... | collective-permute-start | bytes 1769480 | tf_op jit(solution)/shard_map/ppermute | solution.py:455
  45.1 10.1 %collective-permute-done.28.near_upper = f32[576,256]{1,0:T(8,128)S(1)} collective-permute-done((f32[576,256]{1,0:T(8,128)S(1)}, f32[576,256]{1,0:T(8,128)S(1)}, u32[]{:S(2)}, u32[]{:S(2)}) %collective-permute-start.28) | collective-permute-done | bytes 589856 | tf_op jit(solution)/shard_map/ppermute | solution.py:446
  55.3 12.6 %collective-permute-done.29.near_lower = f32[576,256]{1,0:T(8,128)S(1)} collective-permute-done((f32[576,256]{1,0:T(8,128)S(1)}, f32[576,256]{1,0:T(8,128)S(1)}, u32[]{:S(2)}, u32[]{:S(2)}) %collective-permute-start.29) | collective-permute-done | bytes 589856 | tf_op jit(solution)/shard_map/ppermute | solution.py:455
  69.8 2.1 %collective-permute-done.18.refs_6_ = f32[2,256]{1,0:T(2,128)S(1)} collective-permute-done((f32[2,256]{1,0:T(2,128)S(1)}, f32[2,256]{1,0:T(2,128)S(1)}, u32[]{:S(2)}, u32[]{:S(2)}) %collective-permute-start.18) | collective-permute-done | bytes 2080 | tf_op jit(solution)/shard_map/ppermute | solution.py:428
  72.0 0.9 shard_map.55
  73.0 1.4 %collective-permute-start.21 = (f32[2,256]{1,0:T(2,128)S(1)}, f32[2,256]{1,0:T(2,128)S(1)}, u32[]{:S(2)}, u32[]{:S(2)}) collective-permute-start(f32[2,256]{1,0:T(2,128)S(1)} %get-tuple-element.81.refs_4_), channel_id=1, source_target_pairs={{0,2},{1,3},{2,0},{3,1},{4,6},{5,7},{6,4},{7,5},{8,10},{9,11},{10,... | collective-permute-start | bytes 6152 | tf_op jit(solution)/shard_map/ppermute | solution.py:428
  74.8 1.8 %collective-permute-done.21.refs_6_ = f32[2,256]{1,0:T(2,128)S(1)} collective-permute-done((f32[2,256]{1,0:T(2,128)S(1)}, f32[2,256]{1,0:T(2,128)S(1)}, u32[]{:S(2)}, u32[]{:S(2)}) %collective-permute-start.21) | collective-permute-done | bytes 2080 | tf_op jit(solution)/shard_map/ppermute | solution.py:428
  77.4 0.9 shard_map.56
  79.1 1.1 collective-permute-start.25
  80.2 1.9 %collective-permute-done.24.refs_6_ = f32[2,256]{1,0:T(2,128)S(1)} collective-permute-done((f32[2,256]{1,0:T(2,128)S(1)}, f32[2,256]{1,0:T(2,128)S(1)}, u32[]{:S(2)}, u32[]{:S(2)}) %collective-permute-start.24) | collective-permute-done | bytes 2080 | tf_op jit(solution)/shard_map/ppermute | solution.py:428
  82.1 1.0 shard_map.58
  83.8 1.4 %collective-permute-start.33 = (f32[96,256]{1,0:T(8,128)S(1)}, f32[96,256]{1,0:T(8,128)S(1)}, u32[]{:S(2)}, u32[]{:S(2)}) collective-permute-start(f32[96,256]{1,0:T(8,128)S(1)} %get-tuple-element.90), channel_id=1, source_target_pairs={{0,4},{4,0},{8,12},{12,8},{16,20},{20,16},{24,28},{28,24},{1,5},{5... | collective-permute-start | bytes 294920 | tf_op jit(solution)/shard_map/ppermute | solution.py:477
  85.2 4.5 %collective-permute-done.26.received.refs_1_.refs_3_ = f32[136,256]{1,0:T(8,128)S(1)} collective-permute-done((f32[136,256]{1,0:T(8,128)S(1)}, f32[136,256]{1,0:T(8,128)S(1)}, u32[]{:S(2)}, u32[]{:S(2)}) %collective-permute-start.26) | collective-permute-done | bytes 139296 | tf_op jit(solution)/shard_map/ppermute | solution.py:477
  91.9 1.3 %collective-permute-start.35 = (f32[32,256]{1,0:T(8,128)S(1)}, f32[32,256]{1,0:T(8,128)S(1)}, u32[]{:S(2)}, u32[]{:S(2)}) collective-permute-start(f32[32,256]{1,0:T(8,128)S(1)} %get-tuple-element.91), channel_id=1, source_target_pairs={{0,4},{4,0},{8,12},{12,8},{16,20},{20,16},{24,28},{28,24},{1,5},{5... | collective-permute-start | bytes 98312 | tf_op jit(solution)/shard_map/ppermute | solution.py:477
  93.2 3.9 %collective-permute-done.35.received.refs_5_ = f32[32,256]{1,0:T(8,128)S(1)} collective-permute-done((f32[32,256]{1,0:T(8,128)S(1)}, f32[32,256]{1,0:T(8,128)S(1)}, u32[]{:S(2)}, u32[]{:S(2)}) %collective-permute-start.35) | collective-permute-done | bytes 32800 | tf_op jit(solution)/shard_map/ppermute | solution.py:477
  98.2 1.4 %collective-permute-start.38 = (f32[1,6,16,256]{3,2,1,0:T(8,128)S(1)}, f32[1,6,16,256]{3,2,1,0:T(8,128)S(1)}, u32[]{:S(2)}, u32[]{:S(2)}) collective-permute-start(f32[1,6,16,256]{3,2,1,0:T(8,128)S(1)} %get-tuple-element.107), channel_id=1, source_target_pairs={{0,4},{4,0},{8,16},{12,20},{16,8},{20,12},{24,28},{28,24},{1,5},{5... | collective-permute-start | bytes 294920 | tf_op jit(solution)/shard_map/ppermute | solution.py:499
  100.2 3.7 %collective-permute-done.36.refs_1_ = f32[1,2,16,256]{3,2,1,0:T(8,128)S(1)} collective-permute-done((f32[1,2,16,256]{3,2,1,0:T(8,128)S(1)}, f32[1,2,16,256]{3,2,1,0:T(8,128)S(1)}, u32[]{:S(2)}, u32[]{:S(2)}) %collective-permute-start.36) | collective-permute-done | bytes 32800 | tf_op jit(solution)/shard_map/ppermute | solution.py:499
  103.8 1.3 %collective-permute-start.39 = (f32[1,4,16,256]{3,2,1,0:T(8,128)S(1)}, f32[1,4,16,256]{3,2,1,0:T(8,128)S(1)}, u32[]{:S(2)}, u32[]{:S(2)}) collective-permute-start(f32[1,4,16,256]{3,2,1,0:T(8,128)S(1)} %get-tuple-element.108), channel_id=1, source_target_pairs={{0,4},{4,0},{8,16},{12,20},{16,8},{20,12},{24,28},{28,24},{1,5},{5... | collective-permute-start | bytes 196616 | tf_op jit(solution)/shard_map/ppermute | solution.py:499
  105.1 1.9 %collective-permute-start.37 = (f32[1,4,16,256]{3,2,1,0:T(8,128)S(1)}, f32[1,4,16,256]{3,2,1,0:T(8,128)S(1)}, u32[]{:S(2)}, u32[]{:S(2)}) collective-permute-start(f32[1,4,16,256]{3,2,1,0:T(8,128)S(1)} %get-tuple-element.106), channel_id=1, source_target_pairs={{0,4},{4,0},{8,12},{12,8},{16,24},{20,28},{24,16},{28,20},{1,5},{5... | collective-permute-start | bytes 196616 | tf_op jit(solution)/shard_map/ppermute | solution.py:499
  107.0 1.1 collective-permute-start.41
  108.1 1.9 %collective-permute-start.43 = (f32[1,6,16,256]{3,2,1,0:T(8,128)S(1)}, f32[1,6,16,256]{3,2,1,0:T(8,128)S(1)}, u32[]{:S(2)}, u32[]{:S(2)}) collective-permute-start(f32[1,6,16,256]{3,2,1,0:T(8,128)S(1)} %get-tuple-element.129), channel_id=1, source_target_pairs={{0,4},{4,0},{8,12},{12,8},{16,24},{20,28},{24,16},{28,20},{1,5},{5... | collective-permute-start | bytes 294920 | tf_op jit(solution)/shard_map/ppermute | solution.py:499
  111.6 0.8 shard_map.72
  112.7 0.9 shard_map.73
  113.6 1.3 %collective-permute-start.44 = (f32[1,8,16,256]{3,2,1,0:T(8,128)S(1)}, f32[1,8,16,256]{3,2,1,0:T(8,128)S(1)}, u32[]{:S(2)}, u32[]{:S(2)}) collective-permute-start(f32[1,8,16,256]{3,2,1,0:T(8,128)S(1)} %get-tuple-element.133), channel_id=1, source_target_pairs={{0,4},{4,0},{8,12},{12,8},{16,20},{20,16},{24,28},{28,24},{1,5},{5... | collective-permute-start | bytes 393224 | tf_op jit(solution)/shard_map/ppermute | solution.py:526
  115.7 1.3 %collective-permute-start.40 = (f32[1,2,16,256]{3,2,1,0:T(8,128)S(1)}, f32[1,2,16,256]{3,2,1,0:T(8,128)S(1)}, u32[]{:S(2)}, u32[]{:S(2)}) collective-permute-start(f32[1,2,16,256]{3,2,1,0:T(8,128)S(1)} %get-tuple-element.122), channel_id=1, source_target_pairs={{0,4},{4,0},{8,12},{12,8},{16,20},{20,16},{24,28},{28,24},{1,5},{5... | collective-permute-start | bytes 98312 | tf_op jit(solution)/shard_map/ppermute | solution.py:526
  117.7 2.4 %collective-permute-done.40.refs_0_ = f32[1,2,16,256]{3,2,1,0:T(8,128)S(1)} collective-permute-done((f32[1,2,16,256]{3,2,1,0:T(8,128)S(1)}, f32[1,2,16,256]{3,2,1,0:T(8,128)S(1)}, u32[]{:S(2)}, u32[]{:S(2)}) %collective-permute-start.40) | collective-permute-done | bytes 32800 | tf_op jit(solution)/shard_map/ppermute | solution.py:526
  (93 shorter events, 17.6 us)
Async XLA Ops:
  1.0 5.8 %copy-start.3 = (f32[1,2,16,16,256]{4,3,2,1,0:T(8,128)S(1)}, f32[1,2,16,16,256]{4,3,2,1,0:T(8,128)}, u32[]{:S(2)}) copy-start(f32[1,2,16,16,256]{4,3,2,1,0:T(8,128)} %param.4) | copy-start | bytes 1572868
  1.1 5.7 %collective-permute-start = (f32[2,256]{1,0:T(2,128)S(1)}, f32[2,256]{1,0:T(2,128)S(1)}, u32[]{:S(2)}, u32[]{:S(2)}) collective-permute-start(f32[2,256]{1,0:T(2,128)S(1)} %shard_map.46.refs_0_), channel_id=1, source_target_pairs={{0,1},{1,0},{2,3},{3,2},{4,5},{5,4},{6,7},{7,6},{8,9},{9,8},{10,11... | collective-permute-start | bytes 6152 | tf_op jit(solution)/shard_map/ppermute | solution.py:428
  1.2 5.6 %collective-permute-start.1 = (f32[2,256]{1,0:T(2,128)S(1)}, f32[2,256]{1,0:T(2,128)S(1)}, u32[]{:S(2)}, u32[]{:S(2)}) collective-permute-start(f32[2,256]{1,0:T(2,128)S(1)} %shard_map.46.refs_0_), channel_id=1, source_target_pairs={{0,2},{1,3},{2,0},{3,1},{4,6},{5,7},{6,4},{7,5},{8,10},{9,11},{10,... | collective-permute-start | bytes 6152 | tf_op jit(solution)/shard_map/ppermute | solution.py:428
  2.7 4.0 %collective-permute-start.2 = (f32[2,256]{1,0:T(2,128)S(1)}, f32[2,256]{1,0:T(2,128)S(1)}, u32[]{:S(2)}, u32[]{:S(2)}) collective-permute-start(f32[2,256]{1,0:T(2,128)S(1)} %shard_map.46.refs_0_), channel_id=1, source_target_pairs={{0,3},{1,2},{2,1},{3,0},{4,7},{5,6},{6,5},{7,4},{8,11},{9,10},{10,... | collective-permute-start | bytes 6152 | tf_op jit(solution)/shard_map/ppermute | solution.py:428
  6.8 8.1 %copy-start.5 = (f32[4,256]{1,0:T(4,128)S(1)}, f32[4,256]{1,0:T(4,128)}, u32[]{:S(2)}) copy-start(f32[4,256]{1,0:T(4,128)} %refs_2_.17) | copy-start | bytes 12292
  6.8 12.8 %copy-start.7 = (f32[4,256]{1,0:T(4,128)S(1)}, f32[4,256]{1,0:T(4,128)}, u32[]{:S(2)}) copy-start(f32[4,256]{1,0:T(4,128)} %refs_3_.17) | copy-start | bytes 12292
  9.9 1.9 %collective-permute-start.3 = (f32[2,256]{1,0:T(2,128)S(1)}, f32[2,256]{1,0:T(2,128)S(1)}, u32[]{:S(2)}, u32[]{:S(2)}) collective-permute-start(f32[2,256]{1,0:T(2,128)S(1)} %get-tuple-element.71.refs_0_.after), channel_id=1, source_target_pairs={{0,1},{1,0},{2,3},{3,2},{4,5},{5,4},{6,7},{7,6},{8,9},{9,8},{10,11... | collective-permute-start | bytes 6152 | tf_op jit(solution)/shard_map/ppermute | solution.py:428
  10.4 3.6 %collective-permute-start.4 = (f32[2,256]{1,0:T(2,128)S(1)}, f32[2,256]{1,0:T(2,128)S(1)}, u32[]{:S(2)}, u32[]{:S(2)}) collective-permute-start(f32[2,256]{1,0:T(2,128)S(1)} %get-tuple-element.71.refs_0_.after), channel_id=1, source_target_pairs={{0,2},{1,3},{2,0},{3,1},{4,6},{5,7},{6,4},{7,5},{8,10},{9,11},{10,... | collective-permute-start | bytes 6152 | tf_op jit(solution)/shard_map/ppermute | solution.py:428
  11.9 3.0 %collective-permute-start.5 = (f32[2,256]{1,0:T(2,128)S(1)}, f32[2,256]{1,0:T(2,128)S(1)}, u32[]{:S(2)}, u32[]{:S(2)}) collective-permute-start(f32[2,256]{1,0:T(2,128)S(1)} %get-tuple-element.71.refs_0_.after), channel_id=1, source_target_pairs={{0,3},{1,2},{2,1},{3,0},{4,7},{5,6},{6,5},{7,4},{8,11},{9,10},{10,... | collective-permute-start | bytes 6152 | tf_op jit(solution)/shard_map/ppermute | solution.py:428
  15.7 1.9 %collective-permute-start.6 = (f32[2,256]{1,0:T(2,128)S(1)}, f32[2,256]{1,0:T(2,128)S(1)}, u32[]{:S(2)}, u32[]{:S(2)}) collective-permute-start(f32[2,256]{1,0:T(2,128)S(1)} %get-tuple-element.73.refs_4_), channel_id=1, source_target_pairs={{0,1},{1,0},{2,3},{3,2},{4,5},{5,4},{6,7},{7,6},{8,9},{9,8},{10,11... | collective-permute-start | bytes 6152 | tf_op jit(solution)/shard_map/ppermute | solution.py:428
  15.9 3.6 %collective-permute-start.7 = (f32[2,256]{1,0:T(2,128)S(1)}, f32[2,256]{1,0:T(2,128)S(1)}, u32[]{:S(2)}, u32[]{:S(2)}) collective-permute-start(f32[2,256]{1,0:T(2,128)S(1)} %get-tuple-element.73.refs_4_), channel_id=1, source_target_pairs={{0,2},{1,3},{2,0},{3,1},{4,6},{5,7},{6,4},{7,5},{8,10},{9,11},{10,... | collective-permute-start | bytes 6152 | tf_op jit(solution)/shard_map/ppermute | solution.py:428
  16.5 3.0 %collective-permute-start.8 = (f32[2,256]{1,0:T(2,128)S(1)}, f32[2,256]{1,0:T(2,128)S(1)}, u32[]{:S(2)}, u32[]{:S(2)}) collective-permute-start(f32[2,256]{1,0:T(2,128)S(1)} %get-tuple-element.73.refs_4_), channel_id=1, source_target_pairs={{0,3},{1,2},{2,1},{3,0},{4,7},{5,6},{6,5},{7,4},{8,11},{9,10},{10,... | collective-permute-start | bytes 6152 | tf_op jit(solution)/shard_map/ppermute | solution.py:428
  20.4 3.7 %collective-permute-start.10 = (f32[2,256]{1,0:T(2,128)S(1)}, f32[2,256]{1,0:T(2,128)S(1)}, u32[]{:S(2)}, u32[]{:S(2)}) collective-permute-start(f32[2,256]{1,0:T(2,128)S(1)} %get-tuple-element.75.refs_4_), channel_id=1, source_target_pairs={{0,2},{1,3},{2,0},{3,1},{4,6},{5,7},{6,4},{7,5},{8,10},{9,11},{10,... | collective-permute-start | bytes 6152 | tf_op jit(solution)/shard_map/ppermute | solution.py:428
  21.9 3.0 %collective-permute-start.11 = (f32[2,256]{1,0:T(2,128)S(1)}, f32[2,256]{1,0:T(2,128)S(1)}, u32[]{:S(2)}, u32[]{:S(2)}) collective-permute-start(f32[2,256]{1,0:T(2,128)S(1)} %get-tuple-element.75.refs_4_), channel_id=1, source_target_pairs={{0,3},{1,2},{2,1},{3,0},{4,7},{5,6},{6,5},{7,4},{8,11},{9,10},{10,... | collective-permute-start | bytes 6152 | tf_op jit(solution)/shard_map/ppermute | solution.py:428
  21.9 3.0 %collective-permute-start.9 = (f32[2,256]{1,0:T(2,128)S(1)}, f32[2,256]{1,0:T(2,128)S(1)}, u32[]{:S(2)}, u32[]{:S(2)}) collective-permute-start(f32[2,256]{1,0:T(2,128)S(1)} %get-tuple-element.75.refs_4_), channel_id=1, source_target_pairs={{0,1},{1,0},{2,3},{3,2},{4,5},{5,4},{6,7},{7,6},{8,9},{9,8},{10,11... | collective-permute-start | bytes 6152 | tf_op jit(solution)/shard_map/ppermute | solution.py:428
  25.8 16.9 %collective-permute-start.12 = (f32[2,16,16,256]{3,2,1,0:T(8,128)S(1)}, f32[2,16,16,256]{3,2,1,0:T(8,128)S(1)}, u32[]{:S(2)}, u32[]{:S(2)}) collective-permute-start(f32[2,16,16,256]{3,2,1,0:T(8,128)S(1)} %get-tuple-element.76), channel_id=1, source_target_pairs={{0,4},{4,8},{8,12},{12,16},{16,20},{20,24},{24,28},{1,5},{5,9},{9,... | collective-permute-start | bytes 1572872 | tf_op jit(solution)/shard_map/ppermute | solution.py:448
  29.2 1.9 %collective-permute-start.13 = (f32[2,256]{1,0:T(2,128)S(1)}, f32[2,256]{1,0:T(2,128)S(1)}, u32[]{:S(2)}, u32[]{:S(2)}) collective-permute-start(f32[2,256]{1,0:T(2,128)S(1)} %get-tuple-element.77), channel_id=1, source_target_pairs={{0,1},{1,0},{2,3},{3,2},{4,5},{5,4},{6,7},{7,6},{8,9},{9,8},{10,11... | collective-permute-start | bytes 6152 | tf_op jit(solution)/shard_map/ppermute | solution.py:428
  29.3 3.7 %collective-permute-start.14 = (f32[2,256]{1,0:T(2,128)S(1)}, f32[2,256]{1,0:T(2,128)S(1)}, u32[]{:S(2)}, u32[]{:S(2)}) collective-permute-start(f32[2,256]{1,0:T(2,128)S(1)} %get-tuple-element.77), channel_id=1, source_target_pairs={{0,2},{1,3},{2,0},{3,1},{4,6},{5,7},{6,4},{7,5},{8,10},{9,11},{10,... | collective-permute-start | bytes 6152 | tf_op jit(solution)/shard_map/ppermute | solution.py:428
  29.9 3.0 %collective-permute-start.15 = (f32[2,256]{1,0:T(2,128)S(1)}, f32[2,256]{1,0:T(2,128)S(1)}, u32[]{:S(2)}, u32[]{:S(2)}) collective-permute-start(f32[2,256]{1,0:T(2,128)S(1)} %get-tuple-element.77), channel_id=1, source_target_pairs={{0,3},{1,2},{2,1},{3,0},{4,7},{5,6},{6,5},{7,4},{8,11},{9,10},{10,... | collective-permute-start | bytes 6152 | tf_op jit(solution)/shard_map/ppermute | solution.py:428
  33.0 9.7 %collective-permute-start.16 = (f32[2,256]{1,0:T(2,128)S(1)}, f32[2,256]{1,0:T(2,128)S(1)}, u32[]{:S(2)}, u32[]{:S(2)}) collective-permute-start(f32[2,256]{1,0:T(2,128)S(1)} %add_add_fusion), channel_id=1, source_target_pairs={{0,4},{4,8},{8,12},{12,16},{16,20},{20,24},{24,28},{1,5},{5,9},{9,... | collective-permute-start | bytes 6152 | tf_op jit(solution)/shard_map/ppermute | solution.py:449
  35.0 20.3 %collective-permute-start.28 = (f32[576,256]{1,0:T(8,128)S(1)}, f32[576,256]{1,0:T(8,128)S(1)}, u32[]{:S(2)}, u32[]{:S(2)}) collective-permute-start(f32[576,256]{1,0:T(8,128)S(1)} %shard_map.60), channel_id=1, source_target_pairs={{0,4},{4,0},{8,12},{12,8},{16,20},{20,16},{24,28},{28,24},{1,5},{5... | collective-permute-start | bytes 1769480 | tf_op jit(solution)/shard_map/ppermute | solution.py:446
  43.7 24.1 %collective-permute-start.29 = (f32[576,256]{1,0:T(8,128)S(1)}, f32[576,256]{1,0:T(8,128)S(1)}, u32[]{:S(2)}, u32[]{:S(2)}) collective-permute-start(f32[576,256]{1,0:T(8,128)S(1)} %shard_map.61), channel_id=1, source_target_pairs={{0,4},{4,0},{8,12},{12,8},{16,20},{20,16},{24,28},{28,24},{1,5},{5... | collective-permute-start | bytes 1769480 | tf_op jit(solution)/shard_map/ppermute | solution.py:455
  55.2 41.9 %collective-permute-start.30 = (f32[576,256]{1,0:T(8,128)S(1)}, f32[576,256]{1,0:T(8,128)S(1)}, u32[]{:S(2)}, u32[]{:S(2)}) collective-permute-start(f32[576,256]{1,0:T(8,128)S(1)} %collective-permute-done.28.near_upper), channel_id=1, source_target_pairs={{0,1},{1,0},{2,3},{3,2},{4,5},{5,4},{6,7},{7,6},{8,9},{9,8},{10,11... | collective-permute-start | bytes 1769480 | tf_op jit(solution)/shard_map/ppermute | solution.py:456
  67.8 29.3 %collective-permute-start.31 = (f32[576,256]{1,0:T(8,128)S(1)}, f32[576,256]{1,0:T(8,128)S(1)}, u32[]{:S(2)}, u32[]{:S(2)}) collective-permute-start(f32[576,256]{1,0:T(8,128)S(1)} %collective-permute-done.29.near_lower), channel_id=1, source_target_pairs={{0,1},{1,0},{2,3},{3,2},{4,5},{5,4},{6,7},{7,6},{8,9},{9,8},{10,11... | collective-permute-start | bytes 1769480 | tf_op jit(solution)/shard_map/ppermute | solution.py:460
  67.9 1.9 %collective-permute-start.17 = (f32[2,256]{1,0:T(2,128)S(1)}, f32[2,256]{1,0:T(2,128)S(1)}, u32[]{:S(2)}, u32[]{:S(2)}) collective-permute-start(f32[2,256]{1,0:T(2,128)S(1)} %get-tuple-element.79.refs_0_.after), channel_id=1, source_target_pairs={{0,1},{1,0},{2,3},{3,2},{4,5},{5,4},{6,7},{7,6},{8,9},{9,8},{10,11... | collective-permute-start | bytes 6152 | tf_op jit(solution)/shard_map/ppermute | solution.py:428
  68.3 3.6 %collective-permute-start.18 = (f32[2,256]{1,0:T(2,128)S(1)}, f32[2,256]{1,0:T(2,128)S(1)}, u32[]{:S(2)}, u32[]{:S(2)}) collective-permute-start(f32[2,256]{1,0:T(2,128)S(1)} %get-tuple-element.79.refs_0_.after), channel_id=1, source_target_pairs={{0,2},{1,3},{2,0},{3,1},{4,6},{5,7},{6,4},{7,5},{8,10},{9,11},{10,... | collective-permute-start | bytes 6152 | tf_op jit(solution)/shard_map/ppermute | solution.py:428
  68.9 3.0 %collective-permute-start.19 = (f32[2,256]{1,0:T(2,128)S(1)}, f32[2,256]{1,0:T(2,128)S(1)}, u32[]{:S(2)}, u32[]{:S(2)}) collective-permute-start(f32[2,256]{1,0:T(2,128)S(1)} %get-tuple-element.79.refs_0_.after), channel_id=1, source_target_pairs={{0,3},{1,2},{2,1},{3,0},{4,7},{5,6},{6,5},{7,4},{8,11},{9,10},{10,... | collective-permute-start | bytes 6152 | tf_op jit(solution)/shard_map/ppermute | solution.py:428
  72.8 1.9 %collective-permute-start.20 = (f32[2,256]{1,0:T(2,128)S(1)}, f32[2,256]{1,0:T(2,128)S(1)}, u32[]{:S(2)}, u32[]{:S(2)}) collective-permute-start(f32[2,256]{1,0:T(2,128)S(1)} %get-tuple-element.81.refs_4_), channel_id=1, source_target_pairs={{0,1},{1,0},{2,3},{3,2},{4,5},{5,4},{6,7},{7,6},{8,9},{9,8},{10,11... | collective-permute-start | bytes 6152 | tf_op jit(solution)/shard_map/ppermute | solution.py:428
  73.0 3.6 %collective-permute-start.21 = (f32[2,256]{1,0:T(2,128)S(1)}, f32[2,256]{1,0:T(2,128)S(1)}, u32[]{:S(2)}, u32[]{:S(2)}) collective-permute-start(f32[2,256]{1,0:T(2,128)S(1)} %get-tuple-element.81.refs_4_), channel_id=1, source_target_pairs={{0,2},{1,3},{2,0},{3,1},{4,6},{5,7},{6,4},{7,5},{8,10},{9,11},{10,... | collective-permute-start | bytes 6152 | tf_op jit(solution)/shard_map/ppermute | solution.py:428
  74.4 3.0 %collective-permute-start.22 = (f32[2,256]{1,0:T(2,128)S(1)}, f32[2,256]{1,0:T(2,128)S(1)}, u32[]{:S(2)}, u32[]{:S(2)}) collective-permute-start(f32[2,256]{1,0:T(2,128)S(1)} %get-tuple-element.81.refs_4_), channel_id=1, source_target_pairs={{0,3},{1,2},{2,1},{3,0},{4,7},{5,6},{6,5},{7,4},{8,11},{9,10},{10,... | collective-permute-start | bytes 6152 | tf_op jit(solution)/shard_map/ppermute | solution.py:428
  78.3 1.9 %collective-permute-start.23 = (f32[2,256]{1,0:T(2,128)S(1)}, f32[2,256]{1,0:T(2,128)S(1)}, u32[]{:S(2)}, u32[]{:S(2)}) collective-permute-start(f32[2,256]{1,0:T(2,128)S(1)} %get-tuple-element.83.refs_0_), channel_id=1, source_target_pairs={{0,1},{1,0},{2,3},{3,2},{4,5},{5,4},{6,7},{7,6},{8,9},{9,8},{10,11... | collective-permute-start | bytes 6152 | tf_op jit(solution)/shard_map/ppermute | solution.py:428
  78.5 3.6 %collective-permute-start.24 = (f32[2,256]{1,0:T(2,128)S(1)}, f32[2,256]{1,0:T(2,128)S(1)}, u32[]{:S(2)}, u32[]{:S(2)}) collective-permute-start(f32[2,256]{1,0:T(2,128)S(1)} %get-tuple-element.83.refs_0_), channel_id=1, source_target_pairs={{0,2},{1,3},{2,0},{3,1},{4,6},{5,7},{6,4},{7,5},{8,10},{9,11},{10,... | collective-permute-start | bytes 6152 | tf_op jit(solution)/shard_map/ppermute | solution.py:428
  79.1 3.0 %collective-permute-start.25 = (f32[2,256]{1,0:T(2,128)S(1)}, f32[2,256]{1,0:T(2,128)S(1)}, u32[]{:S(2)}, u32[]{:S(2)}) collective-permute-start(f32[2,256]{1,0:T(2,128)S(1)} %get-tuple-element.83.refs_0_), channel_id=1, source_target_pairs={{0,3},{1,2},{2,1},{3,0},{4,7},{5,6},{6,5},{7,4},{8,11},{9,10},{10,... | collective-permute-start | bytes 6152 | tf_op jit(solution)/shard_map/ppermute | solution.py:428
  83.1 6.6 %collective-permute-start.26 = (f32[136,256]{1,0:T(8,128)S(1)}, f32[136,256]{1,0:T(8,128)S(1)}, u32[]{:S(2)}, u32[]{:S(2)}) collective-permute-start(f32[136,256]{1,0:T(8,128)S(1)} %get-tuple-element.86), channel_id=1, source_target_pairs={{0,4},{4,0},{8,12},{12,8},{16,20},{20,16},{24,28},{28,24},{1,5},{5... | collective-permute-start | bytes 417800 | tf_op jit(solution)/shard_map/ppermute | solution.py:477
  83.8 7.3 %collective-permute-start.33 = (f32[96,256]{1,0:T(8,128)S(1)}, f32[96,256]{1,0:T(8,128)S(1)}, u32[]{:S(2)}, u32[]{:S(2)}) collective-permute-start(f32[96,256]{1,0:T(8,128)S(1)} %get-tuple-element.90), channel_id=1, source_target_pairs={{0,4},{4,0},{8,12},{12,8},{16,20},{20,16},{24,28},{28,24},{1,5},{5... | collective-permute-start | bytes 294920 | tf_op jit(solution)/shard_map/ppermute | solution.py:477
  89.7 7.6 %collective-permute-start.27 = (f32[1,8,16,256]{3,2,1,0:T(8,128)S(1)}, f32[1,8,16,256]{3,2,1,0:T(8,128)S(1)}, u32[]{:S(2)}, u32[]{:S(2)}) collective-permute-start(f32[1,8,16,256]{3,2,1,0:T(8,128)S(1)} %shard_map.59), channel_id=1, source_target_pairs={{0,8},{4,12},{8,0},{12,4},{16,20},{20,16},{24,28},{28,24},{1,9},{5... | collective-permute-start | bytes 393224 | tf_op jit(solution)/shard_map/ppermute | solution.py:499
  91.1 7.0 %collective-permute-start.34 = (f32[1,6,16,256]{3,2,1,0:T(8,128)S(1)}, f32[1,6,16,256]{3,2,1,0:T(8,128)S(1)}, u32[]{:S(2)}, u32[]{:S(2)}) collective-permute-start(f32[1,6,16,256]{3,2,1,0:T(8,128)S(1)} %shard_map.64), channel_id=1, source_target_pairs={{0,8},{4,12},{8,0},{12,4},{16,20},{20,16},{24,28},{28,24},{1,9},{5... | collective-permute-start | bytes 294920 | tf_op jit(solution)/shard_map/ppermute | solution.py:499
  91.9 5.2 %collective-permute-start.35 = (f32[32,256]{1,0:T(8,128)S(1)}, f32[32,256]{1,0:T(8,128)S(1)}, u32[]{:S(2)}, u32[]{:S(2)}) collective-permute-start(f32[32,256]{1,0:T(8,128)S(1)} %get-tuple-element.91), channel_id=1, source_target_pairs={{0,4},{4,0},{8,12},{12,8},{16,20},{20,16},{24,28},{28,24},{1,5},{5... | collective-permute-start | bytes 98312 | tf_op jit(solution)/shard_map/ppermute | solution.py:477
  97.5 7.7 %collective-permute-start.32 = (f32[1,6,16,256]{3,2,1,0:T(8,128)S(1)}, f32[1,6,16,256]{3,2,1,0:T(8,128)S(1)}, u32[]{:S(2)}, u32[]{:S(2)}) collective-permute-start(f32[1,6,16,256]{3,2,1,0:T(8,128)S(1)} %get-tuple-element.89), channel_id=1, source_target_pairs={{0,4},{4,0},{8,16},{12,20},{16,8},{20,12},{24,28},{28,24},{1,5},{5... | collective-permute-start | bytes 294920 | tf_op jit(solution)/shard_map/ppermute | solution.py:499
  98.2 8.8 %collective-permute-start.38 = (f32[1,6,16,256]{3,2,1,0:T(8,128)S(1)}, f32[1,6,16,256]{3,2,1,0:T(8,128)S(1)}, u32[]{:S(2)}, u32[]{:S(2)}) collective-permute-start(f32[1,6,16,256]{3,2,1,0:T(8,128)S(1)} %get-tuple-element.107), channel_id=1, source_target_pairs={{0,4},{4,0},{8,16},{12,20},{16,8},{20,12},{24,28},{28,24},{1,5},{5... | collective-permute-start | bytes 294920 | tf_op jit(solution)/shard_map/ppermute | solution.py:499
  99.6 4.3 %collective-permute-start.36 = (f32[1,2,16,256]{3,2,1,0:T(8,128)S(1)}, f32[1,2,16,256]{3,2,1,0:T(8,128)S(1)}, u32[]{:S(2)}, u32[]{:S(2)}) collective-permute-start(f32[1,2,16,256]{3,2,1,0:T(8,128)S(1)} %shard_map.65), channel_id=1, source_target_pairs={{0,8},{4,12},{8,0},{12,4},{16,20},{20,16},{24,28},{28,24},{1,9},{5... | collective-permute-start | bytes 98312 | tf_op jit(solution)/shard_map/ppermute | solution.py:499
  103.8 4.3 %collective-permute-start.39 = (f32[1,4,16,256]{3,2,1,0:T(8,128)S(1)}, f32[1,4,16,256]{3,2,1,0:T(8,128)S(1)}, u32[]{:S(2)}, u32[]{:S(2)}) collective-permute-start(f32[1,4,16,256]{3,2,1,0:T(8,128)S(1)} %get-tuple-element.108), channel_id=1, source_target_pairs={{0,4},{4,0},{8,16},{12,20},{16,8},{20,12},{24,28},{28,24},{1,5},{5... | collective-permute-start | bytes 196616 | tf_op jit(solution)/shard_map/ppermute | solution.py:499
  105.1 4.9 %collective-permute-start.37 = (f32[1,4,16,256]{3,2,1,0:T(8,128)S(1)}, f32[1,4,16,256]{3,2,1,0:T(8,128)S(1)}, u32[]{:S(2)}, u32[]{:S(2)}) collective-permute-start(f32[1,4,16,256]{3,2,1,0:T(8,128)S(1)} %get-tuple-element.106), channel_id=1, source_target_pairs={{0,4},{4,0},{8,12},{12,8},{16,24},{20,28},{24,16},{28,20},{1,5},{5... | collective-permute-start | bytes 196616 | tf_op jit(solution)/shard_map/ppermute | solution.py:499
  107.0 4.6 %collective-permute-start.41 = (f32[1,6,16,256]{3,2,1,0:T(8,128)S(1)}, f32[1,6,16,256]{3,2,1,0:T(8,128)S(1)}, u32[]{:S(2)}, u32[]{:S(2)}) collective-permute-start(f32[1,6,16,256]{3,2,1,0:T(8,128)S(1)} %get-tuple-element.123), channel_id=1, source_target_pairs={{0,4},{4,0},{8,12},{12,8},{16,24},{20,28},{24,16},{28,20},{1,5},{5... | collective-permute-start | bytes 294920 | tf_op jit(solution)/shard_map/ppermute | solution.py:499
  108.1 4.6 %collective-permute-start.43 = (f32[1,6,16,256]{3,2,1,0:T(8,128)S(1)}, f32[1,6,16,256]{3,2,1,0:T(8,128)S(1)}, u32[]{:S(2)}, u32[]{:S(2)}) collective-permute-start(f32[1,6,16,256]{3,2,1,0:T(8,128)S(1)} %get-tuple-element.129), channel_id=1, source_target_pairs={{0,4},{4,0},{8,12},{12,8},{16,24},{20,28},{24,16},{28,20},{1,5},{5... | collective-permute-start | bytes 294920 | tf_op jit(solution)/shard_map/ppermute | solution.py:499
  113.6 6.4 %collective-permute-start.44 = (f32[1,8,16,256]{3,2,1,0:T(8,128)S(1)}, f32[1,8,16,256]{3,2,1,0:T(8,128)S(1)}, u32[]{:S(2)}, u32[]{:S(2)}) collective-permute-start(f32[1,8,16,256]{3,2,1,0:T(8,128)S(1)} %get-tuple-element.133), channel_id=1, source_target_pairs={{0,4},{4,0},{8,12},{12,8},{16,20},{20,16},{24,28},{28,24},{1,5},{5... | collective-permute-start | bytes 393224 | tf_op jit(solution)/shard_map/ppermute | solution.py:526
  114.9 5.1 %collective-permute-start.42 = (f32[1,6,16,256]{3,2,1,0:T(8,128)S(1)}, f32[1,6,16,256]{3,2,1,0:T(8,128)S(1)}, u32[]{:S(2)}, u32[]{:S(2)}) collective-permute-start(f32[1,6,16,256]{3,2,1,0:T(8,128)S(1)} %get-tuple-element.128), channel_id=1, source_target_pairs={{0,4},{4,0},{8,12},{12,8},{16,20},{20,16},{24,28},{28,24},{1,5},{5... | collective-permute-start | bytes 294920 | tf_op jit(solution)/shard_map/ppermute | solution.py:526
  115.7 4.3 %collective-permute-start.40 = (f32[1,2,16,256]{3,2,1,0:T(8,128)S(1)}, f32[1,2,16,256]{3,2,1,0:T(8,128)S(1)}, u32[]{:S(2)}, u32[]{:S(2)}) collective-permute-start(f32[1,2,16,256]{3,2,1,0:T(8,128)S(1)} %get-tuple-element.122), channel_id=1, source_target_pairs={{0,4},{4,0},{8,12},{12,8},{16,20},{20,16},{24,28},{28,24},{1,5},{5... | collective-permute-start | bytes 98312 | tf_op jit(solution)/shard_map/ppermute | solution.py:526
  (5 other events, 7.1 us)
where the time goes:
time: 122 us; the launch traced here: 121 us
  waiting for transfers between devices  62.2 us (51%)
  starting transfers between devices  39.6 us (32%)
  Pallas kernels  11.5 us (9%)
  local copies, waits for them, and re-layouts  7.09 us (6%)
    ppermute x24, waiting for transfers between devices, gathered(): lax.ppermute(sums, 'batch', [(i, i ^ m) for i in range(group)])  15.7 us
    ppermute x24, starting transfers between devices, gathered(): lax.ppermute(sums, 'batch', [(i, i ^ m) for i in range(group)])  15.6 us
    ppermute x1, waiting for transfers between devices, steps(): near_lower = lax.ppermute(widen(1, weights, sums), 'depth', partners)  12.6 us
    pallas_call x30, Pallas kernels, call(): pl.pallas_call(body, out_shape=outs, in_specs=[whole] * len(operands) if...  11.5 us
    ppermute x9, starting transfers between devices, steps(): arriving = [lax.ppermute(part, 'depth', route) for part in passed]  10.3 us
    ppermute x1, waiting for transfers between devices, steps(): near_upper = lax.ppermute(widen(0, weights, sums), 'depth', partners)  10.1 us
    ppermute x3, waiting for transfers between devices, steps(): exchange = [lax.ppermute(part, 'depth', partners) for part in sent]  9.09 us
    ppermute x1, waiting for transfers between devices, steps(): arrived_totals = lax.ppermute(sum(totals[1:], totals[0]), 'depth', onward)  7.6 us
  transfers between devices with their start and end apart: 45, of which 22 were waited for; matrix products, arithmetic and copies ran while one was open for 0% of the time, Pallas kernels for 5%

commit v1 on v0

--- a/solution.py
+++ b/solution.py
@@ -19,7 +19,7 @@
 
 def call(
     body, operands, outs, scratch=(), specs=None, out_specs=None, aliases=None,
-    flops=0, moved=0,
+    flops=0, moved=0, limit=vmem_bytes,
 ):
     return pl.pallas_call(
         body,
@@ -28,7 +28,7 @@
         out_specs=jax.tree.map(lambda _: whole, outs) if out_specs is None else out_specs,
         scratch_shapes=list(scratch),
         input_output_aliases=aliases or {},
-        compiler_params=pltpu.CompilerParams(vmem_limit_bytes=vmem_bytes),
+        compiler_params=pltpu.CompilerParams(vmem_limit_bytes=limit),
         cost_estimate=pl.CostEstimate(flops=flops, bytes_accessed=moved, transcendentals=0),
     )(*operands)
 
@@ -94,10 +94,11 @@
     return center, lax.rsqrt(totals[1:2] * (1.0 / entries) - center * center + epsilon)
 
 
-def layer_kernel(number, parts, batch_entries, kind, cut, *refs):
-    state, weights, gains, offsets = refs[:4]
-    totals = refs[4 : 4 + parts]
-    refs = refs[4 + parts :]
+def layer_kernel(number, count, keep, parts, batch_entries, kind, cut, *refs):
+    states, refs = refs[:count], refs[count:]
+    weights, gains, offsets = refs[:3]
+    totals = refs[3 : 3 + parts]
+    refs = refs[3 + parts :]
     position = lax.axis_index("depth")
     if kind == "first":
         initial, initial_totals = refs[0], refs[1 : 1 + lax.axis_size("batch")]
@@ -107,11 +108,11 @@
         outs, taps = refs[2:-1], refs[-1]
     else:
         outs, taps = refs[:-1], refs[-1]
-    samples, rows, width, channels = state.shape
+    samples, rows, width, channels = states[0].shape
     entries = rows * width
 
     def load(i):
-        values = state[i]
+        values = states[i // samples][i % samples]
         if kind == "first":
             values = jnp.where(position == 0, initial[i], values)
         return values.reshape(entries, channels)
@@ -128,10 +129,10 @@
     center, inverse = statistics(summed, batch_entries)
     scale = gains[number : number + 1] * inverse
     offset = offsets[number : number + 1]
-    for i in range(samples):
+    for i in range(count * samples):
         lay_out(jnp.maximum((load(i) - center) * scale + offset, 0.0), taps.at[i], width)
     total = jnp.zeros((2, channels), jnp.float32)
-    for i in range(samples):
+    for i in range(count * samples):
         change = convolved(taps.at[i], lambda row: weights[number, row], width, entries)
         values = load(i)
         made = values + fine_step * change
@@ -141,7 +142,8 @@
             outs[0][i] = (begun + forcing).reshape(rows, width, channels)
             outs[1][i] = forcing
         else:
-            outs[0][i] = made.reshape(rows, width, channels)
+            if i < keep * samples:
+                outs[i // samples][i % samples] = made.reshape(rows, width, channels)
             total += both_sums(made)
             if kind == "first":
                 outs[2][i] = (values + coarse_step * change).reshape(rows, width, channels)
@@ -157,14 +159,15 @@
                 out[i * size : (i + 1) * size] = sent[low * width : high * width]
         outs[2][half * cut[0] * width :] = terms[...]
     else:
-        outs[1][...] = total
+        outs[keep][...] = total
     if kind == "first":
         outs[3][...] = jnp.concatenate(
             [center, scale, offset, jnp.zeros((5, channels), jnp.float32)], axis=0
         )
 
 
-def layer(number, state, weights, gains, offsets, totals, batch_entries, kind, extra=(), cut=None):
+def layer(number, states, weights, gains, offsets, totals, batch_entries, kind, extra=(), cut=None, keep=None):
+    state, keep = states[0], keep or len(states)
     samples, rows, width, channels = state.shape
     entries = rows * width
     half = samples // 2
@@ -178,27 +181,26 @@
             ),
         )
     else:
-        outs = (f32(*state.shape), f32(2, channels))
+        outs = (*(f32(*state.shape) for state in states[:keep]), f32(2, channels))
         if kind == "first":
             outs += (f32(*state.shape), f32(8, channels))
     return call(
-        functools.partial(layer_kernel, number, len(totals), batch_entries, kind, cut),
-        (state, weights, gains, offsets, *totals, *extra),
+        functools.partial(
+            layer_kernel, number, len(states), keep, len(totals), batch_entries, kind, cut
+        ),
+        (*states, weights, gains, offsets, *totals, *extra),
         outs,
-        [pltpu.VMEM((samples, entries + 2 * width, 3 * channels), jnp.bfloat16)],
-        flops=2 * samples * entries * 9 * channels * channels,
-        moved=4 * samples * entries * channels,
-    )
-
-
-def widen_kernel(part, weights, after, out, held, done):
+        [pltpu.VMEM((len(states) * samples, entries + 2 * width, 3 * channels), jnp.bfloat16)],
+        flops=2 * len(states) * samples * entries * 9 * channels * channels,
+        moved=4 * len(states) * samples * entries * channels,
+    )
+
+
+def widen_kernel(part, weights, after, out):
     piece = out.shape[0] // 3
     at = pl.multiple_of((lax.axis_index("batch") % 2) * 2 * piece + part * piece, piece)
-    copy = pltpu.make_async_copy(weights.at[0, :, pl.ds(at, piece)], held, done)
-    copy.start()
-    copy.wait()
     for row in range(3):
-        out[row * piece : (row + 1) * piece] = held[row].astype(jnp.float32)
+        out[row * piece : (row + 1) * piece] = weights[0, row, pl.ds(at, piece)].astype(jnp.float32)
 
 
 def widen(part, weights, after):
@@ -208,10 +210,18 @@
         functools.partial(widen_kernel, part),
         (weights, after),
         f32(3 * piece, channels),
-        [pltpu.VMEM((3, piece, channels), jnp.bfloat16), pltpu.SemaphoreType.DMA],
-        specs=[in_place, whole],
         moved=3 * piece * channels * 6,
     )
+
+
+def stage_kernel(weights, out, done):
+    copies = [
+        pltpu.make_async_copy(weights.at[n], out.at[n], done.at[n]) for n in range(out.shape[0])
+    ]
+    for copy in copies:
+        copy.start()
+    for copy in copies:
+        copy.wait()
 
 
 def gather_kernel(weights, near_upper, near_lower, far_upper, far_lower, out):
@@ -423,10 +433,10 @@
     weights = weights.reshape(layers_of_block, 3, 3 * channels, channels)
     run = functools.partial(layer, batch_entries=batch_entries)
 
-    def gathered(sums, mark=False, ready=()):
+    def gathered(sums, mark=False, chips=False, ready=()):
         others = [
             lax.ppermute(sums, "batch", [(i, i ^ m) for i in range(group)])
-            for m in range(1, group)
+            for m in (range(2, group, 2) if chips else range(1, group))
         ]
         if mark:
             sums = call(copy_kernel, (sums, *ready), f32(*sums.shape))
@@ -437,32 +447,48 @@
     onward = [(i, i + 1) for i in range(devices - 1)]
 
     sums = call(sums_kernel, (initial,), f32(2, channels), moved=initial.size * 4)
-    first_totals = gathered(sums, True, (weights, norm_scale, norm_shift))
+    first_totals = gathered(sums)
+    other = lax.ppermute(initial, "batch", cores)
+    weights = call(
+        stage_kernel,
+        (weights,),
+        jax.ShapeDtypeStruct(weights.shape, weights.dtype),
+        [pltpu.SemaphoreType.DMA((layers_of_block,))],
+        specs=[in_place],
+        moved=weights.size * 4,
+        limit=47 << 20,
+    )
     norms = (weights, norm_scale, norm_shift)
-    current, totals = initial, first_totals
-    for number in range(layers_of_block):
-        current, sums = run(number, current, *norms, totals, kind="plain")
+    states, totals = (initial, other), first_totals
+    for number in range(layers_of_block - 1):
+        keep = 2 if number < layers_of_block - 2 else 1
+        *states, sums = run(number, states, *norms, totals, kind="plain", keep=keep)
         if number == 0:
             near_upper = lax.ppermute(widen(0, weights, sums), "depth", partners)
-        totals = gathered(sums, number == 0)
+        totals = gathered(sums, number == 0, True)
+    current, sums = run(layers_of_block - 1, states[:1], *norms, totals, kind="plain")
+    totals = gathered(sums)
     arrived = lax.ppermute(current, "depth", onward)
     arrived_totals = lax.ppermute(sum(totals[1:], totals[0]), "depth", onward)
 
     start, plan = turns_of(devices // 2 - 1, rows)
     current, sums, coarse_begin, terms = run(
-        0, arrived, *norms, (arrived_totals,), kind="first", extra=(initial, *first_totals)
-    )
+        0, (arrived,), *norms, (arrived_totals,), kind="first", extra=(initial, *first_totals)
+    )
+    other = lax.ppermute(current, "batch", cores)
     near_lower = lax.ppermute(widen(1, weights, sums), "depth", partners)
     far_upper = lax.ppermute(near_upper, "batch", cores)
+    states = (current, other)
     for number in range(1, layers_of_block - 1):
-        totals = gathered(sums, number == 1)
-        current, sums = run(number, current, *norms, totals, kind="plain")
+        totals = gathered(sums, number == 2, number > 1)
+        keep = 2 if number < layers_of_block - 2 else 1
+        *states, sums = run(number, states, *norms, totals, kind="plain", keep=keep)
     far_lower = lax.ppermute(near_lower, "batch", cores)
     early, forcing, *sent = run(
         layers_of_block - 1,
-        current,
+        states[:1],
         *norms,
-        gathered(sums, True),
+        gathered(sums, True, True),
         kind="last",
         extra=(coarse_begin, terms),
         cut=start,

time: 122 us -> 116 us (0.951)
  Pallas kernels: 11.5 us -> 17.5 us
  local copies, waits for them, and re-layouts: 7.09 us -> 1.09 us
  starting transfers between devices: 39.6 us -> 35.3 us
    unnamed x16 -> x8, local copies, waits for them, and re-layouts: 7.05 us -> 1.05 us
    pallas_call x30, Pallas kernels: 11.5 us -> 17.5 us  [call(): pl.pallas_call(body, out_shape=outs, in_specs=[whole] * len(operands) if...]
    ppermute x1, waiting for transfers between devices: 7.6 us -> 4.41 us  [steps(): arrived_totals = lax.ppermute(sum(totals[1:], totals[0]), 'depth', onward)]
    ppermute x24 -> x14, starting transfers between devices: 15.6 us -> 13.5 us  [gathered(): lax.ppermute(sums, 'batch', [(i, i ^ m) for i in range(group)])]
    ppermute x9, waiting for transfers between devices: 4.75 us -> 6.35 us  [steps(): arriving = [lax.ppermute(part, 'depth', route) for part in passed]]
    ppermute x9, starting transfers between devices: 10.3 us -> 8.86 us  [steps(): arriving = [lax.ppermute(part, 'depth', route) for part in passed]]
    ppermute x24 -> x14, waiting for transfers between devices: 15.7 us -> 17 us  [gathered(): lax.ppermute(sums, 'batch', [(i, i ^ m) for i in range(group)])]
  transfers between devices with their start and end apart: 45 -> 37, of which waited for: 22 -> 21; matrix products, arithmetic and copies ran while one was open for 0% -> 0% of each run, Pallas kernels for 5% -> 9%
where the time goes in v1:
time: 116 us
  waiting for transfers between devices  61.4 us (53%)
  starting transfers between devices  35.3 us (30%)
  Pallas kernels  17.5 us (15%)
    pallas_call x30, Pallas kernels, call(): pl.pallas_call(body, out_shape=outs, in_specs=[whole] * len(operands) if...  17.5 us
    ppermute x14, waiting for transfers between devices, gathered(): lax.ppermute(sums, 'batch', [(i, i ^ m) for i in range(group)])  17 us
    ppermute x14, starting transfers between devices, gathered(): lax.ppermute(sums, 'batch', [(i, i ^ m) for i in range(group)])  13.5 us
    ppermute x1, waiting for transfers between devices, steps(): near_lower = lax.ppermute(widen(1, weights, sums), 'depth', partners)  12.2 us
    ppermute x1, waiting for transfers between devices, steps(): near_upper = lax.ppermute(widen(0, weights, sums), 'depth', partners)  9.6 us
    ppermute x9, starting transfers between devices, steps(): arriving = [lax.ppermute(part, 'depth', route) for part in passed]  8.86 us
    ppermute x3, waiting for transfers between devices, steps(): exchange = [lax.ppermute(part, 'depth', partners) for part in sent]  8.84 us
    ppermute x9, waiting for transfers between devices, steps(): arriving = [lax.ppermute(part, 'depth', route) for part in passed]  6.35 us
  transfers between devices with their start and end apart: 37, of which 21 were waited for; matrix products, arithmetic and copies ran while one was open for 0% of the time, Pallas kernels for 9%

profile of v1, /device:TPU:24, one launch (start us, length us, event | category | flops | bytes accessed | tf_op | source)
XLA Modules:
  0.0 115.7 jit_solution(13506932014921945456)
XLA Ops:
  0.0 1.0 copy-done
  1.7 1.5 %collective-permute-start.2 = (f32[2,256]{1,0:T(2,128)S(1)}, f32[2,256]{1,0:T(2,128)S(1)}, u32[]{:S(2)}, u32[]{:S(2)}) collective-permute-start(f32[2,256]{1,0:T(2,128)S(1)} %shard_map.47.refs_5_.refs_6_), channel_id=1, source_target_pairs={{0,2},{1,3},{2,0},{3,1},{4,6},{5,7},{6,4},{7,5},{8,10},{9,11},{10,... | collective-permute-start | bytes 6152 | tf_op jit(solution)/shard_map/ppermute | solution.py:438
  3.2 2.4 %shard_map.46.refs_2_.refs_1_.weights = bf16[4,3,768,256]{3,2,1,0:T(8,128)(2,1)S(1)} custom-call(bf16[4,3,768,256]{3,2,1,0:T(8,128)(2,1)} %bitcast.7), custom_call_target="tpu_custom_call" | custom-call | bytes 9437184 | tf_op jit(solution)/shard_map/pallas_call | solution.py:24
  6.2 1.5 %shard_map.48 = (f32[2,16,16,256]{3,2,1,0:T(8,128)S(1)}, f32[2,16,16,256]{3,2,1,0:T(8,128)S(1)}, f32[2,256]{1,0:T(2,128)S(1)}) custom-call(f32[2,16,16,256]{3,2,1,0:T(8,128)S(1)} %bitcast.5, f32[2,16,16,256]{3,2,1,0:T(8,128)S(1)} %collective-permute-done.refs_1_, bf16[4,3,768,256]{3,2,1,0:T(8,128)(2,1)S(1)} %shard_map.46.refs_2_.refs_1_.weights, ...), custom_call_target="tpu_custom_call" | custom-call | flops 1207959552 | bytes 1048576 | tf_op jit(solution)/shard_map/pallas_call | solution.py:24
  7.8 1.0 collective-permute-start.4
  8.7 2.7 %collective-permute-done.4.refs_6_ = f32[2,256]{1,0:T(2,128)S(1)} collective-permute-done((f32[2,256]{1,0:T(2,128)S(1)}, f32[2,256]{1,0:T(2,128)S(1)}, u32[]{:S(2)}, u32[]{:S(2)}) %collective-permute-start.4) | collective-permute-done | bytes 2080 | tf_op jit(solution)/shard_map/ppermute | solution.py:438
  11.4 1.5 %shard_map.50 = (f32[2,16,16,256]{3,2,1,0:T(8,128)S(1)}, f32[2,16,16,256]{3,2,1,0:T(8,128)S(1)}, f32[2,256]{1,0:T(2,128)S(1)}) custom-call(f32[2,16,16,256]{3,2,1,0:T(8,128)S(1)} %get-tuple-element.73.refs_0_, f32[2,16,16,256]{3,2,1,0:T(8,128)S(1)} %get-tuple-element.74.refs_1_, bf16[4,3,768,256]{3,2,1,0:T(8,128)(2,1)S(1)} %shard_map.46.refs_2_.refs_1_.weights, ...), custom_call_target="tpu_custom_call" | custom-call | flops 1207959552 | bytes 1048576 | tf_op jit(solution)/shard_map/pallas_call | solution.py:24
  13.0 1.0 collective-permute-start.5
  13.9 2.7 %collective-permute-done.5.refs_6_ = f32[2,256]{1,0:T(2,128)S(1)} collective-permute-done((f32[2,256]{1,0:T(2,128)S(1)}, f32[2,256]{1,0:T(2,128)S(1)}, u32[]{:S(2)}, u32[]{:S(2)}) %collective-permute-start.5) | collective-permute-done | bytes 2080 | tf_op jit(solution)/shard_map/ppermute | solution.py:438
  16.6 1.5 %shard_map.51 = (f32[2,16,16,256]{3,2,1,0:T(8,128)S(1)}, f32[2,256]{1,0:T(2,128)S(1)}) custom-call(f32[2,16,16,256]{3,2,1,0:T(8,128)S(1)} %get-tuple-element.76.refs_0_, f32[2,16,16,256]{3,2,1,0:T(8,128)S(1)} %get-tuple-element.77.refs_1_, bf16[4,3,768,256]{3,2,1,0:T(8,128)(2,1)S(1)} %shard_map.46.refs_2_.refs_1_.weights, f32[4,256]{1,0:T(4,128)S(1)} %copy-done.2, ...), custom_call_target="tpu_custom_call" | custom-call | flops 1207959552 | bytes 1048576 | tf_op jit(solution)/shard_map/pallas_call | solution.py:24
  18.1 1.0 collective-permute-start.6
  19.1 2.7 %collective-permute-done.6.refs_5_ = f32[2,256]{1,0:T(2,128)S(1)} collective-permute-done((f32[2,256]{1,0:T(2,128)S(1)}, f32[2,256]{1,0:T(2,128)S(1)}, u32[]{:S(2)}, u32[]{:S(2)}) %collective-permute-start.6) | collective-permute-done | bytes 2080 | tf_op jit(solution)/shard_map/ppermute | solution.py:438
  22.7 3.4 %collective-permute-start.7 = (f32[2,16,16,256]{3,2,1,0:T(8,128)S(1)}, f32[2,16,16,256]{3,2,1,0:T(8,128)S(1)}, u32[]{:S(2)}, u32[]{:S(2)}) collective-permute-start(f32[2,16,16,256]{3,2,1,0:T(8,128)S(1)} %get-tuple-element.81), channel_id=1, source_target_pairs={{0,4},{4,8},{8,12},{12,16},{16,20},{20,24},{24,28},{1,5},{5,9},{9,... | collective-permute-start | bytes 1572872 | tf_op jit(solution)/shard_map/ppermute | solution.py:471
  26.2 1.0 collective-permute-start.8
  27.2 1.1 collective-permute-start.9
  28.3 0.9 collective-permute-done.10
  29.2 1.6 %collective-permute-done.9 = f32[2,256]{1,0:T(2,128)S(1)} collective-permute-done((f32[2,256]{1,0:T(2,128)S(1)}, f32[2,256]{1,0:T(2,128)S(1)}, u32[]{:S(2)}, u32[]{:S(2)}) %collective-permute-start.9) | collective-permute-done | bytes 2080 | tf_op jit(solution)/shard_map/ppermute | solution.py:438
  30.8 1.9 %collective-permute-start.11 = (f32[2,256]{1,0:T(2,128)S(1)}, f32[2,256]{1,0:T(2,128)S(1)}, u32[]{:S(2)}, u32[]{:S(2)}) collective-permute-start(f32[2,256]{1,0:T(2,128)S(1)} %add_add_fusion), channel_id=1, source_target_pairs={{0,4},{4,8},{8,12},{12,16},{16,20},{20,24},{24,28},{1,5},{5,9},{9,... | collective-permute-start | bytes 6152 | tf_op jit(solution)/shard_map/ppermute | solution.py:472
  32.8 4.4 %collective-permute-done.11.refs_4_ = f32[2,256]{1,0:T(2,128)S(1)} collective-permute-done((f32[2,256]{1,0:T(2,128)S(1)}, f32[2,256]{1,0:T(2,128)S(1)}, u32[]{:S(2)}, u32[]{:S(2)}) %collective-permute-start.11) | collective-permute-done | bytes 2080 | tf_op jit(solution)/shard_map/ppermute | solution.py:472
  37.2 0.9 shard_map.53
  38.2 1.2 %collective-permute-start.21 = (f32[576,256]{1,0:T(8,128)S(1)}, f32[576,256]{1,0:T(8,128)S(1)}, u32[]{:S(2)}, u32[]{:S(2)}) collective-permute-start(f32[576,256]{1,0:T(8,128)S(1)} %shard_map.61), channel_id=1, source_target_pairs={{0,4},{4,0},{8,12},{12,8},{16,20},{20,16},{24,28},{28,24},{1,5},{5... | collective-permute-start | bytes 1769480 | tf_op jit(solution)/shard_map/ppermute | solution.py:479
  39.4 9.6 %collective-permute-done.20.near_upper = f32[576,256]{1,0:T(8,128)S(1)} collective-permute-done((f32[576,256]{1,0:T(8,128)S(1)}, f32[576,256]{1,0:T(8,128)S(1)}, u32[]{:S(2)}, u32[]{:S(2)}) %collective-permute-start.20) | collective-permute-done | bytes 589856 | tf_op jit(solution)/shard_map/ppermute | solution.py:467
  49.0 12.2 %collective-permute-done.21.near_lower = f32[576,256]{1,0:T(8,128)S(1)} collective-permute-done((f32[576,256]{1,0:T(8,128)S(1)}, f32[576,256]{1,0:T(8,128)S(1)}, u32[]{:S(2)}, u32[]{:S(2)}) %collective-permute-start.21) | collective-permute-done | bytes 589856 | tf_op jit(solution)/shard_map/ppermute | solution.py:479
  61.8 1.5 %collective-permute-start.14 = (f32[2,256]{1,0:T(2,128)S(1)}, f32[2,256]{1,0:T(2,128)S(1)}, u32[]{:S(2)}, u32[]{:S(2)}) collective-permute-start(f32[2,256]{1,0:T(2,128)S(1)} %get-tuple-element.84.refs_5_.after), channel_id=1, source_target_pairs={{0,2},{1,3},{2,0},{3,1},{4,6},{5,7},{6,4},{7,5},{8,10},{9,11},{10,... | collective-permute-start | bytes 6152 | tf_op jit(solution)/shard_map/ppermute | solution.py:438
  63.3 1.2 %collective-permute-start.15 = (f32[2,256]{1,0:T(2,128)S(1)}, f32[2,256]{1,0:T(2,128)S(1)}, u32[]{:S(2)}, u32[]{:S(2)}) collective-permute-start(f32[2,256]{1,0:T(2,128)S(1)} %get-tuple-element.84.refs_5_.after), channel_id=1, source_target_pairs={{0,3},{1,2},{2,1},{3,0},{4,7},{5,6},{6,5},{7,4},{8,11},{9,10},{10,... | collective-permute-start | bytes 6152 | tf_op jit(solution)/shard_map/ppermute | solution.py:438
  64.5 0.9 collective-permute-done.14.refs_7_
  65.4 0.9 collective-permute-done.15.refs_8_
  66.3 1.6 %shard_map.54 = (f32[2,16,16,256]{3,2,1,0:T(8,128)S(1)}, f32[2,16,16,256]{3,2,1,0:T(8,128)S(1)}, f32[2,256]{1,0:T(2,128)S(1)}) custom-call(f32[2,16,16,256]{3,2,1,0:T(8,128)S(1)} %get-tuple-element.83.refs_0_, f32[2,16,16,256]{3,2,1,0:T(8,128)S(1)} %collective-permute-done.12.refs_1_, bf16[4,3,768,256]{3,2,1,0:T(8,128)(2,1)S(1)} %shard_map.46.refs_2_.refs_1_.weights, ...), custom_call_target="tpu_custom_call" | custom-call | flops 1207959552 | bytes 1048576 | tf_op jit(solution)/shard_map/pallas_call | solution.py:24
  67.9 1.6 %collective-permute-start.16 = (f32[2,256]{1,0:T(2,128)S(1)}, f32[2,256]{1,0:T(2,128)S(1)}, u32[]{:S(2)}, u32[]{:S(2)}) collective-permute-start(f32[2,256]{1,0:T(2,128)S(1)} %get-tuple-element.87.refs_0_), channel_id=1, source_target_pairs={{0,2},{1,3},{2,0},{3,1},{4,6},{5,7},{6,4},{7,5},{8,10},{9,11},{10,... | collective-permute-start | bytes 6152 | tf_op jit(solution)/shard_map/ppermute | solution.py:438
  69.4 2.1 %collective-permute-done.16.refs_6_ = f32[2,256]{1,0:T(2,128)S(1)} collective-permute-done((f32[2,256]{1,0:T(2,128)S(1)}, f32[2,256]{1,0:T(2,128)S(1)}, u32[]{:S(2)}, u32[]{:S(2)}) %collective-permute-start.16) | collective-permute-done | bytes 2080 | tf_op jit(solution)/shard_map/ppermute | solution.py:438
  71.5 1.6 %shard_map.56 = (f32[2,16,16,256]{3,2,1,0:T(8,128)S(1)}, f32[2,256]{1,0:T(2,128)S(1)}) custom-call(f32[2,16,16,256]{3,2,1,0:T(8,128)S(1)} %get-tuple-element.85.refs_0_, f32[2,16,16,256]{3,2,1,0:T(8,128)S(1)} %get-tuple-element.86.refs_1_, bf16[4,3,768,256]{3,2,1,0:T(8,128)(2,1)S(1)} %shard_map.46.refs_2_.refs_1_.weights, f32[4,256]{1,0:T(4,128)S(1)} %copy-done.2, ...), custom_call_target="tpu_custom_call" | custom-call | flops 1207959552 | bytes 1048576 | tf_op jit(solution)/shard_map/pallas_call | solution.py:24
  73.1 1.5 %collective-permute-start.17 = (f32[2,256]{1,0:T(2,128)S(1)}, f32[2,256]{1,0:T(2,128)S(1)}, u32[]{:S(2)}, u32[]{:S(2)}) collective-permute-start(f32[2,256]{1,0:T(2,128)S(1)} %get-tuple-element.89.refs_0_), channel_id=1, source_target_pairs={{0,2},{1,3},{2,0},{3,1},{4,6},{5,7},{6,4},{7,5},{8,10},{9,11},{10,... | collective-permute-start | bytes 6152 | tf_op jit(solution)/shard_map/ppermute | solution.py:438
  74.6 2.1 %collective-permute-done.17.refs_5_ = f32[2,256]{1,0:T(2,128)S(1)} collective-permute-done((f32[2,256]{1,0:T(2,128)S(1)}, f32[2,256]{1,0:T(2,128)S(1)}, u32[]{:S(2)}, u32[]{:S(2)}) %collective-permute-start.17) | collective-permute-done | bytes 2080 | tf_op jit(solution)/shard_map/ppermute | solution.py:438
  76.7 1.0 shard_map.58
  78.4 1.4 %collective-permute-start.25 = (f32[96,256]{1,0:T(8,128)S(1)}, f32[96,256]{1,0:T(8,128)S(1)}, u32[]{:S(2)}, u32[]{:S(2)}) collective-permute-start(f32[96,256]{1,0:T(8,128)S(1)} %get-tuple-element.96), channel_id=1, source_target_pairs={{0,4},{4,0},{8,12},{12,8},{16,20},{20,16},{24,28},{28,24},{1,5},{5... | collective-permute-start | bytes 294920 | tf_op jit(solution)/shard_map/ppermute | solution.py:503
  79.8 3.6 %collective-permute-done.18.received.refs_1_.refs_3_ = f32[136,256]{1,0:T(8,128)S(1)} collective-permute-done((f32[136,256]{1,0:T(8,128)S(1)}, f32[136,256]{1,0:T(8,128)S(1)}, u32[]{:S(2)}, u32[]{:S(2)}) %collective-permute-start.18) | collective-permute-done | bytes 139296 | tf_op jit(solution)/shard_map/ppermute | solution.py:503
  84.2 1.4 %collective-permute-done.25.received.refs_4_ = f32[96,256]{1,0:T(8,128)S(1)} collective-permute-done((f32[96,256]{1,0:T(8,128)S(1)}, f32[96,256]{1,0:T(8,128)S(1)}, u32[]{:S(2)}, u32[]{:S(2)}) %collective-permute-start.25) | collective-permute-done | bytes 98336 | tf_op jit(solution)/shard_map/ppermute | solution.py:503
  86.3 1.4 %collective-permute-start.27 = (f32[32,256]{1,0:T(8,128)S(1)}, f32[32,256]{1,0:T(8,128)S(1)}, u32[]{:S(2)}, u32[]{:S(2)}) collective-permute-start(f32[32,256]{1,0:T(8,128)S(1)} %get-tuple-element.97), channel_id=1, source_target_pairs={{0,4},{4,0},{8,12},{12,8},{16,20},{20,16},{24,28},{28,24},{1,5},{5... | collective-permute-start | bytes 98312 | tf_op jit(solution)/shard_map/ppermute | solution.py:503
  87.7 3.8 %collective-permute-done.27.received.refs_5_ = f32[32,256]{1,0:T(8,128)S(1)} collective-permute-done((f32[32,256]{1,0:T(8,128)S(1)}, f32[32,256]{1,0:T(8,128)S(1)}, u32[]{:S(2)}, u32[]{:S(2)}) %collective-permute-start.27) | collective-permute-done | bytes 32800 | tf_op jit(solution)/shard_map/ppermute | solution.py:503
  92.8 1.4 %collective-permute-start.30 = (f32[1,6,16,256]{3,2,1,0:T(8,128)S(1)}, f32[1,6,16,256]{3,2,1,0:T(8,128)S(1)}, u32[]{:S(2)}, u32[]{:S(2)}) collective-permute-start(f32[1,6,16,256]{3,2,1,0:T(8,128)S(1)} %get-tuple-element.113), channel_id=1, source_target_pairs={{0,4},{4,0},{8,16},{12,20},{16,8},{20,12},{24,28},{28,24},{1,5},{5... | collective-permute-start | bytes 294920 | tf_op jit(solution)/shard_map/ppermute | solution.py:525
  94.8 3.8 %collective-permute-done.28.refs_1_ = f32[1,2,16,256]{3,2,1,0:T(8,128)S(1)} collective-permute-done((f32[1,2,16,256]{3,2,1,0:T(8,128)S(1)}, f32[1,2,16,256]{3,2,1,0:T(8,128)S(1)}, u32[]{:S(2)}, u32[]{:S(2)}) %collective-permute-start.28) | collective-permute-done | bytes 32800 | tf_op jit(solution)/shard_map/ppermute | solution.py:525
  99.3 1.5 %collective-permute-start.29 = (f32[1,4,16,256]{3,2,1,0:T(8,128)S(1)}, f32[1,4,16,256]{3,2,1,0:T(8,128)S(1)}, u32[]{:S(2)}, u32[]{:S(2)}) collective-permute-start(f32[1,4,16,256]{3,2,1,0:T(8,128)S(1)} %get-tuple-element.112), channel_id=1, source_target_pairs={{0,4},{4,0},{8,12},{12,8},{16,24},{20,28},{24,16},{28,20},{1,5},{5... | collective-permute-start | bytes 196616 | tf_op jit(solution)/shard_map/ppermute | solution.py:525
  100.8 1.5 %collective-permute-start.33 = (f32[1,6,16,256]{3,2,1,0:T(8,128)S(1)}, f32[1,6,16,256]{3,2,1,0:T(8,128)S(1)}, u32[]{:S(2)}, u32[]{:S(2)}) collective-permute-start(f32[1,6,16,256]{3,2,1,0:T(8,128)S(1)} %get-tuple-element.129), channel_id=1, source_target_pairs={{0,4},{4,0},{8,12},{12,8},{16,24},{20,28},{24,16},{28,20},{1,5},{5... | collective-permute-start | bytes 294920 | tf_op jit(solution)/shard_map/ppermute | solution.py:525
  102.9 1.1 collective-permute-start.35
  106.2 1.3 %collective-permute-done.35.refs_1_ = f32[1,6,16,256]{3,2,1,0:T(8,128)S(1)} collective-permute-done((f32[1,6,16,256]{3,2,1,0:T(8,128)S(1)}, f32[1,6,16,256]{3,2,1,0:T(8,128)S(1)}, u32[]{:S(2)}, u32[]{:S(2)}) %collective-permute-start.35) | collective-permute-done | bytes 98336 | tf_op jit(solution)/shard_map/ppermute | solution.py:525
  107.5 0.9 shard_map.73
  109.2 1.3 %collective-permute-start.34 = (f32[1,6,16,256]{3,2,1,0:T(8,128)S(1)}, f32[1,6,16,256]{3,2,1,0:T(8,128)S(1)}, u32[]{:S(2)}, u32[]{:S(2)}) collective-permute-start(f32[1,6,16,256]{3,2,1,0:T(8,128)S(1)} %get-tuple-element.134), channel_id=1, source_target_pairs={{0,4},{4,0},{8,12},{12,8},{16,20},{20,16},{24,28},{28,24},{1,5},{5... | collective-permute-start | bytes 294920 | tf_op jit(solution)/shard_map/ppermute | solution.py:552
  111.9 2.9 %collective-permute-done.32.refs_0_ = f32[1,2,16,256]{3,2,1,0:T(8,128)S(1)} collective-permute-done((f32[1,2,16,256]{3,2,1,0:T(8,128)S(1)}, f32[1,2,16,256]{3,2,1,0:T(8,128)S(1)}, u32[]{:S(2)}, u32[]{:S(2)}) %collective-permute-start.32) | collective-permute-done | bytes 32800 | tf_op jit(solution)/shard_map/ppermute | solution.py:552
  (69 shorter events, 13.4 us)
Async XLA Ops:
  0.0 6.2 %collective-permute-start = (f32[2,16,16,256]{3,2,1,0:T(8,128)}, f32[2,16,16,256]{3,2,1,0:T(8,128)S(1)}, u32[]{:S(2)}, u32[]{:S(2)}) collective-permute-start(f32[2,16,16,256]{3,2,1,0:T(8,128)} %bitcast.3), channel_id=1, source_target_pairs={{0,1},{1,0},{2,3},{3,2},{4,5},{5,4},{6,7},{7,6},{8,9},{9,8},{10,11... | collective-permute-start | bytes 1572872 | tf_op jit(solution)/shard_map/ppermute | solution.py:451
  0.0 1.0 copy-start
  1.1 4.5 %collective-permute-start.1 = (f32[2,256]{1,0:T(2,128)S(1)}, f32[2,256]{1,0:T(2,128)S(1)}, u32[]{:S(2)}, u32[]{:S(2)}) collective-permute-start(f32[2,256]{1,0:T(2,128)S(1)} %shard_map.47.refs_5_.refs_6_), channel_id=1, source_target_pairs={{0,1},{1,0},{2,3},{3,2},{4,5},{5,4},{6,7},{7,6},{8,9},{9,8},{10,11... | collective-permute-start | bytes 6152 | tf_op jit(solution)/shard_map/ppermute | solution.py:438
  1.7 4.0 %collective-permute-start.2 = (f32[2,256]{1,0:T(2,128)S(1)}, f32[2,256]{1,0:T(2,128)S(1)}, u32[]{:S(2)}, u32[]{:S(2)}) collective-permute-start(f32[2,256]{1,0:T(2,128)S(1)} %shard_map.47.refs_5_.refs_6_), channel_id=1, source_target_pairs={{0,2},{1,3},{2,0},{3,1},{4,6},{5,7},{6,4},{7,5},{8,10},{9,11},{10,... | collective-permute-start | bytes 6152 | tf_op jit(solution)/shard_map/ppermute | solution.py:438
  3.2 3.0 %collective-permute-start.3 = (f32[2,256]{1,0:T(2,128)S(1)}, f32[2,256]{1,0:T(2,128)S(1)}, u32[]{:S(2)}, u32[]{:S(2)}) collective-permute-start(f32[2,256]{1,0:T(2,128)S(1)} %shard_map.47.refs_5_.refs_6_), channel_id=1, source_target_pairs={{0,3},{1,2},{2,1},{3,0},{4,7},{5,6},{6,5},{7,4},{8,11},{9,10},{10,... | collective-permute-start | bytes 6152 | tf_op jit(solution)/shard_map/ppermute | solution.py:438
  3.2 3.0 %copy-start.1 = (f32[1,2,16,16,256]{4,3,2,1,0:T(8,128)S(1)}, f32[1,2,16,16,256]{4,3,2,1,0:T(8,128)}, u32[]{:S(2)}) copy-start(f32[1,2,16,16,256]{4,3,2,1,0:T(8,128)} %param.4) | copy-start | bytes 1572868
  3.2 3.0 %copy-start.2 = (f32[4,256]{1,0:T(4,128)S(1)}, f32[4,256]{1,0:T(4,128)}, u32[]{:S(2)}) copy-start(f32[4,256]{1,0:T(4,128)} %refs_2_.5) | copy-start | bytes 12292
  3.2 3.0 %copy-start.3 = (f32[4,256]{1,0:T(4,128)S(1)}, f32[4,256]{1,0:T(4,128)}, u32[]{:S(2)}) copy-start(f32[4,256]{1,0:T(4,128)} %refs_3_.15) | copy-start | bytes 12292
  7.8 3.7 %collective-permute-start.4 = (f32[2,256]{1,0:T(2,128)S(1)}, f32[2,256]{1,0:T(2,128)S(1)}, u32[]{:S(2)}, u32[]{:S(2)}) collective-permute-start(f32[2,256]{1,0:T(2,128)S(1)} %get-tuple-element.75.refs_0_.after), channel_id=1, source_target_pairs={{0,2},{1,3},{2,0},{3,1},{4,6},{5,7},{6,4},{7,5},{8,10},{9,11},{10,... | collective-permute-start | bytes 6152 | tf_op jit(solution)/shard_map/ppermute | solution.py:438
  13.0 3.7 %collective-permute-start.5 = (f32[2,256]{1,0:T(2,128)S(1)}, f32[2,256]{1,0:T(2,128)S(1)}, u32[]{:S(2)}, u32[]{:S(2)}) collective-permute-start(f32[2,256]{1,0:T(2,128)S(1)} %get-tuple-element.78.refs_5_), channel_id=1, source_target_pairs={{0,2},{1,3},{2,0},{3,1},{4,6},{5,7},{6,4},{7,5},{8,10},{9,11},{10,... | collective-permute-start | bytes 6152 | tf_op jit(solution)/shard_map/ppermute | solution.py:438
  18.1 3.7 %collective-permute-start.6 = (f32[2,256]{1,0:T(2,128)S(1)}, f32[2,256]{1,0:T(2,128)S(1)}, u32[]{:S(2)}, u32[]{:S(2)}) collective-permute-start(f32[2,256]{1,0:T(2,128)S(1)} %get-tuple-element.80.refs_4_), channel_id=1, source_target_pairs={{0,2},{1,3},{2,0},{3,1},{4,6},{5,7},{6,4},{7,5},{8,10},{9,11},{10,... | collective-permute-start | bytes 6152 | tf_op jit(solution)/shard_map/ppermute | solution.py:438
  22.7 14.6 %collective-permute-start.7 = (f32[2,16,16,256]{3,2,1,0:T(8,128)S(1)}, f32[2,16,16,256]{3,2,1,0:T(8,128)S(1)}, u32[]{:S(2)}, u32[]{:S(2)}) collective-permute-start(f32[2,16,16,256]{3,2,1,0:T(8,128)S(1)} %get-tuple-element.81), channel_id=1, source_target_pairs={{0,4},{4,8},{8,12},{12,16},{16,20},{20,24},{24,28},{1,5},{5,9},{9,... | collective-permute-start | bytes 1572872 | tf_op jit(solution)/shard_map/ppermute | solution.py:471
  26.1 3.1 %collective-permute-start.10 = (f32[2,256]{1,0:T(2,128)S(1)}, f32[2,256]{1,0:T(2,128)S(1)}, u32[]{:S(2)}, u32[]{:S(2)}) collective-permute-start(f32[2,256]{1,0:T(2,128)S(1)} %get-tuple-element.82), channel_id=1, source_target_pairs={{0,3},{1,2},{2,1},{3,0},{4,7},{5,6},{6,5},{7,4},{8,11},{9,10},{10,... | collective-permute-start | bytes 6152 | tf_op jit(solution)/shard_map/ppermute | solution.py:438
  26.2 3.0 %collective-permute-start.8 = (f32[2,256]{1,0:T(2,128)S(1)}, f32[2,256]{1,0:T(2,128)S(1)}, u32[]{:S(2)}, u32[]{:S(2)}) collective-permute-start(f32[2,256]{1,0:T(2,128)S(1)} %get-tuple-element.82), channel_id=1, source_target_pairs={{0,1},{1,0},{2,3},{3,2},{4,5},{5,4},{6,7},{7,6},{8,9},{9,8},{10,11... | collective-permute-start | bytes 6152 | tf_op jit(solution)/shard_map/ppermute | solution.py:438
  27.2 3.6 %collective-permute-start.9 = (f32[2,256]{1,0:T(2,128)S(1)}, f32[2,256]{1,0:T(2,128)S(1)}, u32[]{:S(2)}, u32[]{:S(2)}) collective-permute-start(f32[2,256]{1,0:T(2,128)S(1)} %get-tuple-element.82), channel_id=1, source_target_pairs={{0,2},{1,3},{2,0},{3,1},{4,6},{5,7},{6,4},{7,5},{8,10},{9,11},{10,... | collective-permute-start | bytes 6152 | tf_op jit(solution)/shard_map/ppermute | solution.py:438
  30.8 6.5 %collective-permute-start.11 = (f32[2,256]{1,0:T(2,128)S(1)}, f32[2,256]{1,0:T(2,128)S(1)}, u32[]{:S(2)}, u32[]{:S(2)}) collective-permute-start(f32[2,256]{1,0:T(2,128)S(1)} %add_add_fusion), channel_id=1, source_target_pairs={{0,4},{4,8},{8,12},{12,16},{16,20},{20,24},{24,28},{1,5},{5,9},{9,... | collective-permute-start | bytes 6152 | tf_op jit(solution)/shard_map/ppermute | solution.py:472
  32.8 16.3 %collective-permute-start.20 = (f32[576,256]{1,0:T(8,128)S(1)}, f32[576,256]{1,0:T(8,128)S(1)}, u32[]{:S(2)}, u32[]{:S(2)}) collective-permute-start(f32[576,256]{1,0:T(8,128)S(1)} %shard_map.60), channel_id=1, source_target_pairs={{0,4},{4,0},{8,12},{12,8},{16,20},{20,16},{24,28},{28,24},{1,5},{5... | collective-permute-start | bytes 1769480 | tf_op jit(solution)/shard_map/ppermute | solution.py:467
  38.2 23.1 %collective-permute-start.21 = (f32[576,256]{1,0:T(8,128)S(1)}, f32[576,256]{1,0:T(8,128)S(1)}, u32[]{:S(2)}, u32[]{:S(2)}) collective-permute-start(f32[576,256]{1,0:T(8,128)S(1)} %shard_map.61), channel_id=1, source_target_pairs={{0,4},{4,0},{8,12},{12,8},{16,20},{20,16},{24,28},{28,24},{1,5},{5... | collective-permute-start | bytes 1769480 | tf_op jit(solution)/shard_map/ppermute | solution.py:479
  39.4 26.9 %collective-permute-start.12 = (f32[2,16,16,256]{3,2,1,0:T(8,128)S(1)}, f32[2,16,16,256]{3,2,1,0:T(8,128)S(1)}, u32[]{:S(2)}, u32[]{:S(2)}) collective-permute-start(f32[2,16,16,256]{3,2,1,0:T(8,128)S(1)} %get-tuple-element.83.refs_0_), channel_id=1, source_target_pairs={{0,1},{1,0},{2,3},{3,2},{4,5},{5,4},{6,7},{7,6},{8,9},{9,8},{10,11... | collective-permute-start | bytes 1572872 | tf_op jit(solution)/shard_map/ppermute | solution.py:478
  49.0 42.5 %collective-permute-start.22 = (f32[576,256]{1,0:T(8,128)S(1)}, f32[576,256]{1,0:T(8,128)S(1)}, u32[]{:S(2)}, u32[]{:S(2)}) collective-permute-start(f32[576,256]{1,0:T(8,128)S(1)} %collective-permute-done.20.near_upper), channel_id=1, source_target_pairs={{0,1},{1,0},{2,3},{3,2},{4,5},{5,4},{6,7},{7,6},{8,9},{9,8},{10,11... | collective-permute-start | bytes 1769480 | tf_op jit(solution)/shard_map/ppermute | solution.py:480
  61.3 30.2 %collective-permute-start.23 = (f32[576,256]{1,0:T(8,128)S(1)}, f32[576,256]{1,0:T(8,128)S(1)}, u32[]{:S(2)}, u32[]{:S(2)}) collective-permute-start(f32[576,256]{1,0:T(8,128)S(1)} %collective-permute-done.21.near_lower), channel_id=1, source_target_pairs={{0,1},{1,0},{2,3},{3,2},{4,5},{5,4},{6,7},{7,6},{8,9},{9,8},{10,11... | collective-permute-start | bytes 1769480 | tf_op jit(solution)/shard_map/ppermute | solution.py:486
  61.3 2.0 %collective-permute-start.13 = (f32[2,256]{1,0:T(2,128)S(1)}, f32[2,256]{1,0:T(2,128)S(1)}, u32[]{:S(2)}, u32[]{:S(2)}) collective-permute-start(f32[2,256]{1,0:T(2,128)S(1)} %get-tuple-element.84.refs_5_.after), channel_id=1, source_target_pairs={{0,1},{1,0},{2,3},{3,2},{4,5},{5,4},{6,7},{7,6},{8,9},{9,8},{10,11... | collective-permute-start | bytes 6152 | tf_op jit(solution)/shard_map/ppermute | solution.py:438
  61.8 3.6 %collective-permute-start.14 = (f32[2,256]{1,0:T(2,128)S(1)}, f32[2,256]{1,0:T(2,128)S(1)}, u32[]{:S(2)}, u32[]{:S(2)}) collective-permute-start(f32[2,256]{1,0:T(2,128)S(1)} %get-tuple-element.84.refs_5_.after), channel_id=1, source_target_pairs={{0,2},{1,3},{2,0},{3,1},{4,6},{5,7},{6,4},{7,5},{8,10},{9,11},{10,... | collective-permute-start | bytes 6152 | tf_op jit(solution)/shard_map/ppermute | solution.py:438
  63.3 3.0 %collective-permute-start.15 = (f32[2,256]{1,0:T(2,128)S(1)}, f32[2,256]{1,0:T(2,128)S(1)}, u32[]{:S(2)}, u32[]{:S(2)}) collective-permute-start(f32[2,256]{1,0:T(2,128)S(1)} %get-tuple-element.84.refs_5_.after), channel_id=1, source_target_pairs={{0,3},{1,2},{2,1},{3,0},{4,7},{5,6},{6,5},{7,4},{8,11},{9,10},{10,... | collective-permute-start | bytes 6152 | tf_op jit(solution)/shard_map/ppermute | solution.py:438
  67.9 3.7 %collective-permute-start.16 = (f32[2,256]{1,0:T(2,128)S(1)}, f32[2,256]{1,0:T(2,128)S(1)}, u32[]{:S(2)}, u32[]{:S(2)}) collective-permute-start(f32[2,256]{1,0:T(2,128)S(1)} %get-tuple-element.87.refs_0_), channel_id=1, source_target_pairs={{0,2},{1,3},{2,0},{3,1},{4,6},{5,7},{6,4},{7,5},{8,10},{9,11},{10,... | collective-permute-start | bytes 6152 | tf_op jit(solution)/shard_map/ppermute | solution.py:438
  73.1 3.7 %collective-permute-start.17 = (f32[2,256]{1,0:T(2,128)S(1)}, f32[2,256]{1,0:T(2,128)S(1)}, u32[]{:S(2)}, u32[]{:S(2)}) collective-permute-start(f32[2,256]{1,0:T(2,128)S(1)} %get-tuple-element.89.refs_0_), channel_id=1, source_target_pairs={{0,2},{1,3},{2,0},{3,1},{4,6},{5,7},{6,4},{7,5},{8,10},{9,11},{10,... | collective-permute-start | bytes 6152 | tf_op jit(solution)/shard_map/ppermute | solution.py:438
  77.7 5.7 %collective-permute-start.18 = (f32[136,256]{1,0:T(8,128)S(1)}, f32[136,256]{1,0:T(8,128)S(1)}, u32[]{:S(2)}, u32[]{:S(2)}) collective-permute-start(f32[136,256]{1,0:T(8,128)S(1)} %get-tuple-element.92), channel_id=1, source_target_pairs={{0,4},{4,0},{8,12},{12,8},{16,20},{20,16},{24,28},{28,24},{1,5},{5... | collective-permute-start | bytes 417800 | tf_op jit(solution)/shard_map/ppermute | solution.py:503
  78.4 7.1 %collective-permute-start.25 = (f32[96,256]{1,0:T(8,128)S(1)}, f32[96,256]{1,0:T(8,128)S(1)}, u32[]{:S(2)}, u32[]{:S(2)}) collective-permute-start(f32[96,256]{1,0:T(8,128)S(1)} %get-tuple-element.96), channel_id=1, source_target_pairs={{0,4},{4,0},{8,12},{12,8},{16,20},{20,16},{24,28},{28,24},{1,5},{5... | collective-permute-start | bytes 294920 | tf_op jit(solution)/shard_map/ppermute | solution.py:503
  83.5 8.3 %collective-permute-start.19 = (f32[1,8,16,256]{3,2,1,0:T(8,128)S(1)}, f32[1,8,16,256]{3,2,1,0:T(8,128)S(1)}, u32[]{:S(2)}, u32[]{:S(2)}) collective-permute-start(f32[1,8,16,256]{3,2,1,0:T(8,128)S(1)} %shard_map.59), channel_id=1, source_target_pairs={{0,8},{4,12},{8,0},{12,4},{16,20},{20,16},{24,28},{28,24},{1,9},{5... | collective-permute-start | bytes 393224 | tf_op jit(solution)/shard_map/ppermute | solution.py:525
  85.6 7.2 %collective-permute-start.26 = (f32[1,6,16,256]{3,2,1,0:T(8,128)S(1)}, f32[1,6,16,256]{3,2,1,0:T(8,128)S(1)}, u32[]{:S(2)}, u32[]{:S(2)}) collective-permute-start(f32[1,6,16,256]{3,2,1,0:T(8,128)S(1)} %shard_map.64), channel_id=1, source_target_pairs={{0,8},{4,12},{8,0},{12,4},{16,20},{20,16},{24,28},{28,24},{1,9},{5... | collective-permute-start | bytes 294920 | tf_op jit(solution)/shard_map/ppermute | solution.py:525
  86.3 5.2 %collective-permute-start.27 = (f32[32,256]{1,0:T(8,128)S(1)}, f32[32,256]{1,0:T(8,128)S(1)}, u32[]{:S(2)}, u32[]{:S(2)}) collective-permute-start(f32[32,256]{1,0:T(8,128)S(1)} %get-tuple-element.97), channel_id=1, source_target_pairs={{0,4},{4,0},{8,12},{12,8},{16,20},{20,16},{24,28},{28,24},{1,5},{5... | collective-permute-start | bytes 98312 | tf_op jit(solution)/shard_map/ppermute | solution.py:503
  92.0 7.2 %collective-permute-start.24 = (f32[1,6,16,256]{3,2,1,0:T(8,128)S(1)}, f32[1,6,16,256]{3,2,1,0:T(8,128)S(1)}, u32[]{:S(2)}, u32[]{:S(2)}) collective-permute-start(f32[1,6,16,256]{3,2,1,0:T(8,128)S(1)} %get-tuple-element.95), channel_id=1, source_target_pairs={{0,4},{4,0},{8,16},{12,20},{16,8},{20,12},{24,28},{28,24},{1,5},{5... | collective-permute-start | bytes 294920 | tf_op jit(solution)/shard_map/ppermute | solution.py:525
  92.8 8.0 %collective-permute-start.30 = (f32[1,6,16,256]{3,2,1,0:T(8,128)S(1)}, f32[1,6,16,256]{3,2,1,0:T(8,128)S(1)}, u32[]{:S(2)}, u32[]{:S(2)}) collective-permute-start(f32[1,6,16,256]{3,2,1,0:T(8,128)S(1)} %get-tuple-element.113), channel_id=1, source_target_pairs={{0,4},{4,0},{8,16},{12,20},{16,8},{20,12},{24,28},{28,24},{1,5},{5... | collective-permute-start | bytes 294920 | tf_op jit(solution)/shard_map/ppermute | solution.py:525
  94.1 4.5 %collective-permute-start.28 = (f32[1,2,16,256]{3,2,1,0:T(8,128)S(1)}, f32[1,2,16,256]{3,2,1,0:T(8,128)S(1)}, u32[]{:S(2)}, u32[]{:S(2)}) collective-permute-start(f32[1,2,16,256]{3,2,1,0:T(8,128)S(1)} %shard_map.65), channel_id=1, source_target_pairs={{0,8},{4,12},{8,0},{12,4},{16,20},{20,16},{24,28},{28,24},{1,9},{5... | collective-permute-start | bytes 98312 | tf_op jit(solution)/shard_map/ppermute | solution.py:525
  98.6 4.3 %collective-permute-start.31 = (f32[1,4,16,256]{3,2,1,0:T(8,128)S(1)}, f32[1,4,16,256]{3,2,1,0:T(8,128)S(1)}, u32[]{:S(2)}, u32[]{:S(2)}) collective-permute-start(f32[1,4,16,256]{3,2,1,0:T(8,128)S(1)} %get-tuple-element.114), channel_id=1, source_target_pairs={{0,4},{4,0},{8,16},{12,20},{16,8},{20,12},{24,28},{28,24},{1,5},{5... | collective-permute-start | bytes 196616 | tf_op jit(solution)/shard_map/ppermute | solution.py:525
  99.3 4.7 %collective-permute-start.29 = (f32[1,4,16,256]{3,2,1,0:T(8,128)S(1)}, f32[1,4,16,256]{3,2,1,0:T(8,128)S(1)}, u32[]{:S(2)}, u32[]{:S(2)}) collective-permute-start(f32[1,4,16,256]{3,2,1,0:T(8,128)S(1)} %get-tuple-element.112), channel_id=1, source_target_pairs={{0,4},{4,0},{8,12},{12,8},{16,24},{20,28},{24,16},{28,20},{1,5},{5... | collective-permute-start | bytes 196616 | tf_op jit(solution)/shard_map/ppermute | solution.py:525
  100.8 4.6 %collective-permute-start.33 = (f32[1,6,16,256]{3,2,1,0:T(8,128)S(1)}, f32[1,6,16,256]{3,2,1,0:T(8,128)S(1)}, u32[]{:S(2)}, u32[]{:S(2)}) collective-permute-start(f32[1,6,16,256]{3,2,1,0:T(8,128)S(1)} %get-tuple-element.129), channel_id=1, source_target_pairs={{0,4},{4,0},{8,12},{12,8},{16,24},{20,28},{24,16},{28,20},{1,5},{5... | collective-permute-start | bytes 294920 | tf_op jit(solution)/shard_map/ppermute | solution.py:525
  102.9 4.6 %collective-permute-start.35 = (f32[1,6,16,256]{3,2,1,0:T(8,128)S(1)}, f32[1,6,16,256]{3,2,1,0:T(8,128)S(1)}, u32[]{:S(2)}, u32[]{:S(2)}) collective-permute-start(f32[1,6,16,256]{3,2,1,0:T(8,128)S(1)} %get-tuple-element.135), channel_id=1, source_target_pairs={{0,4},{4,0},{8,12},{12,8},{16,24},{20,28},{24,16},{28,20},{1,5},{5... | collective-permute-start | bytes 294920 | tf_op jit(solution)/shard_map/ppermute | solution.py:525
  108.4 6.4 %collective-permute-start.36 = (f32[1,8,16,256]{3,2,1,0:T(8,128)S(1)}, f32[1,8,16,256]{3,2,1,0:T(8,128)S(1)}, u32[]{:S(2)}, u32[]{:S(2)}) collective-permute-start(f32[1,8,16,256]{3,2,1,0:T(8,128)S(1)} %get-tuple-element.139), channel_id=1, source_target_pairs={{0,4},{4,0},{8,12},{12,8},{16,20},{20,16},{24,28},{28,24},{1,5},{5... | collective-permute-start | bytes 393224 | tf_op jit(solution)/shard_map/ppermute | solution.py:552
  109.2 5.6 %collective-permute-start.34 = (f32[1,6,16,256]{3,2,1,0:T(8,128)S(1)}, f32[1,6,16,256]{3,2,1,0:T(8,128)S(1)}, u32[]{:S(2)}, u32[]{:S(2)}) collective-permute-start(f32[1,6,16,256]{3,2,1,0:T(8,128)S(1)} %get-tuple-element.134), channel_id=1, source_target_pairs={{0,4},{4,0},{8,12},{12,8},{16,20},{20,16},{24,28},{28,24},{1,5},{5... | collective-permute-start | bytes 294920 | tf_op jit(solution)/shard_map/ppermute | solution.py:552
  110.5 4.3 %collective-permute-start.32 = (f32[1,2,16,256]{3,2,1,0:T(8,128)S(1)}, f32[1,2,16,256]{3,2,1,0:T(8,128)S(1)}, u32[]{:S(2)}, u32[]{:S(2)}) collective-permute-start(f32[1,2,16,256]{3,2,1,0:T(8,128)S(1)} %get-tuple-element.128), channel_id=1, source_target_pairs={{0,4},{4,0},{8,12},{12,8},{16,20},{20,16},{24,28},{28,24},{1,5},{5... | collective-permute-start | bytes 98312 | tf_op jit(solution)/shard_map/ppermute | solution.py:552

commit v2 on v1

--- a/solution.py
+++ b/solution.py
@@ -77,10 +77,11 @@
     return list(zip(edges, edges[1:]))
 
 
-def sums_kernel(state, sums):
+def sums_kernel(state, held, sums):
     samples, rows, width, channels = state.shape
     total = jnp.zeros((2, channels), jnp.float32)
     for i in range(samples):
+        held[i] = state[i]
         total += both_sums(state[i].reshape(rows * width, channels))
     sums[...] = total
 
@@ -436,7 +437,7 @@
     def gathered(sums, mark=False, chips=False, ready=()):
         others = [
             lax.ppermute(sums, "batch", [(i, i ^ m) for i in range(group)])
-            for m in (range(2, group, 2) if chips else range(1, group))
+            for m in (range(3, group, 2) if chips else range(1, group))
         ]
         if mark:
             sums = call(copy_kernel, (sums, *ready), f32(*sums.shape))
@@ -446,7 +447,9 @@
     cores = [(i, i ^ 1) for i in range(group)]
     onward = [(i, i + 1) for i in range(devices - 1)]
 
-    sums = call(sums_kernel, (initial,), f32(2, channels), moved=initial.size * 4)
+    initial, sums = call(
+        sums_kernel, (initial,), (f32(*initial.shape), f32(2, channels)), moved=initial.size * 4
+    )
     first_totals = gathered(sums)
     other = lax.ppermute(initial, "batch", cores)
     weights = call(
@@ -480,7 +483,7 @@
     far_upper = lax.ppermute(near_upper, "batch", cores)
     states = (current, other)
     for number in range(1, layers_of_block - 1):
-        totals = gathered(sums, number == 2, number > 1)
+        totals = gathered(sums, number == 1, number > 1)
         keep = 2 if number < layers_of_block - 2 else 1
         *states, sums = run(number, states, *norms, totals, kind="plain", keep=keep)
     far_lower = lax.ppermute(near_lower, "batch", cores)

time: 116 us -> 118 us (1.017); the launches traced: 116 us -> 116 us
  starting transfers between devices: 35.3 us -> 37.7 us
  waiting for transfers between devices: 61.4 us -> 59.6 us
    ppermute x14, waiting for transfers between devices: 17 us -> 13.8 us  [gathered(): lax.ppermute(sums, 'batch', [(i, i ^ m) for i in range(group)])]
    ppermute x1, waiting for transfers between devices: 4.41 us -> 6.75 us  [steps(): arrived_totals = lax.ppermute(sum(totals[1:], totals[0]), 'depth', onward)]
    ppermute x9, waiting for transfers between devices: 6.35 us -> 4.69 us  [steps(): arriving = [lax.ppermute(part, 'depth', route) for part in passed]]
    ppermute x9, starting transfers between devices: 8.86 us -> 10.3 us  [steps(): arriving = [lax.ppermute(part, 'depth', route) for part in passed]]
where the time goes in v2:
time: 118 us; the launch traced here: 116 us
  waiting for transfers between devices  59.6 us (51%)
  starting transfers between devices  37.7 us (32%)
  Pallas kernels  17.5 us (15%)
    pallas_call x30, Pallas kernels, call(): pl.pallas_call(body, out_shape=outs, in_specs=[whole] * len(operands) if...  17.5 us
    ppermute x14, waiting for transfers between devices, gathered(): lax.ppermute(sums, 'batch', [(i, i ^ m) for i in range(group)])  13.8 us
    ppermute x14, starting transfers between devices, gathered(): lax.ppermute(sums, 'batch', [(i, i ^ m) for i in range(group)])  13.7 us
    ppermute x1, waiting for transfers between devices, steps(): near_lower = lax.ppermute(widen(1, weights, sums), 'depth', partners)  12.5 us
    ppermute x9, starting transfers between devices, steps(): arriving = [lax.ppermute(part, 'depth', route) for part in passed]  10.3 us
    ppermute x1, waiting for transfers between devices, steps(): near_upper = lax.ppermute(widen(0, weights, sums), 'depth', partners)  10.2 us
    ppermute x3, waiting for transfers between devices, steps(): exchange = [lax.ppermute(part, 'depth', partners) for part in sent]  9.15 us
    ppermute x1, waiting for transfers between devices, steps(): arrived_totals = lax.ppermute(sum(totals[1:], totals[0]), 'depth', onward)  6.75 us
  transfers between devices with their start and end apart: 37, of which 21 were waited for; matrix products, arithmetic and copies ran while one was open for 0% of the time, Pallas kernels for 9%

profile of v2, /device:TPU:24, one launch (start us, length us, event | category | flops | bytes accessed | tf_op | source)
XLA Modules:
  0.0 116.3 jit_solution(12102809014058683354)
XLA Ops:
  0.0 1.0 copy-done
  1.7 1.5 %collective-permute-start.2 = (f32[2,256]{1,0:T(2,128)S(1)}, f32[2,256]{1,0:T(2,128)S(1)}, u32[]{:S(2)}, u32[]{:S(2)}) collective-permute-start(f32[2,256]{1,0:T(2,128)S(1)} %get-tuple-element.76.refs_5_.refs_6_), channel_id=1, source_target_pairs={{0,2},{1,3},{2,0},{3,1},{4,6},{5,7},{6,4},{7,5},{8,10},{9,11},{10,... | collective-permute-start | bytes 6152 | tf_op jit(solution)/shard_map/ppermute | solution.py:439
  3.2 2.4 %shard_map.47.refs_2_.refs_1_.weights = bf16[4,3,768,256]{3,2,1,0:T(8,128)(2,1)S(1)} custom-call(bf16[4,3,768,256]{3,2,1,0:T(8,128)(2,1)} %bitcast.4), custom_call_target="tpu_custom_call" | custom-call | bytes 9437184 | tf_op jit(solution)/shard_map/pallas_call | solution.py:24
  6.2 1.5 %shard_map.48 = (f32[2,16,16,256]{3,2,1,0:T(8,128)S(1)}, f32[2,16,16,256]{3,2,1,0:T(8,128)S(1)}, f32[2,256]{1,0:T(2,128)S(1)}) custom-call(f32[2,16,16,256]{3,2,1,0:T(8,128)S(1)} %get-tuple-element.75.refs_0_.refs_5_, f32[2,16,16,256]{3,2,1,0:T(8,128)S(1)} %collective-permute-done.refs_1_, bf16[4,3,768,256]{3,2,1,0:T(8,128)(2,1)S(1)} %shard_map.47.refs_2_.refs_1_.weights, ...), custom_call_target="tpu_custom_call" | custom-call | flops 1207959552 | bytes 1048576 | tf_op jit(solution)/shard_map/pallas_call | solution.py:24
  7.8 1.3 %collective-permute-start.4 = (f32[2,256]{1,0:T(2,128)S(1)}, f32[2,256]{1,0:T(2,128)S(1)}, u32[]{:S(2)}, u32[]{:S(2)}) collective-permute-start(f32[2,256]{1,0:T(2,128)S(1)} %get-tuple-element.79.refs_0_.after), channel_id=1, source_target_pairs={{0,3},{1,2},{2,1},{3,0},{4,7},{5,6},{6,5},{7,4},{8,11},{9,10},{10,... | collective-permute-start | bytes 6152 | tf_op jit(solution)/shard_map/ppermute | solution.py:439
  9.1 1.8 %collective-permute-done.4.refs_6_ = f32[2,256]{1,0:T(2,128)S(1)} collective-permute-done((f32[2,256]{1,0:T(2,128)S(1)}, f32[2,256]{1,0:T(2,128)S(1)}, u32[]{:S(2)}, u32[]{:S(2)}) %collective-permute-start.4) | collective-permute-done | bytes 2080 | tf_op jit(solution)/shard_map/ppermute | solution.py:439
  10.9 1.5 %shard_map.50 = (f32[2,16,16,256]{3,2,1,0:T(8,128)S(1)}, f32[2,16,16,256]{3,2,1,0:T(8,128)S(1)}, f32[2,256]{1,0:T(2,128)S(1)}) custom-call(f32[2,16,16,256]{3,2,1,0:T(8,128)S(1)} %get-tuple-element.77.refs_0_, f32[2,16,16,256]{3,2,1,0:T(8,128)S(1)} %get-tuple-element.78.refs_1_, bf16[4,3,768,256]{3,2,1,0:T(8,128)(2,1)S(1)} %shard_map.47.refs_2_.refs_1_.weights, ...), custom_call_target="tpu_custom_call" | custom-call | flops 1207959552 | bytes 1048576 | tf_op jit(solution)/shard_map/pallas_call | solution.py:24
  12.4 1.3 %collective-permute-start.5 = (f32[2,256]{1,0:T(2,128)S(1)}, f32[2,256]{1,0:T(2,128)S(1)}, u32[]{:S(2)}, u32[]{:S(2)}) collective-permute-start(f32[2,256]{1,0:T(2,128)S(1)} %get-tuple-element.82.refs_5_), channel_id=1, source_target_pairs={{0,3},{1,2},{2,1},{3,0},{4,7},{5,6},{6,5},{7,4},{8,11},{9,10},{10,... | collective-permute-start | bytes 6152 | tf_op jit(solution)/shard_map/ppermute | solution.py:439
  13.7 1.8 %collective-permute-done.5.refs_6_ = f32[2,256]{1,0:T(2,128)S(1)} collective-permute-done((f32[2,256]{1,0:T(2,128)S(1)}, f32[2,256]{1,0:T(2,128)S(1)}, u32[]{:S(2)}, u32[]{:S(2)}) %collective-permute-start.5) | collective-permute-done | bytes 2080 | tf_op jit(solution)/shard_map/ppermute | solution.py:439
  15.5 1.5 %shard_map.51 = (f32[2,16,16,256]{3,2,1,0:T(8,128)S(1)}, f32[2,256]{1,0:T(2,128)S(1)}) custom-call(f32[2,16,16,256]{3,2,1,0:T(8,128)S(1)} %get-tuple-element.80.refs_0_, f32[2,16,16,256]{3,2,1,0:T(8,128)S(1)} %get-tuple-element.81.refs_1_, bf16[4,3,768,256]{3,2,1,0:T(8,128)(2,1)S(1)} %shard_map.47.refs_2_.refs_1_.weights, f32[4,256]{1,0:T(4,128)S(1)} %copy-done.1, ...), custom_call_target="tpu_custom_call" | custom-call | flops 1207959552 | bytes 1048576 | tf_op jit(solution)/shard_map/pallas_call | solution.py:24
  17.0 1.3 %collective-permute-start.6 = (f32[2,256]{1,0:T(2,128)S(1)}, f32[2,256]{1,0:T(2,128)S(1)}, u32[]{:S(2)}, u32[]{:S(2)}) collective-permute-start(f32[2,256]{1,0:T(2,128)S(1)} %get-tuple-element.84.refs_4_), channel_id=1, source_target_pairs={{0,3},{1,2},{2,1},{3,0},{4,7},{5,6},{6,5},{7,4},{8,11},{9,10},{10,... | collective-permute-start | bytes 6152 | tf_op jit(solution)/shard_map/ppermute | solution.py:439
  18.3 1.8 %collective-permute-done.6.refs_5_ = f32[2,256]{1,0:T(2,128)S(1)} collective-permute-done((f32[2,256]{1,0:T(2,128)S(1)}, f32[2,256]{1,0:T(2,128)S(1)}, u32[]{:S(2)}, u32[]{:S(2)}) %collective-permute-start.6) | collective-permute-done | bytes 2080 | tf_op jit(solution)/shard_map/ppermute | solution.py:439
  21.0 3.4 %collective-permute-start.7 = (f32[2,16,16,256]{3,2,1,0:T(8,128)S(1)}, f32[2,16,16,256]{3,2,1,0:T(8,128)S(1)}, u32[]{:S(2)}, u32[]{:S(2)}) collective-permute-start(f32[2,16,16,256]{3,2,1,0:T(8,128)S(1)} %get-tuple-element.85), channel_id=1, source_target_pairs={{0,4},{4,8},{8,12},{12,16},{16,20},{20,24},{24,28},{1,5},{5,9},{9,... | collective-permute-start | bytes 1572872 | tf_op jit(solution)/shard_map/ppermute | solution.py:474
  24.4 1.0 collective-permute-start.10
  25.4 1.1 collective-permute-start.9
  26.6 0.9 collective-permute-done.10
  27.5 1.6 %collective-permute-done.9 = f32[2,256]{1,0:T(2,128)S(1)} collective-permute-done((f32[2,256]{1,0:T(2,128)S(1)}, f32[2,256]{1,0:T(2,128)S(1)}, u32[]{:S(2)}, u32[]{:S(2)}) %collective-permute-start.9) | collective-permute-done | bytes 2080 | tf_op jit(solution)/shard_map/ppermute | solution.py:439
  29.0 1.9 %collective-permute-start.11 = (f32[2,256]{1,0:T(2,128)S(1)}, f32[2,256]{1,0:T(2,128)S(1)}, u32[]{:S(2)}, u32[]{:S(2)}) collective-permute-start(f32[2,256]{1,0:T(2,128)S(1)} %add_add_fusion), channel_id=1, source_target_pairs={{0,4},{4,8},{8,12},{12,16},{16,20},{20,24},{24,28},{1,5},{5,9},{9,... | collective-permute-start | bytes 6152 | tf_op jit(solution)/shard_map/ppermute | solution.py:475
  31.1 6.7 %collective-permute-done.11.refs_4_ = f32[2,256]{1,0:T(2,128)S(1)} collective-permute-done((f32[2,256]{1,0:T(2,128)S(1)}, f32[2,256]{1,0:T(2,128)S(1)}, u32[]{:S(2)}, u32[]{:S(2)}) %collective-permute-start.11) | collective-permute-done | bytes 2080 | tf_op jit(solution)/shard_map/ppermute | solution.py:475
  37.8 0.9 shard_map.53
  38.8 1.4 %collective-permute-start.21 = (f32[576,256]{1,0:T(8,128)S(1)}, f32[576,256]{1,0:T(8,128)S(1)}, u32[]{:S(2)}, u32[]{:S(2)}) collective-permute-start(f32[576,256]{1,0:T(8,128)S(1)} %shard_map.61), channel_id=1, source_target_pairs={{0,4},{4,0},{8,12},{12,8},{16,20},{20,16},{24,28},{28,24},{1,5},{5... | collective-permute-start | bytes 1769480 | tf_op jit(solution)/shard_map/ppermute | solution.py:482
  40.3 10.2 %collective-permute-done.20.near_upper = f32[576,256]{1,0:T(8,128)S(1)} collective-permute-done((f32[576,256]{1,0:T(8,128)S(1)}, f32[576,256]{1,0:T(8,128)S(1)}, u32[]{:S(2)}, u32[]{:S(2)}) %collective-permute-start.20) | collective-permute-done | bytes 589856 | tf_op jit(solution)/shard_map/ppermute | solution.py:470
  50.5 12.5 %collective-permute-done.21.near_lower = f32[576,256]{1,0:T(8,128)S(1)} collective-permute-done((f32[576,256]{1,0:T(8,128)S(1)}, f32[576,256]{1,0:T(8,128)S(1)}, u32[]{:S(2)}, u32[]{:S(2)}) %collective-permute-start.21) | collective-permute-done | bytes 589856 | tf_op jit(solution)/shard_map/ppermute | solution.py:482
  63.5 1.5 %collective-permute-start.14 = (f32[2,256]{1,0:T(2,128)S(1)}, f32[2,256]{1,0:T(2,128)S(1)}, u32[]{:S(2)}, u32[]{:S(2)}) collective-permute-start(f32[2,256]{1,0:T(2,128)S(1)} %get-tuple-element.88.refs_0_.after), channel_id=1, source_target_pairs={{0,2},{1,3},{2,0},{3,1},{4,6},{5,7},{6,4},{7,5},{8,10},{9,11},{10,... | collective-permute-start | bytes 6152 | tf_op jit(solution)/shard_map/ppermute | solution.py:439
  65.0 1.2 %collective-permute-start.15 = (f32[2,256]{1,0:T(2,128)S(1)}, f32[2,256]{1,0:T(2,128)S(1)}, u32[]{:S(2)}, u32[]{:S(2)}) collective-permute-start(f32[2,256]{1,0:T(2,128)S(1)} %get-tuple-element.88.refs_0_.after), channel_id=1, source_target_pairs={{0,3},{1,2},{2,1},{3,0},{4,7},{5,6},{6,5},{7,4},{8,11},{9,10},{10,... | collective-permute-start | bytes 6152 | tf_op jit(solution)/shard_map/ppermute | solution.py:439
  66.3 0.9 collective-permute-done.14.refs_7_
  67.1 0.9 collective-permute-done.15.refs_8_
  68.0 1.6 %shard_map.55 = (f32[2,16,16,256]{3,2,1,0:T(8,128)S(1)}, f32[2,16,16,256]{3,2,1,0:T(8,128)S(1)}, f32[2,256]{1,0:T(2,128)S(1)}) custom-call(f32[2,16,16,256]{3,2,1,0:T(8,128)S(1)} %get-tuple-element.87.refs_0_, f32[2,16,16,256]{3,2,1,0:T(8,128)S(1)} %collective-permute-done.12.refs_1_, bf16[4,3,768,256]{3,2,1,0:T(8,128)(2,1)S(1)} %shard_map.47.refs_2_.refs_1_.weights, ...), custom_call_target="tpu_custom_call" | custom-call | flops 1207959552 | bytes 1048576 | tf_op jit(solution)/shard_map/pallas_call | solution.py:24
  69.6 1.3 %collective-permute-start.16 = (f32[2,256]{1,0:T(2,128)S(1)}, f32[2,256]{1,0:T(2,128)S(1)}, u32[]{:S(2)}, u32[]{:S(2)}) collective-permute-start(f32[2,256]{1,0:T(2,128)S(1)} %get-tuple-element.91.refs_5_), channel_id=1, source_target_pairs={{0,3},{1,2},{2,1},{3,0},{4,7},{5,6},{6,5},{7,4},{8,11},{9,10},{10,... | collective-permute-start | bytes 6152 | tf_op jit(solution)/shard_map/ppermute | solution.py:439
  70.9 1.8 %collective-permute-done.16.refs_6_ = f32[2,256]{1,0:T(2,128)S(1)} collective-permute-done((f32[2,256]{1,0:T(2,128)S(1)}, f32[2,256]{1,0:T(2,128)S(1)}, u32[]{:S(2)}, u32[]{:S(2)}) %collective-permute-start.16) | collective-permute-done | bytes 2080 | tf_op jit(solution)/shard_map/ppermute | solution.py:439
  72.7 1.5 %shard_map.56 = (f32[2,16,16,256]{3,2,1,0:T(8,128)S(1)}, f32[2,256]{1,0:T(2,128)S(1)}) custom-call(f32[2,16,16,256]{3,2,1,0:T(8,128)S(1)} %get-tuple-element.89.refs_0_, f32[2,16,16,256]{3,2,1,0:T(8,128)S(1)} %get-tuple-element.90.refs_1_, bf16[4,3,768,256]{3,2,1,0:T(8,128)(2,1)S(1)} %shard_map.47.refs_2_.refs_1_.weights, f32[4,256]{1,0:T(4,128)S(1)} %copy-done.1, ...), custom_call_target="tpu_custom_call" | custom-call | flops 1207959552 | bytes 1048576 | tf_op jit(solution)/shard_map/pallas_call | solution.py:24
  74.2 1.3 %collective-permute-start.17 = (f32[2,256]{1,0:T(2,128)S(1)}, f32[2,256]{1,0:T(2,128)S(1)}, u32[]{:S(2)}, u32[]{:S(2)}) collective-permute-start(f32[2,256]{1,0:T(2,128)S(1)} %get-tuple-element.93.refs_0_), channel_id=1, source_target_pairs={{0,3},{1,2},{2,1},{3,0},{4,7},{5,6},{6,5},{7,4},{8,11},{9,10},{10,... | collective-permute-start | bytes 6152 | tf_op jit(solution)/shard_map/ppermute | solution.py:439
  75.5 1.8 %collective-permute-done.17.refs_5_ = f32[2,256]{1,0:T(2,128)S(1)} collective-permute-done((f32[2,256]{1,0:T(2,128)S(1)}, f32[2,256]{1,0:T(2,128)S(1)}, u32[]{:S(2)}, u32[]{:S(2)}) %collective-permute-start.17) | collective-permute-done | bytes 2080 | tf_op jit(solution)/shard_map/ppermute | solution.py:439
  77.3 1.0 shard_map.58
  78.9 1.4 %collective-permute-start.25 = (f32[96,256]{1,0:T(8,128)S(1)}, f32[96,256]{1,0:T(8,128)S(1)}, u32[]{:S(2)}, u32[]{:S(2)}) collective-permute-start(f32[96,256]{1,0:T(8,128)S(1)} %get-tuple-element.100), channel_id=1, source_target_pairs={{0,4},{4,0},{8,12},{12,8},{16,20},{20,16},{24,28},{28,24},{1,5},{5... | collective-permute-start | bytes 294920 | tf_op jit(solution)/shard_map/ppermute | solution.py:506
  80.4 4.5 %collective-permute-done.18.received.refs_1_.refs_3_ = f32[136,256]{1,0:T(8,128)S(1)} collective-permute-done((f32[136,256]{1,0:T(8,128)S(1)}, f32[136,256]{1,0:T(8,128)S(1)}, u32[]{:S(2)}, u32[]{:S(2)}) %collective-permute-start.18) | collective-permute-done | bytes 139296 | tf_op jit(solution)/shard_map/ppermute | solution.py:506
  87.1 1.3 %collective-permute-start.27 = (f32[32,256]{1,0:T(8,128)S(1)}, f32[32,256]{1,0:T(8,128)S(1)}, u32[]{:S(2)}, u32[]{:S(2)}) collective-permute-start(f32[32,256]{1,0:T(8,128)S(1)} %get-tuple-element.101), channel_id=1, source_target_pairs={{0,4},{4,0},{8,12},{12,8},{16,20},{20,16},{24,28},{28,24},{1,5},{5... | collective-permute-start | bytes 98312 | tf_op jit(solution)/shard_map/ppermute | solution.py:506
  88.4 3.9 %collective-permute-done.27.received.refs_5_ = f32[32,256]{1,0:T(8,128)S(1)} collective-permute-done((f32[32,256]{1,0:T(8,128)S(1)}, f32[32,256]{1,0:T(8,128)S(1)}, u32[]{:S(2)}, u32[]{:S(2)}) %collective-permute-start.27) | collective-permute-done | bytes 32800 | tf_op jit(solution)/shard_map/ppermute | solution.py:506
  93.6 1.4 %collective-permute-start.30 = (f32[1,6,16,256]{3,2,1,0:T(8,128)S(1)}, f32[1,6,16,256]{3,2,1,0:T(8,128)S(1)}, u32[]{:S(2)}, u32[]{:S(2)}) collective-permute-start(f32[1,6,16,256]{3,2,1,0:T(8,128)S(1)} %get-tuple-element.117), channel_id=1, source_target_pairs={{0,4},{4,0},{8,16},{12,20},{16,8},{20,12},{24,28},{28,24},{1,5},{5... | collective-permute-start | bytes 294920 | tf_op jit(solution)/shard_map/ppermute | solution.py:528
  95.6 3.6 %collective-permute-done.28.refs_1_ = f32[1,2,16,256]{3,2,1,0:T(8,128)S(1)} collective-permute-done((f32[1,2,16,256]{3,2,1,0:T(8,128)S(1)}, f32[1,2,16,256]{3,2,1,0:T(8,128)S(1)}, u32[]{:S(2)}, u32[]{:S(2)}) %collective-permute-start.28) | collective-permute-done | bytes 32800 | tf_op jit(solution)/shard_map/ppermute | solution.py:528
  99.2 1.3 %collective-permute-start.31 = (f32[1,4,16,256]{3,2,1,0:T(8,128)S(1)}, f32[1,4,16,256]{3,2,1,0:T(8,128)S(1)}, u32[]{:S(2)}, u32[]{:S(2)}) collective-permute-start(f32[1,4,16,256]{3,2,1,0:T(8,128)S(1)} %get-tuple-element.118), channel_id=1, source_target_pairs={{0,4},{4,0},{8,16},{12,20},{16,8},{20,12},{24,28},{28,24},{1,5},{5... | collective-permute-start | bytes 196616 | tf_op jit(solution)/shard_map/ppermute | solution.py:528
  100.5 1.7 %collective-permute-start.29 = (f32[1,4,16,256]{3,2,1,0:T(8,128)S(1)}, f32[1,4,16,256]{3,2,1,0:T(8,128)S(1)}, u32[]{:S(2)}, u32[]{:S(2)}) collective-permute-start(f32[1,4,16,256]{3,2,1,0:T(8,128)S(1)} %get-tuple-element.116), channel_id=1, source_target_pairs={{0,4},{4,0},{8,12},{12,8},{16,24},{20,28},{24,16},{28,20},{1,5},{5... | collective-permute-start | bytes 196616 | tf_op jit(solution)/shard_map/ppermute | solution.py:528
  102.2 1.2 %collective-permute-start.33 = (f32[1,6,16,256]{3,2,1,0:T(8,128)S(1)}, f32[1,6,16,256]{3,2,1,0:T(8,128)S(1)}, u32[]{:S(2)}, u32[]{:S(2)}) collective-permute-start(f32[1,6,16,256]{3,2,1,0:T(8,128)S(1)} %get-tuple-element.133), channel_id=1, source_target_pairs={{0,4},{4,0},{8,12},{12,8},{16,24},{20,28},{24,16},{28,20},{1,5},{5... | collective-permute-start | bytes 294920 | tf_op jit(solution)/shard_map/ppermute | solution.py:528
  103.5 1.9 %collective-permute-start.35 = (f32[1,6,16,256]{3,2,1,0:T(8,128)S(1)}, f32[1,6,16,256]{3,2,1,0:T(8,128)S(1)}, u32[]{:S(2)}, u32[]{:S(2)}) collective-permute-start(f32[1,6,16,256]{3,2,1,0:T(8,128)S(1)} %get-tuple-element.139), channel_id=1, source_target_pairs={{0,4},{4,0},{8,12},{12,8},{16,24},{20,28},{24,16},{28,20},{1,5},{5... | collective-permute-start | bytes 294920 | tf_op jit(solution)/shard_map/ppermute | solution.py:528
  108.1 0.9 shard_map.73
  109.0 1.3 %collective-permute-start.36 = (f32[1,8,16,256]{3,2,1,0:T(8,128)S(1)}, f32[1,8,16,256]{3,2,1,0:T(8,128)S(1)}, u32[]{:S(2)}, u32[]{:S(2)}) collective-permute-start(f32[1,8,16,256]{3,2,1,0:T(8,128)S(1)} %get-tuple-element.143), channel_id=1, source_target_pairs={{0,4},{4,0},{8,12},{12,8},{16,20},{20,16},{24,28},{28,24},{1,5},{5... | collective-permute-start | bytes 393224 | tf_op jit(solution)/shard_map/ppermute | solution.py:555
  111.1 1.3 %collective-permute-start.32 = (f32[1,2,16,256]{3,2,1,0:T(8,128)S(1)}, f32[1,2,16,256]{3,2,1,0:T(8,128)S(1)}, u32[]{:S(2)}, u32[]{:S(2)}) collective-permute-start(f32[1,2,16,256]{3,2,1,0:T(8,128)S(1)} %get-tuple-element.132), channel_id=1, source_target_pairs={{0,4},{4,0},{8,12},{12,8},{16,20},{20,16},{24,28},{28,24},{1,5},{5... | collective-permute-start | bytes 98312 | tf_op jit(solution)/shard_map/ppermute | solution.py:555
  113.1 2.4 %collective-permute-done.32.refs_0_ = f32[1,2,16,256]{3,2,1,0:T(8,128)S(1)} collective-permute-done((f32[1,2,16,256]{3,2,1,0:T(8,128)S(1)}, f32[1,2,16,256]{3,2,1,0:T(8,128)S(1)}, u32[]{:S(2)}, u32[]{:S(2)}) %collective-permute-start.32) | collective-permute-done | bytes 32800 | tf_op jit(solution)/shard_map/ppermute | solution.py:555
  (67 shorter events, 12.5 us)
Async XLA Ops:
  0.0 1.0 copy-start
  1.2 5.1 %collective-permute-start = (f32[2,16,16,256]{3,2,1,0:T(8,128)S(1)}, f32[2,16,16,256]{3,2,1,0:T(8,128)S(1)}, u32[]{:S(2)}, u32[]{:S(2)}) collective-permute-start(f32[2,16,16,256]{3,2,1,0:T(8,128)S(1)} %get-tuple-element.75.refs_0_.refs_5_), channel_id=1, source_target_pairs={{0,1},{1,0},{2,3},{3,2},{4,5},{5,4},{6,7},{7,6},{8,9},{9,8},{10,11... | collective-permute-start | bytes 1572872 | tf_op jit(solution)/shard_map/ppermute | solution.py:454
  1.2 4.4 %collective-permute-start.1 = (f32[2,256]{1,0:T(2,128)S(1)}, f32[2,256]{1,0:T(2,128)S(1)}, u32[]{:S(2)}, u32[]{:S(2)}) collective-permute-start(f32[2,256]{1,0:T(2,128)S(1)} %get-tuple-element.76.refs_5_.refs_6_), channel_id=1, source_target_pairs={{0,1},{1,0},{2,3},{3,2},{4,5},{5,4},{6,7},{7,6},{8,9},{9,8},{10,11... | collective-permute-start | bytes 6152 | tf_op jit(solution)/shard_map/ppermute | solution.py:439
  1.7 3.9 %collective-permute-start.2 = (f32[2,256]{1,0:T(2,128)S(1)}, f32[2,256]{1,0:T(2,128)S(1)}, u32[]{:S(2)}, u32[]{:S(2)}) collective-permute-start(f32[2,256]{1,0:T(2,128)S(1)} %get-tuple-element.76.refs_5_.refs_6_), channel_id=1, source_target_pairs={{0,2},{1,3},{2,0},{3,1},{4,6},{5,7},{6,4},{7,5},{8,10},{9,11},{10,... | collective-permute-start | bytes 6152 | tf_op jit(solution)/shard_map/ppermute | solution.py:439
  3.2 3.0 %collective-permute-start.3 = (f32[2,256]{1,0:T(2,128)S(1)}, f32[2,256]{1,0:T(2,128)S(1)}, u32[]{:S(2)}, u32[]{:S(2)}) collective-permute-start(f32[2,256]{1,0:T(2,128)S(1)} %get-tuple-element.76.refs_5_.refs_6_), channel_id=1, source_target_pairs={{0,3},{1,2},{2,1},{3,0},{4,7},{5,6},{6,5},{7,4},{8,11},{9,10},{10,... | collective-permute-start | bytes 6152 | tf_op jit(solution)/shard_map/ppermute | solution.py:439
  3.2 3.0 %copy-start.1 = (f32[4,256]{1,0:T(4,128)S(1)}, f32[4,256]{1,0:T(4,128)}, u32[]{:S(2)}) copy-start(f32[4,256]{1,0:T(4,128)} %refs_2_.5) | copy-start | bytes 12292
  3.2 3.0 %copy-start.2 = (f32[4,256]{1,0:T(4,128)S(1)}, f32[4,256]{1,0:T(4,128)}, u32[]{:S(2)}) copy-start(f32[4,256]{1,0:T(4,128)} %refs_3_.15) | copy-start | bytes 12292
  7.8 3.1 %collective-permute-start.4 = (f32[2,256]{1,0:T(2,128)S(1)}, f32[2,256]{1,0:T(2,128)S(1)}, u32[]{:S(2)}, u32[]{:S(2)}) collective-permute-start(f32[2,256]{1,0:T(2,128)S(1)} %get-tuple-element.79.refs_0_.after), channel_id=1, source_target_pairs={{0,3},{1,2},{2,1},{3,0},{4,7},{5,6},{6,5},{7,4},{8,11},{9,10},{10,... | collective-permute-start | bytes 6152 | tf_op jit(solution)/shard_map/ppermute | solution.py:439
  12.4 3.1 %collective-permute-start.5 = (f32[2,256]{1,0:T(2,128)S(1)}, f32[2,256]{1,0:T(2,128)S(1)}, u32[]{:S(2)}, u32[]{:S(2)}) collective-permute-start(f32[2,256]{1,0:T(2,128)S(1)} %get-tuple-element.82.refs_5_), channel_id=1, source_target_pairs={{0,3},{1,2},{2,1},{3,0},{4,7},{5,6},{6,5},{7,4},{8,11},{9,10},{10,... | collective-permute-start | bytes 6152 | tf_op jit(solution)/shard_map/ppermute | solution.py:439
  17.0 3.1 %collective-permute-start.6 = (f32[2,256]{1,0:T(2,128)S(1)}, f32[2,256]{1,0:T(2,128)S(1)}, u32[]{:S(2)}, u32[]{:S(2)}) collective-permute-start(f32[2,256]{1,0:T(2,128)S(1)} %get-tuple-element.84.refs_4_), channel_id=1, source_target_pairs={{0,3},{1,2},{2,1},{3,0},{4,7},{5,6},{6,5},{7,4},{8,11},{9,10},{10,... | collective-permute-start | bytes 6152 | tf_op jit(solution)/shard_map/ppermute | solution.py:439
  21.0 16.9 %collective-permute-start.7 = (f32[2,16,16,256]{3,2,1,0:T(8,128)S(1)}, f32[2,16,16,256]{3,2,1,0:T(8,128)S(1)}, u32[]{:S(2)}, u32[]{:S(2)}) collective-permute-start(f32[2,16,16,256]{3,2,1,0:T(8,128)S(1)} %get-tuple-element.85), channel_id=1, source_target_pairs={{0,4},{4,8},{8,12},{12,16},{16,20},{20,24},{24,28},{1,5},{5,9},{9,... | collective-permute-start | bytes 1572872 | tf_op jit(solution)/shard_map/ppermute | solution.py:474
  24.4 3.1 %collective-permute-start.10 = (f32[2,256]{1,0:T(2,128)S(1)}, f32[2,256]{1,0:T(2,128)S(1)}, u32[]{:S(2)}, u32[]{:S(2)}) collective-permute-start(f32[2,256]{1,0:T(2,128)S(1)} %get-tuple-element.86), channel_id=1, source_target_pairs={{0,3},{1,2},{2,1},{3,0},{4,7},{5,6},{6,5},{7,4},{8,11},{9,10},{10,... | collective-permute-start | bytes 6152 | tf_op jit(solution)/shard_map/ppermute | solution.py:439
  25.4 2.1 %collective-permute-start.8 = (f32[2,256]{1,0:T(2,128)S(1)}, f32[2,256]{1,0:T(2,128)S(1)}, u32[]{:S(2)}, u32[]{:S(2)}) collective-permute-start(f32[2,256]{1,0:T(2,128)S(1)} %get-tuple-element.86), channel_id=1, source_target_pairs={{0,1},{1,0},{2,3},{3,2},{4,5},{5,4},{6,7},{7,6},{8,9},{9,8},{10,11... | collective-permute-start | bytes 6152 | tf_op jit(solution)/shard_map/ppermute | solution.py:439
  25.4 3.6 %collective-permute-start.9 = (f32[2,256]{1,0:T(2,128)S(1)}, f32[2,256]{1,0:T(2,128)S(1)}, u32[]{:S(2)}, u32[]{:S(2)}) collective-permute-start(f32[2,256]{1,0:T(2,128)S(1)} %get-tuple-element.86), channel_id=1, source_target_pairs={{0,2},{1,3},{2,0},{3,1},{4,6},{5,7},{6,4},{7,5},{8,10},{9,11},{10,... | collective-permute-start | bytes 6152 | tf_op jit(solution)/shard_map/ppermute | solution.py:439
  29.0 8.8 %collective-permute-start.11 = (f32[2,256]{1,0:T(2,128)S(1)}, f32[2,256]{1,0:T(2,128)S(1)}, u32[]{:S(2)}, u32[]{:S(2)}) collective-permute-start(f32[2,256]{1,0:T(2,128)S(1)} %add_add_fusion), channel_id=1, source_target_pairs={{0,4},{4,8},{8,12},{12,16},{16,20},{20,24},{24,28},{1,5},{5,9},{9,... | collective-permute-start | bytes 6152 | tf_op jit(solution)/shard_map/ppermute | solution.py:475
  31.0 19.5 %collective-permute-start.20 = (f32[576,256]{1,0:T(8,128)S(1)}, f32[576,256]{1,0:T(8,128)S(1)}, u32[]{:S(2)}, u32[]{:S(2)}) collective-permute-start(f32[576,256]{1,0:T(8,128)S(1)} %shard_map.60), channel_id=1, source_target_pairs={{0,4},{4,0},{8,12},{12,8},{16,20},{20,16},{24,28},{28,24},{1,5},{5... | collective-permute-start | bytes 1769480 | tf_op jit(solution)/shard_map/ppermute | solution.py:470
  38.8 24.2 %collective-permute-start.21 = (f32[576,256]{1,0:T(8,128)S(1)}, f32[576,256]{1,0:T(8,128)S(1)}, u32[]{:S(2)}, u32[]{:S(2)}) collective-permute-start(f32[576,256]{1,0:T(8,128)S(1)} %shard_map.61), channel_id=1, source_target_pairs={{0,4},{4,0},{8,12},{12,8},{16,20},{20,16},{24,28},{28,24},{1,5},{5... | collective-permute-start | bytes 1769480 | tf_op jit(solution)/shard_map/ppermute | solution.py:482
  40.3 27.8 %collective-permute-start.12 = (f32[2,16,16,256]{3,2,1,0:T(8,128)S(1)}, f32[2,16,16,256]{3,2,1,0:T(8,128)S(1)}, u32[]{:S(2)}, u32[]{:S(2)}) collective-permute-start(f32[2,16,16,256]{3,2,1,0:T(8,128)S(1)} %get-tuple-element.87.refs_0_), channel_id=1, source_target_pairs={{0,1},{1,0},{2,3},{3,2},{4,5},{5,4},{6,7},{7,6},{8,9},{9,8},{10,11... | collective-permute-start | bytes 1572872 | tf_op jit(solution)/shard_map/ppermute | solution.py:481
  50.5 41.9 %collective-permute-start.22 = (f32[576,256]{1,0:T(8,128)S(1)}, f32[576,256]{1,0:T(8,128)S(1)}, u32[]{:S(2)}, u32[]{:S(2)}) collective-permute-start(f32[576,256]{1,0:T(8,128)S(1)} %collective-permute-done.20.near_upper), channel_id=1, source_target_pairs={{0,1},{1,0},{2,3},{3,2},{4,5},{5,4},{6,7},{7,6},{8,9},{9,8},{10,11... | collective-permute-start | bytes 1769480 | tf_op jit(solution)/shard_map/ppermute | solution.py:483
  63.0 29.3 %collective-permute-start.23 = (f32[576,256]{1,0:T(8,128)S(1)}, f32[576,256]{1,0:T(8,128)S(1)}, u32[]{:S(2)}, u32[]{:S(2)}) collective-permute-start(f32[576,256]{1,0:T(8,128)S(1)} %collective-permute-done.21.near_lower), channel_id=1, source_target_pairs={{0,1},{1,0},{2,3},{3,2},{4,5},{5,4},{6,7},{7,6},{8,9},{9,8},{10,11... | collective-permute-start | bytes 1769480 | tf_op jit(solution)/shard_map/ppermute | solution.py:489
  63.0 2.0 %collective-permute-start.13 = (f32[2,256]{1,0:T(2,128)S(1)}, f32[2,256]{1,0:T(2,128)S(1)}, u32[]{:S(2)}, u32[]{:S(2)}) collective-permute-start(f32[2,256]{1,0:T(2,128)S(1)} %get-tuple-element.88.refs_0_.after), channel_id=1, source_target_pairs={{0,1},{1,0},{2,3},{3,2},{4,5},{5,4},{6,7},{7,6},{8,9},{9,8},{10,11... | collective-permute-start | bytes 6152 | tf_op jit(solution)/shard_map/ppermute | solution.py:439
  63.5 3.6 %collective-permute-start.14 = (f32[2,256]{1,0:T(2,128)S(1)}, f32[2,256]{1,0:T(2,128)S(1)}, u32[]{:S(2)}, u32[]{:S(2)}) collective-permute-start(f32[2,256]{1,0:T(2,128)S(1)} %get-tuple-element.88.refs_0_.after), channel_id=1, source_target_pairs={{0,2},{1,3},{2,0},{3,1},{4,6},{5,7},{6,4},{7,5},{8,10},{9,11},{10,... | collective-permute-start | bytes 6152 | tf_op jit(solution)/shard_map/ppermute | solution.py:439
  65.0 3.0 %collective-permute-start.15 = (f32[2,256]{1,0:T(2,128)S(1)}, f32[2,256]{1,0:T(2,128)S(1)}, u32[]{:S(2)}, u32[]{:S(2)}) collective-permute-start(f32[2,256]{1,0:T(2,128)S(1)} %get-tuple-element.88.refs_0_.after), channel_id=1, source_target_pairs={{0,3},{1,2},{2,1},{3,0},{4,7},{5,6},{6,5},{7,4},{8,11},{9,10},{10,... | collective-permute-start | bytes 6152 | tf_op jit(solution)/shard_map/ppermute | solution.py:439
  69.6 3.1 %collective-permute-start.16 = (f32[2,256]{1,0:T(2,128)S(1)}, f32[2,256]{1,0:T(2,128)S(1)}, u32[]{:S(2)}, u32[]{:S(2)}) collective-permute-start(f32[2,256]{1,0:T(2,128)S(1)} %get-tuple-element.91.refs_5_), channel_id=1, source_target_pairs={{0,3},{1,2},{2,1},{3,0},{4,7},{5,6},{6,5},{7,4},{8,11},{9,10},{10,... | collective-permute-start | bytes 6152 | tf_op jit(solution)/shard_map/ppermute | solution.py:439
  74.2 3.1 %collective-permute-start.17 = (f32[2,256]{1,0:T(2,128)S(1)}, f32[2,256]{1,0:T(2,128)S(1)}, u32[]{:S(2)}, u32[]{:S(2)}) collective-permute-start(f32[2,256]{1,0:T(2,128)S(1)} %get-tuple-element.93.refs_0_), channel_id=1, source_target_pairs={{0,3},{1,2},{2,1},{3,0},{4,7},{5,6},{6,5},{7,4},{8,11},{9,10},{10,... | collective-permute-start | bytes 6152 | tf_op jit(solution)/shard_map/ppermute | solution.py:439
  78.3 6.6 %collective-permute-start.18 = (f32[136,256]{1,0:T(8,128)S(1)}, f32[136,256]{1,0:T(8,128)S(1)}, u32[]{:S(2)}, u32[]{:S(2)}) collective-permute-start(f32[136,256]{1,0:T(8,128)S(1)} %get-tuple-element.96), channel_id=1, source_target_pairs={{0,4},{4,0},{8,12},{12,8},{16,20},{20,16},{24,28},{28,24},{1,5},{5... | collective-permute-start | bytes 417800 | tf_op jit(solution)/shard_map/ppermute | solution.py:506
  78.9 7.4 %collective-permute-start.25 = (f32[96,256]{1,0:T(8,128)S(1)}, f32[96,256]{1,0:T(8,128)S(1)}, u32[]{:S(2)}, u32[]{:S(2)}) collective-permute-start(f32[96,256]{1,0:T(8,128)S(1)} %get-tuple-element.100), channel_id=1, source_target_pairs={{0,4},{4,0},{8,12},{12,8},{16,20},{20,16},{24,28},{28,24},{1,5},{5... | collective-permute-start | bytes 294920 | tf_op jit(solution)/shard_map/ppermute | solution.py:506
  84.9 7.7 %collective-permute-start.19 = (f32[1,8,16,256]{3,2,1,0:T(8,128)S(1)}, f32[1,8,16,256]{3,2,1,0:T(8,128)S(1)}, u32[]{:S(2)}, u32[]{:S(2)}) collective-permute-start(f32[1,8,16,256]{3,2,1,0:T(8,128)S(1)} %shard_map.59), channel_id=1, source_target_pairs={{0,8},{4,12},{8,0},{12,4},{16,20},{20,16},{24,28},{28,24},{1,9},{5... | collective-permute-start | bytes 393224 | tf_op jit(solution)/shard_map/ppermute | solution.py:528
  86.3 7.2 %collective-permute-start.26 = (f32[1,6,16,256]{3,2,1,0:T(8,128)S(1)}, f32[1,6,16,256]{3,2,1,0:T(8,128)S(1)}, u32[]{:S(2)}, u32[]{:S(2)}) collective-permute-start(f32[1,6,16,256]{3,2,1,0:T(8,128)S(1)} %shard_map.64), channel_id=1, source_target_pairs={{0,8},{4,12},{8,0},{12,4},{16,20},{20,16},{24,28},{28,24},{1,9},{5... | collective-permute-start | bytes 294920 | tf_op jit(solution)/shard_map/ppermute | solution.py:528
  87.1 5.2 %collective-permute-start.27 = (f32[32,256]{1,0:T(8,128)S(1)}, f32[32,256]{1,0:T(8,128)S(1)}, u32[]{:S(2)}, u32[]{:S(2)}) collective-permute-start(f32[32,256]{1,0:T(8,128)S(1)} %get-tuple-element.101), channel_id=1, source_target_pairs={{0,4},{4,0},{8,12},{12,8},{16,20},{20,16},{24,28},{28,24},{1,5},{5... | collective-permute-start | bytes 98312 | tf_op jit(solution)/shard_map/ppermute | solution.py:506
  92.9 7.6 %collective-permute-start.24 = (f32[1,6,16,256]{3,2,1,0:T(8,128)S(1)}, f32[1,6,16,256]{3,2,1,0:T(8,128)S(1)}, u32[]{:S(2)}, u32[]{:S(2)}) collective-permute-start(f32[1,6,16,256]{3,2,1,0:T(8,128)S(1)} %get-tuple-element.99), channel_id=1, source_target_pairs={{0,4},{4,0},{8,16},{12,20},{16,8},{20,12},{24,28},{28,24},{1,5},{5... | collective-permute-start | bytes 294920 | tf_op jit(solution)/shard_map/ppermute | solution.py:528
  93.6 8.7 %collective-permute-start.30 = (f32[1,6,16,256]{3,2,1,0:T(8,128)S(1)}, f32[1,6,16,256]{3,2,1,0:T(8,128)S(1)}, u32[]{:S(2)}, u32[]{:S(2)}) collective-permute-start(f32[1,6,16,256]{3,2,1,0:T(8,128)S(1)} %get-tuple-element.117), channel_id=1, source_target_pairs={{0,4},{4,0},{8,16},{12,20},{16,8},{20,12},{24,28},{28,24},{1,5},{5... | collective-permute-start | bytes 294920 | tf_op jit(solution)/shard_map/ppermute | solution.py:528
  95.0 4.2 %collective-permute-start.28 = (f32[1,2,16,256]{3,2,1,0:T(8,128)S(1)}, f32[1,2,16,256]{3,2,1,0:T(8,128)S(1)}, u32[]{:S(2)}, u32[]{:S(2)}) collective-permute-start(f32[1,2,16,256]{3,2,1,0:T(8,128)S(1)} %shard_map.65), channel_id=1, source_target_pairs={{0,8},{4,12},{8,0},{12,4},{16,20},{20,16},{24,28},{28,24},{1,9},{5... | collective-permute-start | bytes 98312 | tf_op jit(solution)/shard_map/ppermute | solution.py:528
  99.2 4.3 %collective-permute-start.31 = (f32[1,4,16,256]{3,2,1,0:T(8,128)S(1)}, f32[1,4,16,256]{3,2,1,0:T(8,128)S(1)}, u32[]{:S(2)}, u32[]{:S(2)}) collective-permute-start(f32[1,4,16,256]{3,2,1,0:T(8,128)S(1)} %get-tuple-element.118), channel_id=1, source_target_pairs={{0,4},{4,0},{8,16},{12,20},{16,8},{20,12},{24,28},{28,24},{1,5},{5... | collective-permute-start | bytes 196616 | tf_op jit(solution)/shard_map/ppermute | solution.py:528
  100.5 5.0 %collective-permute-start.29 = (f32[1,4,16,256]{3,2,1,0:T(8,128)S(1)}, f32[1,4,16,256]{3,2,1,0:T(8,128)S(1)}, u32[]{:S(2)}, u32[]{:S(2)}) collective-permute-start(f32[1,4,16,256]{3,2,1,0:T(8,128)S(1)} %get-tuple-element.116), channel_id=1, source_target_pairs={{0,4},{4,0},{8,12},{12,8},{16,24},{20,28},{24,16},{28,20},{1,5},{5... | collective-permute-start | bytes 196616 | tf_op jit(solution)/shard_map/ppermute | solution.py:528
  102.2 4.6 %collective-permute-start.33 = (f32[1,6,16,256]{3,2,1,0:T(8,128)S(1)}, f32[1,6,16,256]{3,2,1,0:T(8,128)S(1)}, u32[]{:S(2)}, u32[]{:S(2)}) collective-permute-start(f32[1,6,16,256]{3,2,1,0:T(8,128)S(1)} %get-tuple-element.133), channel_id=1, source_target_pairs={{0,4},{4,0},{8,12},{12,8},{16,24},{20,28},{24,16},{28,20},{1,5},{5... | collective-permute-start | bytes 294920 | tf_op jit(solution)/shard_map/ppermute | solution.py:528
  103.5 4.6 %collective-permute-start.35 = (f32[1,6,16,256]{3,2,1,0:T(8,128)S(1)}, f32[1,6,16,256]{3,2,1,0:T(8,128)S(1)}, u32[]{:S(2)}, u32[]{:S(2)}) collective-permute-start(f32[1,6,16,256]{3,2,1,0:T(8,128)S(1)} %get-tuple-element.139), channel_id=1, source_target_pairs={{0,4},{4,0},{8,12},{12,8},{16,24},{20,28},{24,16},{28,20},{1,5},{5... | collective-permute-start | bytes 294920 | tf_op jit(solution)/shard_map/ppermute | solution.py:528
  109.0 6.4 %collective-permute-start.36 = (f32[1,8,16,256]{3,2,1,0:T(8,128)S(1)}, f32[1,8,16,256]{3,2,1,0:T(8,128)S(1)}, u32[]{:S(2)}, u32[]{:S(2)}) collective-permute-start(f32[1,8,16,256]{3,2,1,0:T(8,128)S(1)} %get-tuple-element.143), channel_id=1, source_target_pairs={{0,4},{4,0},{8,12},{12,8},{16,20},{20,16},{24,28},{28,24},{1,5},{5... | collective-permute-start | bytes 393224 | tf_op jit(solution)/shard_map/ppermute | solution.py:555
  110.3 5.1 %collective-permute-start.34 = (f32[1,6,16,256]{3,2,1,0:T(8,128)S(1)}, f32[1,6,16,256]{3,2,1,0:T(8,128)S(1)}, u32[]{:S(2)}, u32[]{:S(2)}) collective-permute-start(f32[1,6,16,256]{3,2,1,0:T(8,128)S(1)} %get-tuple-element.138), channel_id=1, source_target_pairs={{0,4},{4,0},{8,12},{12,8},{16,20},{20,16},{24,28},{28,24},{1,5},{5... | collective-permute-start | bytes 294920 | tf_op jit(solution)/shard_map/ppermute | solution.py:555
  111.1 4.3 %collective-permute-start.32 = (f32[1,2,16,256]{3,2,1,0:T(8,128)S(1)}, f32[1,2,16,256]{3,2,1,0:T(8,128)S(1)}, u32[]{:S(2)}, u32[]{:S(2)}) collective-permute-start(f32[1,2,16,256]{3,2,1,0:T(8,128)S(1)} %get-tuple-element.132), channel_id=1, source_target_pairs={{0,4},{4,0},{8,12},{12,8},{16,20},{20,16},{24,28},{28,24},{1,5},{5... | collective-permute-start | bytes 98312 | tf_op jit(solution)/shard_map/ppermute | solution.py:555

commit v3 on v2

--- a/solution.py
+++ b/solution.py
@@ -106,7 +106,7 @@
         outs, taps = refs[1 + len(initial_totals) : -1], refs[-1]
     elif kind == "last":
         coarse_begin, terms = refs[:2]
-        outs, taps = refs[2:-1], refs[-1]
+        outs, taps, kept_forcing = refs[2:-2], refs[-2], refs[-1]
     else:
         outs, taps = refs[:-1], refs[-1]
     samples, rows, width, channels = states[0].shape
@@ -141,7 +141,7 @@
             begun = coarse_begin[i].reshape(entries, channels)
             forcing = made - begun
             outs[0][i] = (begun + forcing).reshape(rows, width, channels)
-            outs[1][i] = forcing
+            kept_forcing[i] = forcing
         else:
             if i < keep * samples:
                 outs[i // samples][i % samples] = made.reshape(rows, width, channels)
@@ -152,8 +152,9 @@
         half = samples // 2
         other = (1 - position % 2) * half
         for i in range(half):
+            outs[1][i] = kept_forcing[position % 2 * half + i]
             sent = jnp.where(
-                position == 1, outs[0][other + i].reshape(entries, channels), outs[1][other + i]
+                position == 1, outs[0][other + i].reshape(entries, channels), kept_forcing[other + i]
             )
             for (low, high), out in zip(spans(cut, rows), outs[2:]):
                 size = (high - low) * width
@@ -175,7 +176,7 @@
     if kind == "last":
         outs = (
             f32(*state.shape),
-            f32(samples, entries, channels),
+            f32(half, entries, channels),
             *(
                 f32(half * (high - low) * width + (8 if low == 0 else 0), channels)
                 for low, high in spans(cut, rows)
@@ -191,7 +192,8 @@
         ),
         (*states, weights, gains, offsets, *totals, *extra),
         outs,
-        [pltpu.VMEM((len(states) * samples, entries + 2 * width, 3 * channels), jnp.bfloat16)],
+        [pltpu.VMEM((len(states) * samples, entries + 2 * width, 3 * channels), jnp.bfloat16)]
+        + ([pltpu.VMEM((samples, entries, channels), jnp.float32)] if kind == "last" else []),
         flops=2 * len(states) * samples * entries * 9 * channels * channels,
         moved=4 * len(states) * samples * entries * channels,
     )
@@ -274,7 +276,7 @@
         return values[0] if len(values) == 1 else jnp.concatenate(values, axis=0)
 
     def forced(stage, i, low, high):
-        here = forcing[parity * half + i, low * width : high * width]
+        here = forcing[i, low * width : high * width]
         there = []
         for (first, end), ref in zip(spans(start_cuts, height), exchange):
             a, b = max(low, first), min(high, end)
@@ -379,21 +381,21 @@
     return outs[: len(made)], rest[0], dict(zip(kept, rest[1:]))
 
 
-def finish_own_kernel(early, own, out, done):
+def finish_own_kernel(early, own, own_other, out, done):
     half = own.shape[0]
     position = lax.axis_index("depth")
-
-    @pl.when(position < 2)
-    def _():
-        copy = pltpu.make_async_copy(early, out, done)
-        copy.start()
-        copy.wait()
-
-    @pl.when(position >= 2)
-    def _():
-        copy = pltpu.make_async_copy(own, out.at[pl.ds((position % 2) * half, half)], done)
-        copy.start()
-        copy.wait()
+    here = out.at[pl.ds((position % 2) * half, half)]
+    for condition, source, target in (
+        (position < 2, early, out),
+        ((position >= 2) & (position // 2 % 2 == 0), own, here),
+        (position // 2 % 2 == 1, own_other, here),
+    ):
+
+        @pl.when(condition)
+        def _(source=source, target=target):
+            copy = pltpu.make_async_copy(source, target, done)
+            copy.start()
+            copy.wait()
 
 
 def finish_kernel(cuts, *refs):
@@ -443,6 +445,16 @@
             sums = call(copy_kernel, (sums, *ready), f32(*sums.shape))
         return (sums, *others)
 
+    both = ("depth", "batch")
+
+    def routes(of):
+        return [
+            (i * group + b, of(i)[0] * group + (b ^ 1 if of(i)[1] else b))
+            for i in range(devices)
+            for b in range(group)
+        ]
+
+    swaps = routes(lambda i: (i ^ 1, i // 2 % 2 == 1))
     partners = [(i, i ^ 1) for i in range(devices)]
     cores = [(i, i ^ 1) for i in range(group)]
     onward = [(i, i + 1) for i in range(devices - 1)]
@@ -487,7 +499,7 @@
         keep = 2 if number < layers_of_block - 2 else 1
         *states, sums = run(number, states, *norms, totals, kind="plain", keep=keep)
     far_lower = lax.ppermute(near_lower, "batch", cores)
-    early, forcing, *sent = run(
+    early, mine, *sent = run(
         layers_of_block - 1,
         states[:1],
         *norms,
@@ -503,7 +515,8 @@
         moved=9 * channels * channels * 8,
     )
 
-    exchange = [lax.ppermute(part, "depth", partners) for part in sent]
+    exchange = [lax.ppermute(part, both, swaps) for part in sent]
+    mine_other = lax.ppermute(mine, "batch", cores)
     passed = [
         call(
             functools.partial(relay_kernel, low, high),
@@ -520,12 +533,14 @@
     }
     back_spans = list(gives)
     back = []
-    shared = (forcing, terms, kernels)
     for turn, (cuts, split, out_cuts) in enumerate(plan, 1):
-        across = {2 * turn - 2: 2 * turn, 2 * turn - 1: 2 * turn + 1}
-        across.update({b: a for a, b in across.items()})
-        route = [(i, across.get(i, i ^ 1)) for i in range(devices)]
-        arriving = [lax.ppermute(part, "depth", route) for part in passed]
+        across = {}
+        for first in (turn - 1, *range(0, turn - 2, 2), *range(turn + 1, devices // 2 - 1, 2)):
+            for i in (2 * first, 2 * first + 1):
+                across[i], across[i + 2] = (i + 2, first == turn - 1), (i, first == turn - 1)
+        route = routes(lambda i: across.get(i, (i ^ 1, False)))
+        arriving = [lax.ppermute(part, both, route) for part in passed]
+        shared = (mine_other if turn % 2 else mine, terms, kernels)
         last = turn == len(plan)
         if not split:
             passed, own, gives = pair(
@@ -552,14 +567,14 @@
             gives = {**gives, **now}
             halo = tuple(made[:1]) if n < len(cuts) else ()
             if last:
-                back.append(lax.ppermute(gives[back_spans[n]], "depth", partners))
+                back.append(lax.ppermute(gives[back_spans[n]], both, swaps))
             else:
                 passed.append(made[-1])
     if not back:
-        back = [lax.ppermute(part, "depth", partners) for part in gives.values()]
+        back = [lax.ppermute(part, both, swaps) for part in gives.values()]
     out = call(
         finish_own_kernel,
-        (early, own),
+        (early, own, lax.ppermute(own, "batch", cores)),
         f32(*initial.shape),
         [pltpu.SemaphoreType.DMA],
         out_specs=in_place,

time: 118 us -> 120 us (1.017)
  waiting for transfers between devices: 59.6 us -> 64.5 us
  starting transfers between devices: 37.7 us -> 35.5 us
    ppermute x15 -> x17, waiting for transfers between devices: 16.2 us -> 21.1 us  [the longest x9 8.88 us: steps(): arriving = [lax.ppermute(part, both, route) for part in passed]]
    ppermute x15 -> x17, starting transfers between devices: 17.1 us -> 14.8 us  [the longest x9 9.51 us: steps(): arriving = [lax.ppermute(part, both, route) for part in passed]]
  transfers between devices with their start and end apart: 37 -> 39, of which waited for: 21 -> 23; matrix products, arithmetic and copies ran while one was open for 0% -> 0% of each run, Pallas kernels for 9% -> 9%
where the time goes in v3:
time: 120 us; the launch traced here: 119 us
  waiting for transfers between devices  64.5 us (54%)
  starting transfers between devices  35.5 us (30%)
  Pallas kernels  17.5 us (15%)
    pallas_call x30, Pallas kernels, call(): pl.pallas_call(body, out_shape=outs, in_specs=[whole] * len(operands) if...  17.5 us
    ppermute x14, waiting for transfers between devices, gathered(): lax.ppermute(sums, 'batch', [(i, i ^ m) for i in range(group)])  13.8 us
    ppermute x14, starting transfers between devices, gathered(): lax.ppermute(sums, 'batch', [(i, i ^ m) for i in range(group)])  13.7 us
    ppermute x1, waiting for transfers between devices, steps(): near_lower = lax.ppermute(widen(1, weights, sums), 'depth', partners)  12.5 us
    ppermute x1, waiting for transfers between devices, steps(): near_upper = lax.ppermute(widen(0, weights, sums), 'depth', partners)  10.2 us
    ppermute x9, starting transfers between devices, steps(): arriving = [lax.ppermute(part, both, route) for part in passed]  9.51 us
    ppermute x9, waiting for transfers between devices, steps(): arriving = [lax.ppermute(part, both, route) for part in passed]  8.88 us
    ppermute x3, waiting for transfers between devices, steps(): exchange = [lax.ppermute(part, both, swaps) for part in sent]  7.42 us
  transfers between devices with their start and end apart: 39, of which 23 were waited for; matrix products, arithmetic and copies ran while one was open for 0% of the time, Pallas kernels for 9%

profile of v3, /device:TPU:24, one launch (start us, length us, event | category | flops | bytes accessed | tf_op | source)
XLA Modules:
  0.0 119.0 jit_solution(16002916858888343446)
XLA Ops:
  0.0 1.0 copy-done
  1.7 1.5 %collective-permute-start.2 = (f32[2,256]{1,0:T(2,128)S(1)}, f32[2,256]{1,0:T(2,128)S(1)}, u32[]{:S(2)}, u32[]{:S(2)}) collective-permute-start(f32[2,256]{1,0:T(2,128)S(1)} %get-tuple-element.76.refs_5_.refs_6_), channel_id=1, source_target_pairs={{0,2},{1,3},{2,0},{3,1},{4,6},{5,7},{6,4},{7,5},{8,10},{9,11},{10,... | collective-permute-start | bytes 6152 | tf_op jit(solution)/shard_map/ppermute | solution.py:441
  3.2 2.4 %shard_map.47.refs_2_.refs_1_.weights = bf16[4,3,768,256]{3,2,1,0:T(8,128)(2,1)S(1)} custom-call(bf16[4,3,768,256]{3,2,1,0:T(8,128)(2,1)} %bitcast.4), custom_call_target="tpu_custom_call" | custom-call | bytes 9437184 | tf_op jit(solution)/shard_map/pallas_call | solution.py:24
  6.2 1.5 %shard_map.48 = (f32[2,16,16,256]{3,2,1,0:T(8,128)S(1)}, f32[2,16,16,256]{3,2,1,0:T(8,128)S(1)}, f32[2,256]{1,0:T(2,128)S(1)}) custom-call(f32[2,16,16,256]{3,2,1,0:T(8,128)S(1)} %get-tuple-element.75.refs_0_.refs_5_, f32[2,16,16,256]{3,2,1,0:T(8,128)S(1)} %collective-permute-done.refs_1_, bf16[4,3,768,256]{3,2,1,0:T(8,128)(2,1)S(1)} %shard_map.47.refs_2_.refs_1_.weights, ...), custom_call_target="tpu_custom_call" | custom-call | flops 1207959552 | bytes 1048576 | tf_op jit(solution)/shard_map/pallas_call | solution.py:24
  7.8 1.3 %collective-permute-start.4 = (f32[2,256]{1,0:T(2,128)S(1)}, f32[2,256]{1,0:T(2,128)S(1)}, u32[]{:S(2)}, u32[]{:S(2)}) collective-permute-start(f32[2,256]{1,0:T(2,128)S(1)} %get-tuple-element.79.refs_0_.after), channel_id=1, source_target_pairs={{0,3},{1,2},{2,1},{3,0},{4,7},{5,6},{6,5},{7,4},{8,11},{9,10},{10,... | collective-permute-start | bytes 6152 | tf_op jit(solution)/shard_map/ppermute | solution.py:441
  9.1 1.8 %collective-permute-done.4.refs_6_ = f32[2,256]{1,0:T(2,128)S(1)} collective-permute-done((f32[2,256]{1,0:T(2,128)S(1)}, f32[2,256]{1,0:T(2,128)S(1)}, u32[]{:S(2)}, u32[]{:S(2)}) %collective-permute-start.4) | collective-permute-done | bytes 2080 | tf_op jit(solution)/shard_map/ppermute | solution.py:441
  10.9 1.5 %shard_map.50 = (f32[2,16,16,256]{3,2,1,0:T(8,128)S(1)}, f32[2,16,16,256]{3,2,1,0:T(8,128)S(1)}, f32[2,256]{1,0:T(2,128)S(1)}) custom-call(f32[2,16,16,256]{3,2,1,0:T(8,128)S(1)} %get-tuple-element.77.refs_0_, f32[2,16,16,256]{3,2,1,0:T(8,128)S(1)} %get-tuple-element.78.refs_1_, bf16[4,3,768,256]{3,2,1,0:T(8,128)(2,1)S(1)} %shard_map.47.refs_2_.refs_1_.weights, ...), custom_call_target="tpu_custom_call" | custom-call | flops 1207959552 | bytes 1048576 | tf_op jit(solution)/shard_map/pallas_call | solution.py:24
  12.4 1.3 %collective-permute-start.5 = (f32[2,256]{1,0:T(2,128)S(1)}, f32[2,256]{1,0:T(2,128)S(1)}, u32[]{:S(2)}, u32[]{:S(2)}) collective-permute-start(f32[2,256]{1,0:T(2,128)S(1)} %get-tuple-element.82.refs_5_), channel_id=1, source_target_pairs={{0,3},{1,2},{2,1},{3,0},{4,7},{5,6},{6,5},{7,4},{8,11},{9,10},{10,... | collective-permute-start | bytes 6152 | tf_op jit(solution)/shard_map/ppermute | solution.py:441
  13.7 1.8 %collective-permute-done.5.refs_6_ = f32[2,256]{1,0:T(2,128)S(1)} collective-permute-done((f32[2,256]{1,0:T(2,128)S(1)}, f32[2,256]{1,0:T(2,128)S(1)}, u32[]{:S(2)}, u32[]{:S(2)}) %collective-permute-start.5) | collective-permute-done | bytes 2080 | tf_op jit(solution)/shard_map/ppermute | solution.py:441
  15.5 1.5 %shard_map.51 = (f32[2,16,16,256]{3,2,1,0:T(8,128)S(1)}, f32[2,256]{1,0:T(2,128)S(1)}) custom-call(f32[2,16,16,256]{3,2,1,0:T(8,128)S(1)} %get-tuple-element.80.refs_0_, f32[2,16,16,256]{3,2,1,0:T(8,128)S(1)} %get-tuple-element.81.refs_1_, bf16[4,3,768,256]{3,2,1,0:T(8,128)(2,1)S(1)} %shard_map.47.refs_2_.refs_1_.weights, f32[4,256]{1,0:T(4,128)S(1)} %copy-done.1, ...), custom_call_target="tpu_custom_call" | custom-call | flops 1207959552 | bytes 1048576 | tf_op jit(solution)/shard_map/pallas_call | solution.py:24
  17.0 1.3 %collective-permute-start.6 = (f32[2,256]{1,0:T(2,128)S(1)}, f32[2,256]{1,0:T(2,128)S(1)}, u32[]{:S(2)}, u32[]{:S(2)}) collective-permute-start(f32[2,256]{1,0:T(2,128)S(1)} %get-tuple-element.84.refs_4_), channel_id=1, source_target_pairs={{0,3},{1,2},{2,1},{3,0},{4,7},{5,6},{6,5},{7,4},{8,11},{9,10},{10,... | collective-permute-start | bytes 6152 | tf_op jit(solution)/shard_map/ppermute | solution.py:441
  18.3 1.8 %collective-permute-done.6.refs_5_ = f32[2,256]{1,0:T(2,128)S(1)} collective-permute-done((f32[2,256]{1,0:T(2,128)S(1)}, f32[2,256]{1,0:T(2,128)S(1)}, u32[]{:S(2)}, u32[]{:S(2)}) %collective-permute-start.6) | collective-permute-done | bytes 2080 | tf_op jit(solution)/shard_map/ppermute | solution.py:441
  21.0 3.4 %collective-permute-start.7 = (f32[2,16,16,256]{3,2,1,0:T(8,128)S(1)}, f32[2,16,16,256]{3,2,1,0:T(8,128)S(1)}, u32[]{:S(2)}, u32[]{:S(2)}) collective-permute-start(f32[2,16,16,256]{3,2,1,0:T(8,128)S(1)} %get-tuple-element.85), channel_id=1, source_target_pairs={{0,4},{4,8},{8,12},{12,16},{16,20},{20,24},{24,28},{1,5},{5,9},{9,... | collective-permute-start | bytes 1572872 | tf_op jit(solution)/shard_map/ppermute | solution.py:486
  24.4 1.0 collective-permute-start.10
  25.4 1.1 collective-permute-start.9
  27.5 1.6 %collective-permute-done.9 = f32[2,256]{1,0:T(2,128)S(1)} collective-permute-done((f32[2,256]{1,0:T(2,128)S(1)}, f32[2,256]{1,0:T(2,128)S(1)}, u32[]{:S(2)}, u32[]{:S(2)}) %collective-permute-start.9) | collective-permute-done | bytes 2080 | tf_op jit(solution)/shard_map/ppermute | solution.py:441
  29.0 1.9 %collective-permute-start.11 = (f32[2,256]{1,0:T(2,128)S(1)}, f32[2,256]{1,0:T(2,128)S(1)}, u32[]{:S(2)}, u32[]{:S(2)}) collective-permute-start(f32[2,256]{1,0:T(2,128)S(1)} %add_add_fusion), channel_id=1, source_target_pairs={{0,4},{4,8},{8,12},{12,16},{16,20},{20,24},{24,28},{1,5},{5,9},{9,... | collective-permute-start | bytes 6152 | tf_op jit(solution)/shard_map/ppermute | solution.py:487
  31.1 6.7 %collective-permute-done.11.refs_4_ = f32[2,256]{1,0:T(2,128)S(1)} collective-permute-done((f32[2,256]{1,0:T(2,128)S(1)}, f32[2,256]{1,0:T(2,128)S(1)}, u32[]{:S(2)}, u32[]{:S(2)}) %collective-permute-start.11) | collective-permute-done | bytes 2080 | tf_op jit(solution)/shard_map/ppermute | solution.py:487
  37.8 0.9 shard_map.53
  38.8 1.4 %collective-permute-start.22 = (f32[576,256]{1,0:T(8,128)S(1)}, f32[576,256]{1,0:T(8,128)S(1)}, u32[]{:S(2)}, u32[]{:S(2)}) collective-permute-start(f32[576,256]{1,0:T(8,128)S(1)} %shard_map.61), channel_id=1, source_target_pairs={{0,4},{4,0},{8,12},{12,8},{16,20},{20,16},{24,28},{28,24},{1,5},{5... | collective-permute-start | bytes 1769480 | tf_op jit(solution)/shard_map/ppermute | solution.py:494
  40.3 10.2 %collective-permute-done.21.near_upper = f32[576,256]{1,0:T(8,128)S(1)} collective-permute-done((f32[576,256]{1,0:T(8,128)S(1)}, f32[576,256]{1,0:T(8,128)S(1)}, u32[]{:S(2)}, u32[]{:S(2)}) %collective-permute-start.21) | collective-permute-done | bytes 589856 | tf_op jit(solution)/shard_map/ppermute | solution.py:482
  50.5 12.5 %collective-permute-done.22.near_lower = f32[576,256]{1,0:T(8,128)S(1)} collective-permute-done((f32[576,256]{1,0:T(8,128)S(1)}, f32[576,256]{1,0:T(8,128)S(1)}, u32[]{:S(2)}, u32[]{:S(2)}) %collective-permute-start.22) | collective-permute-done | bytes 589856 | tf_op jit(solution)/shard_map/ppermute | solution.py:494
  63.5 1.5 %collective-permute-start.14 = (f32[2,256]{1,0:T(2,128)S(1)}, f32[2,256]{1,0:T(2,128)S(1)}, u32[]{:S(2)}, u32[]{:S(2)}) collective-permute-start(f32[2,256]{1,0:T(2,128)S(1)} %get-tuple-element.88.refs_0_.after), channel_id=1, source_target_pairs={{0,2},{1,3},{2,0},{3,1},{4,6},{5,7},{6,4},{7,5},{8,10},{9,11},{10,... | collective-permute-start | bytes 6152 | tf_op jit(solution)/shard_map/ppermute | solution.py:441
  65.0 1.2 %collective-permute-start.15 = (f32[2,256]{1,0:T(2,128)S(1)}, f32[2,256]{1,0:T(2,128)S(1)}, u32[]{:S(2)}, u32[]{:S(2)}) collective-permute-start(f32[2,256]{1,0:T(2,128)S(1)} %get-tuple-element.88.refs_0_.after), channel_id=1, source_target_pairs={{0,3},{1,2},{2,1},{3,0},{4,7},{5,6},{6,5},{7,4},{8,11},{9,10},{10,... | collective-permute-start | bytes 6152 | tf_op jit(solution)/shard_map/ppermute | solution.py:441
  66.3 0.9 collective-permute-done.14.refs_7_
  67.1 0.9 collective-permute-done.15.refs_8_
  68.0 1.6 %shard_map.55 = (f32[2,16,16,256]{3,2,1,0:T(8,128)S(1)}, f32[2,16,16,256]{3,2,1,0:T(8,128)S(1)}, f32[2,256]{1,0:T(2,128)S(1)}) custom-call(f32[2,16,16,256]{3,2,1,0:T(8,128)S(1)} %get-tuple-element.87.refs_0_, f32[2,16,16,256]{3,2,1,0:T(8,128)S(1)} %collective-permute-done.12.refs_1_, bf16[4,3,768,256]{3,2,1,0:T(8,128)(2,1)S(1)} %shard_map.47.refs_2_.refs_1_.weights, ...), custom_call_target="tpu_custom_call" | custom-call | flops 1207959552 | bytes 1048576 | tf_op jit(solution)/shard_map/pallas_call | solution.py:24
  69.6 1.3 %collective-permute-start.16 = (f32[2,256]{1,0:T(2,128)S(1)}, f32[2,256]{1,0:T(2,128)S(1)}, u32[]{:S(2)}, u32[]{:S(2)}) collective-permute-start(f32[2,256]{1,0:T(2,128)S(1)} %get-tuple-element.91.refs_5_), channel_id=1, source_target_pairs={{0,3},{1,2},{2,1},{3,0},{4,7},{5,6},{6,5},{7,4},{8,11},{9,10},{10,... | collective-permute-start | bytes 6152 | tf_op jit(solution)/shard_map/ppermute | solution.py:441
  70.9 1.8 %collective-permute-done.16.refs_6_ = f32[2,256]{1,0:T(2,128)S(1)} collective-permute-done((f32[2,256]{1,0:T(2,128)S(1)}, f32[2,256]{1,0:T(2,128)S(1)}, u32[]{:S(2)}, u32[]{:S(2)}) %collective-permute-start.16) | collective-permute-done | bytes 2080 | tf_op jit(solution)/shard_map/ppermute | solution.py:441
  72.7 1.5 %shard_map.56 = (f32[2,16,16,256]{3,2,1,0:T(8,128)S(1)}, f32[2,256]{1,0:T(2,128)S(1)}) custom-call(f32[2,16,16,256]{3,2,1,0:T(8,128)S(1)} %get-tuple-element.89.refs_0_, f32[2,16,16,256]{3,2,1,0:T(8,128)S(1)} %get-tuple-element.90.refs_1_, bf16[4,3,768,256]{3,2,1,0:T(8,128)(2,1)S(1)} %shard_map.47.refs_2_.refs_1_.weights, f32[4,256]{1,0:T(4,128)S(1)} %copy-done.1, ...), custom_call_target="tpu_custom_call" | custom-call | flops 1207959552 | bytes 1048576 | tf_op jit(solution)/shard_map/pallas_call | solution.py:24
  74.2 1.3 %collective-permute-start.17 = (f32[2,256]{1,0:T(2,128)S(1)}, f32[2,256]{1,0:T(2,128)S(1)}, u32[]{:S(2)}, u32[]{:S(2)}) collective-permute-start(f32[2,256]{1,0:T(2,128)S(1)} %get-tuple-element.93.refs_0_), channel_id=1, source_target_pairs={{0,3},{1,2},{2,1},{3,0},{4,7},{5,6},{6,5},{7,4},{8,11},{9,10},{10,... | collective-permute-start | bytes 6152 | tf_op jit(solution)/shard_map/ppermute | solution.py:441
  75.5 1.8 %collective-permute-done.17.refs_5_ = f32[2,256]{1,0:T(2,128)S(1)} collective-permute-done((f32[2,256]{1,0:T(2,128)S(1)}, f32[2,256]{1,0:T(2,128)S(1)}, u32[]{:S(2)}, u32[]{:S(2)}) %collective-permute-start.17) | collective-permute-done | bytes 2080 | tf_op jit(solution)/shard_map/ppermute | solution.py:441
  77.3 1.0 shard_map.58
  79.1 1.2 collective-permute-start.26
  80.3 3.8 %collective-permute-done.18.received.refs_1_.refs_3_ = f32[136,256]{1,0:T(8,128)S(1)} collective-permute-done((f32[136,256]{1,0:T(8,128)S(1)}, f32[136,256]{1,0:T(8,128)S(1)}, u32[]{:S(2)}, u32[]{:S(2)}) %collective-permute-start.18) | collective-permute-done | bytes 139296 | tf_op jit(solution)/shard_map/ppermute | solution.py:518
  84.1 1.4 %collective-permute-start.19 = (f32[1,8,16,256]{3,2,1,0:T(8,128)S(1)}, f32[1,8,16,256]{3,2,1,0:T(8,128)S(1)}, u32[]{:S(2)}, u32[]{:S(2)}) collective-permute-start(f32[1,8,16,256]{3,2,1,0:T(8,128)S(1)} %shard_map.59), channel_id=1, source_target_pairs={{0,9},{1,8},{2,11},{3,10},{4,13},{5,12},{6,15},{7,14},{8,1},{9,0},... | collective-permute-start | bytes 393224 | tf_op jit(solution)/shard_map/ppermute | solution.py:542
  86.5 3.0 %collective-permute-done.28.received.refs_5_ = f32[32,256]{1,0:T(8,128)S(1)} collective-permute-done((f32[32,256]{1,0:T(8,128)S(1)}, f32[32,256]{1,0:T(8,128)S(1)}, u32[]{:S(2)}, u32[]{:S(2)}) %collective-permute-start.28) | collective-permute-done | bytes 32800 | tf_op jit(solution)/shard_map/ppermute | solution.py:518
  89.5 1.1 collective-permute-start.27
  91.8 2.9 %collective-permute-done.27.refs_1_.refs_0_ = f32[1,6,16,256]{3,2,1,0:T(8,128)S(1)} collective-permute-done((f32[1,6,16,256]{3,2,1,0:T(8,128)S(1)}, f32[1,6,16,256]{3,2,1,0:T(8,128)S(1)}, u32[]{:S(2)}, u32[]{:S(2)}) %collective-permute-start.27) | collective-permute-done | bytes 98336 | tf_op jit(solution)/shard_map/ppermute | solution.py:542
  95.3 0.9 collective-permute-start.29
  96.1 3.0 %collective-permute-done.29.refs_1_ = f32[1,2,16,256]{3,2,1,0:T(8,128)S(1)} collective-permute-done((f32[1,2,16,256]{3,2,1,0:T(8,128)S(1)}, f32[1,2,16,256]{3,2,1,0:T(8,128)S(1)}, u32[]{:S(2)}, u32[]{:S(2)}) %collective-permute-start.29) | collective-permute-done | bytes 32800 | tf_op jit(solution)/shard_map/ppermute | solution.py:542
  99.2 1.4 %collective-permute-start.32 = (f32[1,4,16,256]{3,2,1,0:T(8,128)S(1)}, f32[1,4,16,256]{3,2,1,0:T(8,128)S(1)}, u32[]{:S(2)}, u32[]{:S(2)}) collective-permute-start(f32[1,4,16,256]{3,2,1,0:T(8,128)S(1)} %get-tuple-element.118), channel_id=1, source_target_pairs={{0,4},{1,5},{2,6},{3,7},{4,0},{5,1},{6,2},{7,3},{8,17},{9,16},{10,... | collective-permute-start | bytes 196616 | tf_op jit(solution)/shard_map/ppermute | solution.py:542
  101.1 2.2 %collective-permute-start.34 = (f32[1,6,16,256]{3,2,1,0:T(8,128)S(1)}, f32[1,6,16,256]{3,2,1,0:T(8,128)S(1)}, u32[]{:S(2)}, u32[]{:S(2)}) collective-permute-start(f32[1,6,16,256]{3,2,1,0:T(8,128)S(1)} %get-tuple-element.133), channel_id=1, source_target_pairs={{0,8},{1,9},{2,10},{3,11},{4,12},{5,13},{6,14},{7,15},{8,0},{9,1},... | collective-permute-start | bytes 294920 | tf_op jit(solution)/shard_map/ppermute | solution.py:542
  105.7 0.9 collective-permute-done.34.refs_1_.refs_0_
  107.5 1.3 %collective-permute-done.36.refs_1_ = f32[1,6,16,256]{3,2,1,0:T(8,128)S(1)} collective-permute-done((f32[1,6,16,256]{3,2,1,0:T(8,128)S(1)}, f32[1,6,16,256]{3,2,1,0:T(8,128)S(1)}, u32[]{:S(2)}, u32[]{:S(2)}) %collective-permute-start.36) | collective-permute-done | bytes 98336 | tf_op jit(solution)/shard_map/ppermute | solution.py:542
  110.0 0.9 collective-permute-start.37
  111.7 0.9 collective-permute-start.33
  113.3 4.8 %collective-permute-done.33.refs_0_ = f32[1,2,16,256]{3,2,1,0:T(8,128)S(1)} collective-permute-done((f32[1,2,16,256]{3,2,1,0:T(8,128)S(1)}, f32[1,2,16,256]{3,2,1,0:T(8,128)S(1)}, u32[]{:S(2)}, u32[]{:S(2)}) %collective-permute-start.33) | collective-permute-done | bytes 32800 | tf_op jit(solution)/shard_map/ppermute | solution.py:570
  (71 shorter events, 14.7 us)
Async XLA Ops:
  0.0 1.0 copy-start
  1.2 5.1 %collective-permute-start = (f32[2,16,16,256]{3,2,1,0:T(8,128)S(1)}, f32[2,16,16,256]{3,2,1,0:T(8,128)S(1)}, u32[]{:S(2)}, u32[]{:S(2)}) collective-permute-start(f32[2,16,16,256]{3,2,1,0:T(8,128)S(1)} %get-tuple-element.75.refs_0_.refs_5_), channel_id=1, source_target_pairs={{0,1},{1,0},{2,3},{3,2},{4,5},{5,4},{6,7},{7,6},{8,9},{9,8},{10,11... | collective-permute-start | bytes 1572872 | tf_op jit(solution)/shard_map/ppermute | solution.py:466
  1.2 4.4 %collective-permute-start.1 = (f32[2,256]{1,0:T(2,128)S(1)}, f32[2,256]{1,0:T(2,128)S(1)}, u32[]{:S(2)}, u32[]{:S(2)}) collective-permute-start(f32[2,256]{1,0:T(2,128)S(1)} %get-tuple-element.76.refs_5_.refs_6_), channel_id=1, source_target_pairs={{0,1},{1,0},{2,3},{3,2},{4,5},{5,4},{6,7},{7,6},{8,9},{9,8},{10,11... | collective-permute-start | bytes 6152 | tf_op jit(solution)/shard_map/ppermute | solution.py:441
  1.7 3.9 %collective-permute-start.2 = (f32[2,256]{1,0:T(2,128)S(1)}, f32[2,256]{1,0:T(2,128)S(1)}, u32[]{:S(2)}, u32[]{:S(2)}) collective-permute-start(f32[2,256]{1,0:T(2,128)S(1)} %get-tuple-element.76.refs_5_.refs_6_), channel_id=1, source_target_pairs={{0,2},{1,3},{2,0},{3,1},{4,6},{5,7},{6,4},{7,5},{8,10},{9,11},{10,... | collective-permute-start | bytes 6152 | tf_op jit(solution)/shard_map/ppermute | solution.py:441
  3.2 3.0 %collective-permute-start.3 = (f32[2,256]{1,0:T(2,128)S(1)}, f32[2,256]{1,0:T(2,128)S(1)}, u32[]{:S(2)}, u32[]{:S(2)}) collective-permute-start(f32[2,256]{1,0:T(2,128)S(1)} %get-tuple-element.76.refs_5_.refs_6_), channel_id=1, source_target_pairs={{0,3},{1,2},{2,1},{3,0},{4,7},{5,6},{6,5},{7,4},{8,11},{9,10},{10,... | collective-permute-start | bytes 6152 | tf_op jit(solution)/shard_map/ppermute | solution.py:441
  3.2 3.0 %copy-start.1 = (f32[4,256]{1,0:T(4,128)S(1)}, f32[4,256]{1,0:T(4,128)}, u32[]{:S(2)}) copy-start(f32[4,256]{1,0:T(4,128)} %refs_2_.5) | copy-start | bytes 12292
  3.2 3.0 %copy-start.2 = (f32[4,256]{1,0:T(4,128)S(1)}, f32[4,256]{1,0:T(4,128)}, u32[]{:S(2)}) copy-start(f32[4,256]{1,0:T(4,128)} %refs_3_.15) | copy-start | bytes 12292
  7.8 3.1 %collective-permute-start.4 = (f32[2,256]{1,0:T(2,128)S(1)}, f32[2,256]{1,0:T(2,128)S(1)}, u32[]{:S(2)}, u32[]{:S(2)}) collective-permute-start(f32[2,256]{1,0:T(2,128)S(1)} %get-tuple-element.79.refs_0_.after), channel_id=1, source_target_pairs={{0,3},{1,2},{2,1},{3,0},{4,7},{5,6},{6,5},{7,4},{8,11},{9,10},{10,... | collective-permute-start | bytes 6152 | tf_op jit(solution)/shard_map/ppermute | solution.py:441
  12.4 3.1 %collective-permute-start.5 = (f32[2,256]{1,0:T(2,128)S(1)}, f32[2,256]{1,0:T(2,128)S(1)}, u32[]{:S(2)}, u32[]{:S(2)}) collective-permute-start(f32[2,256]{1,0:T(2,128)S(1)} %get-tuple-element.82.refs_5_), channel_id=1, source_target_pairs={{0,3},{1,2},{2,1},{3,0},{4,7},{5,6},{6,5},{7,4},{8,11},{9,10},{10,... | collective-permute-start | bytes 6152 | tf_op jit(solution)/shard_map/ppermute | solution.py:441
  17.0 3.1 %collective-permute-start.6 = (f32[2,256]{1,0:T(2,128)S(1)}, f32[2,256]{1,0:T(2,128)S(1)}, u32[]{:S(2)}, u32[]{:S(2)}) collective-permute-start(f32[2,256]{1,0:T(2,128)S(1)} %get-tuple-element.84.refs_4_), channel_id=1, source_target_pairs={{0,3},{1,2},{2,1},{3,0},{4,7},{5,6},{6,5},{7,4},{8,11},{9,10},{10,... | collective-permute-start | bytes 6152 | tf_op jit(solution)/shard_map/ppermute | solution.py:441
  21.0 16.9 %collective-permute-start.7 = (f32[2,16,16,256]{3,2,1,0:T(8,128)S(1)}, f32[2,16,16,256]{3,2,1,0:T(8,128)S(1)}, u32[]{:S(2)}, u32[]{:S(2)}) collective-permute-start(f32[2,16,16,256]{3,2,1,0:T(8,128)S(1)} %get-tuple-element.85), channel_id=1, source_target_pairs={{0,4},{4,8},{8,12},{12,16},{16,20},{20,24},{24,28},{1,5},{5,9},{9,... | collective-permute-start | bytes 1572872 | tf_op jit(solution)/shard_map/ppermute | solution.py:486
  24.4 3.1 %collective-permute-start.10 = (f32[2,256]{1,0:T(2,128)S(1)}, f32[2,256]{1,0:T(2,128)S(1)}, u32[]{:S(2)}, u32[]{:S(2)}) collective-permute-start(f32[2,256]{1,0:T(2,128)S(1)} %get-tuple-element.86), channel_id=1, source_target_pairs={{0,3},{1,2},{2,1},{3,0},{4,7},{5,6},{6,5},{7,4},{8,11},{9,10},{10,... | collective-permute-start | bytes 6152 | tf_op jit(solution)/shard_map/ppermute | solution.py:441
  25.4 2.1 %collective-permute-start.8 = (f32[2,256]{1,0:T(2,128)S(1)}, f32[2,256]{1,0:T(2,128)S(1)}, u32[]{:S(2)}, u32[]{:S(2)}) collective-permute-start(f32[2,256]{1,0:T(2,128)S(1)} %get-tuple-element.86), channel_id=1, source_target_pairs={{0,1},{1,0},{2,3},{3,2},{4,5},{5,4},{6,7},{7,6},{8,9},{9,8},{10,11... | collective-permute-start | bytes 6152 | tf_op jit(solution)/shard_map/ppermute | solution.py:441
  25.4 3.6 %collective-permute-start.9 = (f32[2,256]{1,0:T(2,128)S(1)}, f32[2,256]{1,0:T(2,128)S(1)}, u32[]{:S(2)}, u32[]{:S(2)}) collective-permute-start(f32[2,256]{1,0:T(2,128)S(1)} %get-tuple-element.86), channel_id=1, source_target_pairs={{0,2},{1,3},{2,0},{3,1},{4,6},{5,7},{6,4},{7,5},{8,10},{9,11},{10,... | collective-permute-start | bytes 6152 | tf_op jit(solution)/shard_map/ppermute | solution.py:441
  29.0 8.8 %collective-permute-start.11 = (f32[2,256]{1,0:T(2,128)S(1)}, f32[2,256]{1,0:T(2,128)S(1)}, u32[]{:S(2)}, u32[]{:S(2)}) collective-permute-start(f32[2,256]{1,0:T(2,128)S(1)} %add_add_fusion), channel_id=1, source_target_pairs={{0,4},{4,8},{8,12},{12,16},{16,20},{20,24},{24,28},{1,5},{5,9},{9,... | collective-permute-start | bytes 6152 | tf_op jit(solution)/shard_map/ppermute | solution.py:487
  31.0 19.5 %collective-permute-start.21 = (f32[576,256]{1,0:T(8,128)S(1)}, f32[576,256]{1,0:T(8,128)S(1)}, u32[]{:S(2)}, u32[]{:S(2)}) collective-permute-start(f32[576,256]{1,0:T(8,128)S(1)} %shard_map.60), channel_id=1, source_target_pairs={{0,4},{4,0},{8,12},{12,8},{16,20},{20,16},{24,28},{28,24},{1,5},{5... | collective-permute-start | bytes 1769480 | tf_op jit(solution)/shard_map/ppermute | solution.py:482
  38.8 24.2 %collective-permute-start.22 = (f32[576,256]{1,0:T(8,128)S(1)}, f32[576,256]{1,0:T(8,128)S(1)}, u32[]{:S(2)}, u32[]{:S(2)}) collective-permute-start(f32[576,256]{1,0:T(8,128)S(1)} %shard_map.61), channel_id=1, source_target_pairs={{0,4},{4,0},{8,12},{12,8},{16,20},{20,16},{24,28},{28,24},{1,5},{5... | collective-permute-start | bytes 1769480 | tf_op jit(solution)/shard_map/ppermute | solution.py:494
  40.3 27.8 %collective-permute-start.12 = (f32[2,16,16,256]{3,2,1,0:T(8,128)S(1)}, f32[2,16,16,256]{3,2,1,0:T(8,128)S(1)}, u32[]{:S(2)}, u32[]{:S(2)}) collective-permute-start(f32[2,16,16,256]{3,2,1,0:T(8,128)S(1)} %get-tuple-element.87.refs_0_), channel_id=1, source_target_pairs={{0,1},{1,0},{2,3},{3,2},{4,5},{5,4},{6,7},{7,6},{8,9},{9,8},{10,11... | collective-permute-start | bytes 1572872 | tf_op jit(solution)/shard_map/ppermute | solution.py:493
  50.5 40.1 %collective-permute-start.23 = (f32[576,256]{1,0:T(8,128)S(1)}, f32[576,256]{1,0:T(8,128)S(1)}, u32[]{:S(2)}, u32[]{:S(2)}) collective-permute-start(f32[576,256]{1,0:T(8,128)S(1)} %collective-permute-done.21.near_upper), channel_id=1, source_target_pairs={{0,1},{1,0},{2,3},{3,2},{4,5},{5,4},{6,7},{7,6},{8,9},{9,8},{10,11... | collective-permute-start | bytes 1769480 | tf_op jit(solution)/shard_map/ppermute | solution.py:495
  63.0 27.5 %collective-permute-start.24 = (f32[576,256]{1,0:T(8,128)S(1)}, f32[576,256]{1,0:T(8,128)S(1)}, u32[]{:S(2)}, u32[]{:S(2)}) collective-permute-start(f32[576,256]{1,0:T(8,128)S(1)} %collective-permute-done.22.near_lower), channel_id=1, source_target_pairs={{0,1},{1,0},{2,3},{3,2},{4,5},{5,4},{6,7},{7,6},{8,9},{9,8},{10,11... | collective-permute-start | bytes 1769480 | tf_op jit(solution)/shard_map/ppermute | solution.py:501
  63.0 2.0 %collective-permute-start.13 = (f32[2,256]{1,0:T(2,128)S(1)}, f32[2,256]{1,0:T(2,128)S(1)}, u32[]{:S(2)}, u32[]{:S(2)}) collective-permute-start(f32[2,256]{1,0:T(2,128)S(1)} %get-tuple-element.88.refs_0_.after), channel_id=1, source_target_pairs={{0,1},{1,0},{2,3},{3,2},{4,5},{5,4},{6,7},{7,6},{8,9},{9,8},{10,11... | collective-permute-start | bytes 6152 | tf_op jit(solution)/shard_map/ppermute | solution.py:441
  63.5 3.6 %collective-permute-start.14 = (f32[2,256]{1,0:T(2,128)S(1)}, f32[2,256]{1,0:T(2,128)S(1)}, u32[]{:S(2)}, u32[]{:S(2)}) collective-permute-start(f32[2,256]{1,0:T(2,128)S(1)} %get-tuple-element.88.refs_0_.after), channel_id=1, source_target_pairs={{0,2},{1,3},{2,0},{3,1},{4,6},{5,7},{6,4},{7,5},{8,10},{9,11},{10,... | collective-permute-start | bytes 6152 | tf_op jit(solution)/shard_map/ppermute | solution.py:441
  65.0 3.0 %collective-permute-start.15 = (f32[2,256]{1,0:T(2,128)S(1)}, f32[2,256]{1,0:T(2,128)S(1)}, u32[]{:S(2)}, u32[]{:S(2)}) collective-permute-start(f32[2,256]{1,0:T(2,128)S(1)} %get-tuple-element.88.refs_0_.after), channel_id=1, source_target_pairs={{0,3},{1,2},{2,1},{3,0},{4,7},{5,6},{6,5},{7,4},{8,11},{9,10},{10,... | collective-permute-start | bytes 6152 | tf_op jit(solution)/shard_map/ppermute | solution.py:441
  69.6 3.1 %collective-permute-start.16 = (f32[2,256]{1,0:T(2,128)S(1)}, f32[2,256]{1,0:T(2,128)S(1)}, u32[]{:S(2)}, u32[]{:S(2)}) collective-permute-start(f32[2,256]{1,0:T(2,128)S(1)} %get-tuple-element.91.refs_5_), channel_id=1, source_target_pairs={{0,3},{1,2},{2,1},{3,0},{4,7},{5,6},{6,5},{7,4},{8,11},{9,10},{10,... | collective-permute-start | bytes 6152 | tf_op jit(solution)/shard_map/ppermute | solution.py:441
  74.2 3.1 %collective-permute-start.17 = (f32[2,256]{1,0:T(2,128)S(1)}, f32[2,256]{1,0:T(2,128)S(1)}, u32[]{:S(2)}, u32[]{:S(2)}) collective-permute-start(f32[2,256]{1,0:T(2,128)S(1)} %get-tuple-element.93.refs_0_), channel_id=1, source_target_pairs={{0,3},{1,2},{2,1},{3,0},{4,7},{5,6},{6,5},{7,4},{8,11},{9,10},{10,... | collective-permute-start | bytes 6152 | tf_op jit(solution)/shard_map/ppermute | solution.py:441
  78.3 5.7 %collective-permute-start.18 = (f32[136,256]{1,0:T(8,128)S(1)}, f32[136,256]{1,0:T(8,128)S(1)}, u32[]{:S(2)}, u32[]{:S(2)}) collective-permute-start(f32[136,256]{1,0:T(8,128)S(1)} %get-tuple-element.96), channel_id=1, source_target_pairs={{0,4},{1,5},{2,6},{3,7},{4,0},{5,1},{6,2},{7,3},{8,13},{9,12},{10,... | collective-permute-start | bytes 417800 | tf_op jit(solution)/shard_map/ppermute | solution.py:518
  78.7 12.1 %collective-permute-start.20 = (f32[1,256,256]{2,1,0:T(8,128)S(1)}, f32[1,256,256]{2,1,0:T(8,128)S(1)}, u32[]{:S(2)}, u32[]{:S(2)}) collective-permute-start(f32[1,256,256]{2,1,0:T(8,128)S(1)} %get-tuple-element.98.refs_2_.refs_5_.refs_6_), channel_id=1, source_target_pairs={{0,1},{1,0},{2,3},{3,2},{4,5},{5,4},{6,7},{7,6},{8,9},{9,8},{10,11... | collective-permute-start | bytes 786440 | tf_op jit(solution)/shard_map/ppermute | solution.py:519
  79.1 7.0 %collective-permute-start.26 = (f32[96,256]{1,0:T(8,128)S(1)}, f32[96,256]{1,0:T(8,128)S(1)}, u32[]{:S(2)}, u32[]{:S(2)}) collective-permute-start(f32[96,256]{1,0:T(8,128)S(1)} %get-tuple-element.100), channel_id=1, source_target_pairs={{0,4},{1,5},{2,6},{3,7},{4,0},{5,1},{6,2},{7,3},{8,13},{9,12},{10,... | collective-permute-start | bytes 294920 | tf_op jit(solution)/shard_map/ppermute | solution.py:518
  84.1 6.7 %collective-permute-start.19 = (f32[1,8,16,256]{3,2,1,0:T(8,128)S(1)}, f32[1,8,16,256]{3,2,1,0:T(8,128)S(1)}, u32[]{:S(2)}, u32[]{:S(2)}) collective-permute-start(f32[1,8,16,256]{3,2,1,0:T(8,128)S(1)} %shard_map.59), channel_id=1, source_target_pairs={{0,9},{1,8},{2,11},{3,10},{4,13},{5,12},{6,15},{7,14},{8,1},{9,0},... | collective-permute-start | bytes 393224 | tf_op jit(solution)/shard_map/ppermute | solution.py:542
  86.1 3.4 %collective-permute-start.28 = (f32[32,256]{1,0:T(8,128)S(1)}, f32[32,256]{1,0:T(8,128)S(1)}, u32[]{:S(2)}, u32[]{:S(2)}) collective-permute-start(f32[32,256]{1,0:T(8,128)S(1)} %get-tuple-element.101), channel_id=1, source_target_pairs={{0,4},{1,5},{2,6},{3,7},{4,0},{5,1},{6,2},{7,3},{8,13},{9,12},{10,... | collective-permute-start | bytes 98312 | tf_op jit(solution)/shard_map/ppermute | solution.py:518
  89.5 5.1 %collective-permute-start.27 = (f32[1,6,16,256]{3,2,1,0:T(8,128)S(1)}, f32[1,6,16,256]{3,2,1,0:T(8,128)S(1)}, u32[]{:S(2)}, u32[]{:S(2)}) collective-permute-start(f32[1,6,16,256]{3,2,1,0:T(8,128)S(1)} %shard_map.64), channel_id=1, source_target_pairs={{0,9},{1,8},{2,11},{3,10},{4,13},{5,12},{6,15},{7,14},{8,1},{9,0},... | collective-permute-start | bytes 294920 | tf_op jit(solution)/shard_map/ppermute | solution.py:542
  91.1 9.5 %collective-permute-start.25 = (f32[1,6,16,256]{3,2,1,0:T(8,128)S(1)}, f32[1,6,16,256]{3,2,1,0:T(8,128)S(1)}, u32[]{:S(2)}, u32[]{:S(2)}) collective-permute-start(f32[1,6,16,256]{3,2,1,0:T(8,128)S(1)} %get-tuple-element.99), channel_id=1, source_target_pairs={{0,4},{1,5},{2,6},{3,7},{4,0},{5,1},{6,2},{7,3},{8,17},{9,16},{10,... | collective-permute-start | bytes 294920 | tf_op jit(solution)/shard_map/ppermute | solution.py:542
  94.6 6.5 %collective-permute-start.31 = (f32[1,6,16,256]{3,2,1,0:T(8,128)S(1)}, f32[1,6,16,256]{3,2,1,0:T(8,128)S(1)}, u32[]{:S(2)}, u32[]{:S(2)}) collective-permute-start(f32[1,6,16,256]{3,2,1,0:T(8,128)S(1)} %get-tuple-element.117), channel_id=1, source_target_pairs={{0,4},{1,5},{2,6},{3,7},{4,0},{5,1},{6,2},{7,3},{8,17},{9,16},{10,... | collective-permute-start | bytes 294920 | tf_op jit(solution)/shard_map/ppermute | solution.py:542
  95.3 3.9 %collective-permute-start.29 = (f32[1,2,16,256]{3,2,1,0:T(8,128)S(1)}, f32[1,2,16,256]{3,2,1,0:T(8,128)S(1)}, u32[]{:S(2)}, u32[]{:S(2)}) collective-permute-start(f32[1,2,16,256]{3,2,1,0:T(8,128)S(1)} %shard_map.65), channel_id=1, source_target_pairs={{0,9},{1,8},{2,11},{3,10},{4,13},{5,12},{6,15},{7,14},{8,1},{9,0},... | collective-permute-start | bytes 98312 | tf_op jit(solution)/shard_map/ppermute | solution.py:542
  99.2 4.3 %collective-permute-start.32 = (f32[1,4,16,256]{3,2,1,0:T(8,128)S(1)}, f32[1,4,16,256]{3,2,1,0:T(8,128)S(1)}, u32[]{:S(2)}, u32[]{:S(2)}) collective-permute-start(f32[1,4,16,256]{3,2,1,0:T(8,128)S(1)} %get-tuple-element.118), channel_id=1, source_target_pairs={{0,4},{1,5},{2,6},{3,7},{4,0},{5,1},{6,2},{7,3},{8,17},{9,16},{10,... | collective-permute-start | bytes 196616 | tf_op jit(solution)/shard_map/ppermute | solution.py:542
  100.6 4.3 %collective-permute-start.30 = (f32[1,4,16,256]{3,2,1,0:T(8,128)S(1)}, f32[1,4,16,256]{3,2,1,0:T(8,128)S(1)}, u32[]{:S(2)}, u32[]{:S(2)}) collective-permute-start(f32[1,4,16,256]{3,2,1,0:T(8,128)S(1)} %get-tuple-element.116), channel_id=1, source_target_pairs={{0,8},{1,9},{2,10},{3,11},{4,12},{5,13},{6,14},{7,15},{8,0},{9,1},... | collective-permute-start | bytes 196616 | tf_op jit(solution)/shard_map/ppermute | solution.py:542
  101.1 5.5 %collective-permute-start.34 = (f32[1,6,16,256]{3,2,1,0:T(8,128)S(1)}, f32[1,6,16,256]{3,2,1,0:T(8,128)S(1)}, u32[]{:S(2)}, u32[]{:S(2)}) collective-permute-start(f32[1,6,16,256]{3,2,1,0:T(8,128)S(1)} %get-tuple-element.133), channel_id=1, source_target_pairs={{0,8},{1,9},{2,10},{3,11},{4,12},{5,13},{6,14},{7,15},{8,0},{9,1},... | collective-permute-start | bytes 294920 | tf_op jit(solution)/shard_map/ppermute | solution.py:542
  103.4 5.3 %collective-permute-start.36 = (f32[1,6,16,256]{3,2,1,0:T(8,128)S(1)}, f32[1,6,16,256]{3,2,1,0:T(8,128)S(1)}, u32[]{:S(2)}, u32[]{:S(2)}) collective-permute-start(f32[1,6,16,256]{3,2,1,0:T(8,128)S(1)} %get-tuple-element.139), channel_id=1, source_target_pairs={{0,8},{1,9},{2,10},{3,11},{4,12},{5,13},{6,14},{7,15},{8,0},{9,1},... | collective-permute-start | bytes 294920 | tf_op jit(solution)/shard_map/ppermute | solution.py:542
  109.6 3.0 %collective-permute-start.38 = (f32[1,16,16,256]{3,2,1,0:T(8,128)S(1)}, f32[1,16,16,256]{3,2,1,0:T(8,128)S(1)}, u32[]{:S(2)}, u32[]{:S(2)}) collective-permute-start(f32[1,16,16,256]{3,2,1,0:T(8,128)S(1)} %get-tuple-element.144.own), channel_id=1, source_target_pairs={{0,1},{1,0},{2,3},{3,2},{4,5},{5,4},{6,7},{7,6},{8,9},{9,8},{10,11... | collective-permute-start | bytes 786440 | tf_op jit(solution)/shard_map/ppermute | solution.py:577
  110.0 8.2 %collective-permute-start.37 = (f32[1,8,16,256]{3,2,1,0:T(8,128)S(1)}, f32[1,8,16,256]{3,2,1,0:T(8,128)S(1)}, u32[]{:S(2)}, u32[]{:S(2)}) collective-permute-start(f32[1,8,16,256]{3,2,1,0:T(8,128)S(1)} %get-tuple-element.143), channel_id=1, source_target_pairs={{0,4},{1,5},{2,6},{3,7},{4,0},{5,1},{6,2},{7,3},{8,13},{9,12},{10,... | collective-permute-start | bytes 393224 | tf_op jit(solution)/shard_map/ppermute | solution.py:570
  110.9 7.3 %collective-permute-start.35 = (f32[1,6,16,256]{3,2,1,0:T(8,128)S(1)}, f32[1,6,16,256]{3,2,1,0:T(8,128)S(1)}, u32[]{:S(2)}, u32[]{:S(2)}) collective-permute-start(f32[1,6,16,256]{3,2,1,0:T(8,128)S(1)} %get-tuple-element.138), channel_id=1, source_target_pairs={{0,4},{1,5},{2,6},{3,7},{4,0},{5,1},{6,2},{7,3},{8,13},{9,12},{10,... | collective-permute-start | bytes 294920 | tf_op jit(solution)/shard_map/ppermute | solution.py:570
  111.7 6.4 %collective-permute-start.33 = (f32[1,2,16,256]{3,2,1,0:T(8,128)S(1)}, f32[1,2,16,256]{3,2,1,0:T(8,128)S(1)}, u32[]{:S(2)}, u32[]{:S(2)}) collective-permute-start(f32[1,2,16,256]{3,2,1,0:T(8,128)S(1)} %get-tuple-element.132), channel_id=1, source_target_pairs={{0,4},{1,5},{2,6},{3,7},{4,0},{5,1},{6,2},{7,3},{8,13},{9,12},{10,... | collective-permute-start | bytes 98312 | tf_op jit(solution)/shard_map/ppermute | solution.py:570

commit v4 on v3

--- a/solution.py
+++ b/solution.py
@@ -455,6 +455,7 @@
         ]
 
     swaps = routes(lambda i: (i ^ 1, i // 2 % 2 == 1))
+    backs = routes(lambda i: (i ^ 1, i // 2 % 2 == 1) if i > 1 else (i, True))
     partners = [(i, i ^ 1) for i in range(devices)]
     cores = [(i, i ^ 1) for i in range(group)]
     onward = [(i, i + 1) for i in range(devices - 1)]
@@ -535,10 +536,9 @@
     back = []
     for turn, (cuts, split, out_cuts) in enumerate(plan, 1):
         across = {}
-        for first in (turn - 1, *range(0, turn - 2, 2), *range(turn + 1, devices // 2 - 1, 2)):
-            for i in (2 * first, 2 * first + 1):
-                across[i], across[i + 2] = (i + 2, first == turn - 1), (i, first == turn - 1)
-        route = routes(lambda i: across.get(i, (i ^ 1, False)))
+        for i in (2 * turn - 2, 2 * turn - 1):
+            across[i], across[i + 2] = i + 2, i
+        route = routes(lambda i: (across.get(i, i), True))
         arriving = [lax.ppermute(part, both, route) for part in passed]
         shared = (mine_other if turn % 2 else mine, terms, kernels)
         last = turn == len(plan)
@@ -567,11 +567,11 @@
             gives = {**gives, **now}
             halo = tuple(made[:1]) if n < len(cuts) else ()
             if last:
-                back.append(lax.ppermute(gives[back_spans[n]], both, swaps))
+                back.append(lax.ppermute(gives[back_spans[n]], both, backs))
             else:
                 passed.append(made[-1])
     if not back:
-        back = [lax.ppermute(part, both, swaps) for part in gives.values()]
+        back = [lax.ppermute(part, both, backs) for part in gives.values()]
     out = call(
         finish_own_kernel,
         (early, own, lax.ppermute(own, "batch", cores)),

time: 120 us -> 120 us (level)
  waiting for transfers between devices: 64.5 us -> 60 us
  starting transfers between devices: 35.5 us -> 39.2 us
    ppermute x9, waiting for transfers between devices: 8.88 us -> 3.16 us  [steps(): arriving = [lax.ppermute(part, both, route) for part in passed]]
    ppermute x9, starting transfers between devices: 9.51 us -> 13.7 us  [steps(): arriving = [lax.ppermute(part, both, route) for part in passed]]
  transfers between devices with their start and end apart: 39 -> 39, of which waited for: 23 -> 21; matrix products, arithmetic and copies ran while one was open for 0% -> 0% of each run, Pallas kernels for 9% -> 9%
where the time goes in v4:
time: 120 us; the launch traced here: 118 us
  waiting for transfers between devices  60 us (50%)
  starting transfers between devices  39.2 us (33%)
  Pallas kernels  17.5 us (15%)
    pallas_call x30, Pallas kernels, call(): pl.pallas_call(body, out_shape=outs, in_specs=[whole] * len(operands) if...  17.5 us
    ppermute x14, waiting for transfers between devices, gathered(): lax.ppermute(sums, 'batch', [(i, i ^ m) for i in range(group)])  13.8 us
    ppermute x14, starting transfers between devices, gathered(): lax.ppermute(sums, 'batch', [(i, i ^ m) for i in range(group)])  13.7 us
    ppermute x9, starting transfers between devices, steps(): arriving = [lax.ppermute(part, both, route) for part in passed]  13.7 us
    ppermute x1, waiting for transfers between devices, steps(): near_lower = lax.ppermute(widen(1, weights, sums), 'depth', partners)  12.5 us
    ppermute x1, waiting for transfers between devices, steps(): near_upper = lax.ppermute(widen(0, weights, sums), 'depth', partners)  10.2 us
    ppermute x3, waiting for transfers between devices, steps(): exchange = [lax.ppermute(part, both, swaps) for part in sent]  8 us
    ppermute x1, waiting for transfers between devices, steps(): arrived_totals = lax.ppermute(sum(totals[1:], totals[0]), 'depth', onward)  6.75 us
  transfers between devices with their start and end apart: 39, of which 21 were waited for; matrix products, arithmetic and copies ran while one was open for 0% of the time, Pallas kernels for 9%

profile of v4, /device:TPU:24, one launch (start us, length us, event | category | flops | bytes accessed | tf_op | source)
XLA Modules:
  0.0 118.3 jit_solution(7560264354977019651)
XLA Ops:
  0.0 1.0 copy-done
  1.7 1.5 %collective-permute-start.2 = (f32[2,256]{1,0:T(2,128)S(1)}, f32[2,256]{1,0:T(2,128)S(1)}, u32[]{:S(2)}, u32[]{:S(2)}) collective-permute-start(f32[2,256]{1,0:T(2,128)S(1)} %get-tuple-element.76.refs_5_.refs_6_), channel_id=1, source_target_pairs={{0,2},{1,3},{2,0},{3,1},{4,6},{5,7},{6,4},{7,5},{8,10},{9,11},{10,... | collective-permute-start | bytes 6152 | tf_op jit(solution)/shard_map/ppermute | solution.py:441
  3.2 2.4 %shard_map.47.refs_2_.refs_1_.weights = bf16[4,3,768,256]{3,2,1,0:T(8,128)(2,1)S(1)} custom-call(bf16[4,3,768,256]{3,2,1,0:T(8,128)(2,1)} %bitcast.4), custom_call_target="tpu_custom_call" | custom-call | bytes 9437184 | tf_op jit(solution)/shard_map/pallas_call | solution.py:24
  6.2 1.5 %shard_map.48 = (f32[2,16,16,256]{3,2,1,0:T(8,128)S(1)}, f32[2,16,16,256]{3,2,1,0:T(8,128)S(1)}, f32[2,256]{1,0:T(2,128)S(1)}) custom-call(f32[2,16,16,256]{3,2,1,0:T(8,128)S(1)} %get-tuple-element.75.refs_0_.refs_5_, f32[2,16,16,256]{3,2,1,0:T(8,128)S(1)} %collective-permute-done.refs_1_, bf16[4,3,768,256]{3,2,1,0:T(8,128)(2,1)S(1)} %shard_map.47.refs_2_.refs_1_.weights, ...), custom_call_target="tpu_custom_call" | custom-call | flops 1207959552 | bytes 1048576 | tf_op jit(solution)/shard_map/pallas_call | solution.py:24
  7.8 1.3 %collective-permute-start.4 = (f32[2,256]{1,0:T(2,128)S(1)}, f32[2,256]{1,0:T(2,128)S(1)}, u32[]{:S(2)}, u32[]{:S(2)}) collective-permute-start(f32[2,256]{1,0:T(2,128)S(1)} %get-tuple-element.79.refs_0_.after), channel_id=1, source_target_pairs={{0,3},{1,2},{2,1},{3,0},{4,7},{5,6},{6,5},{7,4},{8,11},{9,10},{10,... | collective-permute-start | bytes 6152 | tf_op jit(solution)/shard_map/ppermute | solution.py:441
  9.1 1.8 %collective-permute-done.4.refs_6_ = f32[2,256]{1,0:T(2,128)S(1)} collective-permute-done((f32[2,256]{1,0:T(2,128)S(1)}, f32[2,256]{1,0:T(2,128)S(1)}, u32[]{:S(2)}, u32[]{:S(2)}) %collective-permute-start.4) | collective-permute-done | bytes 2080 | tf_op jit(solution)/shard_map/ppermute | solution.py:441
  10.9 1.5 %shard_map.50 = (f32[2,16,16,256]{3,2,1,0:T(8,128)S(1)}, f32[2,16,16,256]{3,2,1,0:T(8,128)S(1)}, f32[2,256]{1,0:T(2,128)S(1)}) custom-call(f32[2,16,16,256]{3,2,1,0:T(8,128)S(1)} %get-tuple-element.77.refs_0_, f32[2,16,16,256]{3,2,1,0:T(8,128)S(1)} %get-tuple-element.78.refs_1_, bf16[4,3,768,256]{3,2,1,0:T(8,128)(2,1)S(1)} %shard_map.47.refs_2_.refs_1_.weights, ...), custom_call_target="tpu_custom_call" | custom-call | flops 1207959552 | bytes 1048576 | tf_op jit(solution)/shard_map/pallas_call | solution.py:24
  12.4 1.3 %collective-permute-start.5 = (f32[2,256]{1,0:T(2,128)S(1)}, f32[2,256]{1,0:T(2,128)S(1)}, u32[]{:S(2)}, u32[]{:S(2)}) collective-permute-start(f32[2,256]{1,0:T(2,128)S(1)} %get-tuple-element.82.refs_5_), channel_id=1, source_target_pairs={{0,3},{1,2},{2,1},{3,0},{4,7},{5,6},{6,5},{7,4},{8,11},{9,10},{10,... | collective-permute-start | bytes 6152 | tf_op jit(solution)/shard_map/ppermute | solution.py:441
  13.7 1.8 %collective-permute-done.5.refs_6_ = f32[2,256]{1,0:T(2,128)S(1)} collective-permute-done((f32[2,256]{1,0:T(2,128)S(1)}, f32[2,256]{1,0:T(2,128)S(1)}, u32[]{:S(2)}, u32[]{:S(2)}) %collective-permute-start.5) | collective-permute-done | bytes 2080 | tf_op jit(solution)/shard_map/ppermute | solution.py:441
  15.5 1.5 %shard_map.51 = (f32[2,16,16,256]{3,2,1,0:T(8,128)S(1)}, f32[2,256]{1,0:T(2,128)S(1)}) custom-call(f32[2,16,16,256]{3,2,1,0:T(8,128)S(1)} %get-tuple-element.80.refs_0_, f32[2,16,16,256]{3,2,1,0:T(8,128)S(1)} %get-tuple-element.81.refs_1_, bf16[4,3,768,256]{3,2,1,0:T(8,128)(2,1)S(1)} %shard_map.47.refs_2_.refs_1_.weights, f32[4,256]{1,0:T(4,128)S(1)} %copy-done.1, ...), custom_call_target="tpu_custom_call" | custom-call | flops 1207959552 | bytes 1048576 | tf_op jit(solution)/shard_map/pallas_call | solution.py:24
  17.0 1.3 %collective-permute-start.6 = (f32[2,256]{1,0:T(2,128)S(1)}, f32[2,256]{1,0:T(2,128)S(1)}, u32[]{:S(2)}, u32[]{:S(2)}) collective-permute-start(f32[2,256]{1,0:T(2,128)S(1)} %get-tuple-element.84.refs_4_), channel_id=1, source_target_pairs={{0,3},{1,2},{2,1},{3,0},{4,7},{5,6},{6,5},{7,4},{8,11},{9,10},{10,... | collective-permute-start | bytes 6152 | tf_op jit(solution)/shard_map/ppermute | solution.py:441
  18.3 1.8 %collective-permute-done.6.refs_5_ = f32[2,256]{1,0:T(2,128)S(1)} collective-permute-done((f32[2,256]{1,0:T(2,128)S(1)}, f32[2,256]{1,0:T(2,128)S(1)}, u32[]{:S(2)}, u32[]{:S(2)}) %collective-permute-start.6) | collective-permute-done | bytes 2080 | tf_op jit(solution)/shard_map/ppermute | solution.py:441
  20.1 0.8 shard_map.52
  21.0 3.4 %collective-permute-start.7 = (f32[2,16,16,256]{3,2,1,0:T(8,128)S(1)}, f32[2,16,16,256]{3,2,1,0:T(8,128)S(1)}, u32[]{:S(2)}, u32[]{:S(2)}) collective-permute-start(f32[2,16,16,256]{3,2,1,0:T(8,128)S(1)} %get-tuple-element.85), channel_id=1, source_target_pairs={{0,4},{4,8},{8,12},{12,16},{16,20},{20,24},{24,28},{1,5},{5,9},{9,... | collective-permute-start | bytes 1572872 | tf_op jit(solution)/shard_map/ppermute | solution.py:487
  24.4 1.0 collective-permute-start.10
  25.4 1.1 collective-permute-start.9
  26.6 0.9 collective-permute-done.10
  27.5 1.6 %collective-permute-done.9 = f32[2,256]{1,0:T(2,128)S(1)} collective-permute-done((f32[2,256]{1,0:T(2,128)S(1)}, f32[2,256]{1,0:T(2,128)S(1)}, u32[]{:S(2)}, u32[]{:S(2)}) %collective-permute-start.9) | collective-permute-done | bytes 2080 | tf_op jit(solution)/shard_map/ppermute | solution.py:441
  29.0 1.9 %collective-permute-start.11 = (f32[2,256]{1,0:T(2,128)S(1)}, f32[2,256]{1,0:T(2,128)S(1)}, u32[]{:S(2)}, u32[]{:S(2)}) collective-permute-start(f32[2,256]{1,0:T(2,128)S(1)} %add_add_fusion), channel_id=1, source_target_pairs={{0,4},{4,8},{8,12},{12,16},{16,20},{20,24},{24,28},{1,5},{5,9},{9,... | collective-permute-start | bytes 6152 | tf_op jit(solution)/shard_map/ppermute | solution.py:488
  31.1 6.7 %collective-permute-done.11.refs_4_ = f32[2,256]{1,0:T(2,128)S(1)} collective-permute-done((f32[2,256]{1,0:T(2,128)S(1)}, f32[2,256]{1,0:T(2,128)S(1)}, u32[]{:S(2)}, u32[]{:S(2)}) %collective-permute-start.11) | collective-permute-done | bytes 2080 | tf_op jit(solution)/shard_map/ppermute | solution.py:488
  37.8 0.9 shard_map.53
  38.8 1.4 %collective-permute-start.22 = (f32[576,256]{1,0:T(8,128)S(1)}, f32[576,256]{1,0:T(8,128)S(1)}, u32[]{:S(2)}, u32[]{:S(2)}) collective-permute-start(f32[576,256]{1,0:T(8,128)S(1)} %shard_map.61), channel_id=1, source_target_pairs={{0,4},{4,0},{8,12},{12,8},{16,20},{20,16},{24,28},{28,24},{1,5},{5... | collective-permute-start | bytes 1769480 | tf_op jit(solution)/shard_map/ppermute | solution.py:495
  40.3 10.2 %collective-permute-done.21.near_upper = f32[576,256]{1,0:T(8,128)S(1)} collective-permute-done((f32[576,256]{1,0:T(8,128)S(1)}, f32[576,256]{1,0:T(8,128)S(1)}, u32[]{:S(2)}, u32[]{:S(2)}) %collective-permute-start.21) | collective-permute-done | bytes 589856 | tf_op jit(solution)/shard_map/ppermute | solution.py:483
  50.5 12.5 %collective-permute-done.22.near_lower = f32[576,256]{1,0:T(8,128)S(1)} collective-permute-done((f32[576,256]{1,0:T(8,128)S(1)}, f32[576,256]{1,0:T(8,128)S(1)}, u32[]{:S(2)}, u32[]{:S(2)}) %collective-permute-start.22) | collective-permute-done | bytes 589856 | tf_op jit(solution)/shard_map/ppermute | solution.py:495
  63.5 1.5 %collective-permute-start.14 = (f32[2,256]{1,0:T(2,128)S(1)}, f32[2,256]{1,0:T(2,128)S(1)}, u32[]{:S(2)}, u32[]{:S(2)}) collective-permute-start(f32[2,256]{1,0:T(2,128)S(1)} %get-tuple-element.88.refs_0_.after), channel_id=1, source_target_pairs={{0,2},{1,3},{2,0},{3,1},{4,6},{5,7},{6,4},{7,5},{8,10},{9,11},{10,... | collective-permute-start | bytes 6152 | tf_op jit(solution)/shard_map/ppermute | solution.py:441
  65.0 1.2 %collective-permute-start.15 = (f32[2,256]{1,0:T(2,128)S(1)}, f32[2,256]{1,0:T(2,128)S(1)}, u32[]{:S(2)}, u32[]{:S(2)}) collective-permute-start(f32[2,256]{1,0:T(2,128)S(1)} %get-tuple-element.88.refs_0_.after), channel_id=1, source_target_pairs={{0,3},{1,2},{2,1},{3,0},{4,7},{5,6},{6,5},{7,4},{8,11},{9,10},{10,... | collective-permute-start | bytes 6152 | tf_op jit(solution)/shard_map/ppermute | solution.py:441
  66.3 0.9 collective-permute-done.14.refs_7_
  67.1 0.9 collective-permute-done.15.refs_8_
  68.0 1.6 %shard_map.55 = (f32[2,16,16,256]{3,2,1,0:T(8,128)S(1)}, f32[2,16,16,256]{3,2,1,0:T(8,128)S(1)}, f32[2,256]{1,0:T(2,128)S(1)}) custom-call(f32[2,16,16,256]{3,2,1,0:T(8,128)S(1)} %get-tuple-element.87.refs_0_, f32[2,16,16,256]{3,2,1,0:T(8,128)S(1)} %collective-permute-done.12.refs_1_, bf16[4,3,768,256]{3,2,1,0:T(8,128)(2,1)S(1)} %shard_map.47.refs_2_.refs_1_.weights, ...), custom_call_target="tpu_custom_call" | custom-call | flops 1207959552 | bytes 1048576 | tf_op jit(solution)/shard_map/pallas_call | solution.py:24
  69.6 1.3 %collective-permute-start.16 = (f32[2,256]{1,0:T(2,128)S(1)}, f32[2,256]{1,0:T(2,128)S(1)}, u32[]{:S(2)}, u32[]{:S(2)}) collective-permute-start(f32[2,256]{1,0:T(2,128)S(1)} %get-tuple-element.91.refs_5_), channel_id=1, source_target_pairs={{0,3},{1,2},{2,1},{3,0},{4,7},{5,6},{6,5},{7,4},{8,11},{9,10},{10,... | collective-permute-start | bytes 6152 | tf_op jit(solution)/shard_map/ppermute | solution.py:441
  70.9 1.8 %collective-permute-done.16.refs_6_ = f32[2,256]{1,0:T(2,128)S(1)} collective-permute-done((f32[2,256]{1,0:T(2,128)S(1)}, f32[2,256]{1,0:T(2,128)S(1)}, u32[]{:S(2)}, u32[]{:S(2)}) %collective-permute-start.16) | collective-permute-done | bytes 2080 | tf_op jit(solution)/shard_map/ppermute | solution.py:441
  72.7 1.5 %shard_map.56 = (f32[2,16,16,256]{3,2,1,0:T(8,128)S(1)}, f32[2,256]{1,0:T(2,128)S(1)}) custom-call(f32[2,16,16,256]{3,2,1,0:T(8,128)S(1)} %get-tuple-element.89.refs_0_, f32[2,16,16,256]{3,2,1,0:T(8,128)S(1)} %get-tuple-element.90.refs_1_, bf16[4,3,768,256]{3,2,1,0:T(8,128)(2,1)S(1)} %shard_map.47.refs_2_.refs_1_.weights, f32[4,256]{1,0:T(4,128)S(1)} %copy-done.1, ...), custom_call_target="tpu_custom_call" | custom-call | flops 1207959552 | bytes 1048576 | tf_op jit(solution)/shard_map/pallas_call | solution.py:24
  74.2 1.3 %collective-permute-start.17 = (f32[2,256]{1,0:T(2,128)S(1)}, f32[2,256]{1,0:T(2,128)S(1)}, u32[]{:S(2)}, u32[]{:S(2)}) collective-permute-start(f32[2,256]{1,0:T(2,128)S(1)} %get-tuple-element.93.refs_0_), channel_id=1, source_target_pairs={{0,3},{1,2},{2,1},{3,0},{4,7},{5,6},{6,5},{7,4},{8,11},{9,10},{10,... | collective-permute-start | bytes 6152 | tf_op jit(solution)/shard_map/ppermute | solution.py:441
  75.5 1.8 %collective-permute-done.17.refs_5_ = f32[2,256]{1,0:T(2,128)S(1)} collective-permute-done((f32[2,256]{1,0:T(2,128)S(1)}, f32[2,256]{1,0:T(2,128)S(1)}, u32[]{:S(2)}, u32[]{:S(2)}) %collective-permute-start.17) | collective-permute-done | bytes 2080 | tf_op jit(solution)/shard_map/ppermute | solution.py:441
  77.3 1.0 shard_map.58
  79.1 1.2 collective-permute-start.26
  80.3 3.8 %collective-permute-done.18.received.refs_1_.refs_3_ = f32[136,256]{1,0:T(8,128)S(1)} collective-permute-done((f32[136,256]{1,0:T(8,128)S(1)}, f32[136,256]{1,0:T(8,128)S(1)}, u32[]{:S(2)}, u32[]{:S(2)}) %collective-permute-start.18) | collective-permute-done | bytes 139296 | tf_op jit(solution)/shard_map/ppermute | solution.py:519
  84.9 1.3 %collective-permute-done.26.received.refs_4_ = f32[96,256]{1,0:T(8,128)S(1)} collective-permute-done((f32[96,256]{1,0:T(8,128)S(1)}, f32[96,256]{1,0:T(8,128)S(1)}, u32[]{:S(2)}, u32[]{:S(2)}) %collective-permute-start.26) | collective-permute-done | bytes 98336 | tf_op jit(solution)/shard_map/ppermute | solution.py:519
  86.5 3.0 %collective-permute-done.28.received.refs_5_ = f32[32,256]{1,0:T(8,128)S(1)} collective-permute-done((f32[32,256]{1,0:T(8,128)S(1)}, f32[32,256]{1,0:T(8,128)S(1)}, u32[]{:S(2)}, u32[]{:S(2)}) %collective-permute-start.28) | collective-permute-done | bytes 32800 | tf_op jit(solution)/shard_map/ppermute | solution.py:519
  91.3 0.9 collective-permute-done.29.refs_1_
  92.5 8.6 %collective-permute-start.30 = (f32[1,4,16,256]{3,2,1,0:T(8,128)S(1)}, f32[1,4,16,256]{3,2,1,0:T(8,128)S(1)}, u32[]{:S(2)}, u32[]{:S(2)}) collective-permute-start(f32[1,4,16,256]{3,2,1,0:T(8,128)S(1)} %get-tuple-element.116), channel_id=1, source_target_pairs={{0,1},{1,0},{2,3},{3,2},{4,5},{5,4},{6,7},{7,6},{8,9},{9,8},{10,11... | collective-permute-start | bytes 196616 | tf_op jit(solution)/shard_map/ppermute | solution.py:542
  101.1 1.0 collective-permute-start.34
  102.1 1.9 %collective-permute-start.36 = (f32[1,6,16,256]{3,2,1,0:T(8,128)S(1)}, f32[1,6,16,256]{3,2,1,0:T(8,128)S(1)}, u32[]{:S(2)}, u32[]{:S(2)}) collective-permute-start(f32[1,6,16,256]{3,2,1,0:T(8,128)S(1)} %get-tuple-element.139), channel_id=1, source_target_pairs={{0,1},{1,0},{2,3},{3,2},{4,5},{5,4},{6,7},{7,6},{8,9},{9,8},{10,11... | collective-permute-start | bytes 294920 | tf_op jit(solution)/shard_map/ppermute | solution.py:542
  104.8 0.9 collective-permute-done.34.refs_1_.refs_0_
  106.5 1.3 %collective-permute-done.36.refs_1_ = f32[1,6,16,256]{3,2,1,0:T(8,128)S(1)} collective-permute-done((f32[1,6,16,256]{3,2,1,0:T(8,128)S(1)}, f32[1,6,16,256]{3,2,1,0:T(8,128)S(1)}, u32[]{:S(2)}, u32[]{:S(2)}) %collective-permute-start.36) | collective-permute-done | bytes 98336 | tf_op jit(solution)/shard_map/ppermute | solution.py:542
  107.8 0.9 shard_map.73
  109.4 1.4 %collective-permute-start.35 = (f32[1,6,16,256]{3,2,1,0:T(8,128)S(1)}, f32[1,6,16,256]{3,2,1,0:T(8,128)S(1)}, u32[]{:S(2)}, u32[]{:S(2)}) collective-permute-start(f32[1,6,16,256]{3,2,1,0:T(8,128)S(1)} %get-tuple-element.138), channel_id=1, source_target_pairs={{0,1},{1,0},{2,3},{3,2},{4,5},{5,4},{6,7},{7,6},{8,13},{9,12},{10,... | collective-permute-start | bytes 294920 | tf_op jit(solution)/shard_map/ppermute | solution.py:570
  111.9 5.5 %collective-permute-done.33.refs_0_ = f32[1,2,16,256]{3,2,1,0:T(8,128)S(1)} collective-permute-done((f32[1,2,16,256]{3,2,1,0:T(8,128)S(1)}, f32[1,2,16,256]{3,2,1,0:T(8,128)S(1)}, u32[]{:S(2)}, u32[]{:S(2)}) %collective-permute-start.33) | collective-permute-done | bytes 32800 | tf_op jit(solution)/shard_map/ppermute | solution.py:570
  (71 shorter events, 10.5 us)
Async XLA Ops:
  0.0 1.0 copy-start
  1.2 5.1 %collective-permute-start = (f32[2,16,16,256]{3,2,1,0:T(8,128)S(1)}, f32[2,16,16,256]{3,2,1,0:T(8,128)S(1)}, u32[]{:S(2)}, u32[]{:S(2)}) collective-permute-start(f32[2,16,16,256]{3,2,1,0:T(8,128)S(1)} %get-tuple-element.75.refs_0_.refs_5_), channel_id=1, source_target_pairs={{0,1},{1,0},{2,3},{3,2},{4,5},{5,4},{6,7},{7,6},{8,9},{9,8},{10,11... | collective-permute-start | bytes 1572872 | tf_op jit(solution)/shard_map/ppermute | solution.py:467
  1.2 4.4 %collective-permute-start.1 = (f32[2,256]{1,0:T(2,128)S(1)}, f32[2,256]{1,0:T(2,128)S(1)}, u32[]{:S(2)}, u32[]{:S(2)}) collective-permute-start(f32[2,256]{1,0:T(2,128)S(1)} %get-tuple-element.76.refs_5_.refs_6_), channel_id=1, source_target_pairs={{0,1},{1,0},{2,3},{3,2},{4,5},{5,4},{6,7},{7,6},{8,9},{9,8},{10,11... | collective-permute-start | bytes 6152 | tf_op jit(solution)/shard_map/ppermute | solution.py:441
  1.7 3.9 %collective-permute-start.2 = (f32[2,256]{1,0:T(2,128)S(1)}, f32[2,256]{1,0:T(2,128)S(1)}, u32[]{:S(2)}, u32[]{:S(2)}) collective-permute-start(f32[2,256]{1,0:T(2,128)S(1)} %get-tuple-element.76.refs_5_.refs_6_), channel_id=1, source_target_pairs={{0,2},{1,3},{2,0},{3,1},{4,6},{5,7},{6,4},{7,5},{8,10},{9,11},{10,... | collective-permute-start | bytes 6152 | tf_op jit(solution)/shard_map/ppermute | solution.py:441
  3.2 3.0 %collective-permute-start.3 = (f32[2,256]{1,0:T(2,128)S(1)}, f32[2,256]{1,0:T(2,128)S(1)}, u32[]{:S(2)}, u32[]{:S(2)}) collective-permute-start(f32[2,256]{1,0:T(2,128)S(1)} %get-tuple-element.76.refs_5_.refs_6_), channel_id=1, source_target_pairs={{0,3},{1,2},{2,1},{3,0},{4,7},{5,6},{6,5},{7,4},{8,11},{9,10},{10,... | collective-permute-start | bytes 6152 | tf_op jit(solution)/shard_map/ppermute | solution.py:441
  3.2 3.0 %copy-start.1 = (f32[4,256]{1,0:T(4,128)S(1)}, f32[4,256]{1,0:T(4,128)}, u32[]{:S(2)}) copy-start(f32[4,256]{1,0:T(4,128)} %refs_2_.5) | copy-start | bytes 12292
  3.2 3.0 %copy-start.2 = (f32[4,256]{1,0:T(4,128)S(1)}, f32[4,256]{1,0:T(4,128)}, u32[]{:S(2)}) copy-start(f32[4,256]{1,0:T(4,128)} %refs_3_.15) | copy-start | bytes 12292
  7.8 3.1 %collective-permute-start.4 = (f32[2,256]{1,0:T(2,128)S(1)}, f32[2,256]{1,0:T(2,128)S(1)}, u32[]{:S(2)}, u32[]{:S(2)}) collective-permute-start(f32[2,256]{1,0:T(2,128)S(1)} %get-tuple-element.79.refs_0_.after), channel_id=1, source_target_pairs={{0,3},{1,2},{2,1},{3,0},{4,7},{5,6},{6,5},{7,4},{8,11},{9,10},{10,... | collective-permute-start | bytes 6152 | tf_op jit(solution)/shard_map/ppermute | solution.py:441
  12.4 3.1 %collective-permute-start.5 = (f32[2,256]{1,0:T(2,128)S(1)}, f32[2,256]{1,0:T(2,128)S(1)}, u32[]{:S(2)}, u32[]{:S(2)}) collective-permute-start(f32[2,256]{1,0:T(2,128)S(1)} %get-tuple-element.82.refs_5_), channel_id=1, source_target_pairs={{0,3},{1,2},{2,1},{3,0},{4,7},{5,6},{6,5},{7,4},{8,11},{9,10},{10,... | collective-permute-start | bytes 6152 | tf_op jit(solution)/shard_map/ppermute | solution.py:441
  17.0 3.1 %collective-permute-start.6 = (f32[2,256]{1,0:T(2,128)S(1)}, f32[2,256]{1,0:T(2,128)S(1)}, u32[]{:S(2)}, u32[]{:S(2)}) collective-permute-start(f32[2,256]{1,0:T(2,128)S(1)} %get-tuple-element.84.refs_4_), channel_id=1, source_target_pairs={{0,3},{1,2},{2,1},{3,0},{4,7},{5,6},{6,5},{7,4},{8,11},{9,10},{10,... | collective-permute-start | bytes 6152 | tf_op jit(solution)/shard_map/ppermute | solution.py:441
  21.0 16.9 %collective-permute-start.7 = (f32[2,16,16,256]{3,2,1,0:T(8,128)S(1)}, f32[2,16,16,256]{3,2,1,0:T(8,128)S(1)}, u32[]{:S(2)}, u32[]{:S(2)}) collective-permute-start(f32[2,16,16,256]{3,2,1,0:T(8,128)S(1)} %get-tuple-element.85), channel_id=1, source_target_pairs={{0,4},{4,8},{8,12},{12,16},{16,20},{20,24},{24,28},{1,5},{5,9},{9,... | collective-permute-start | bytes 1572872 | tf_op jit(solution)/shard_map/ppermute | solution.py:487
  24.4 3.1 %collective-permute-start.10 = (f32[2,256]{1,0:T(2,128)S(1)}, f32[2,256]{1,0:T(2,128)S(1)}, u32[]{:S(2)}, u32[]{:S(2)}) collective-permute-start(f32[2,256]{1,0:T(2,128)S(1)} %get-tuple-element.86), channel_id=1, source_target_pairs={{0,3},{1,2},{2,1},{3,0},{4,7},{5,6},{6,5},{7,4},{8,11},{9,10},{10,... | collective-permute-start | bytes 6152 | tf_op jit(solution)/shard_map/ppermute | solution.py:441
  25.4 2.1 %collective-permute-start.8 = (f32[2,256]{1,0:T(2,128)S(1)}, f32[2,256]{1,0:T(2,128)S(1)}, u32[]{:S(2)}, u32[]{:S(2)}) collective-permute-start(f32[2,256]{1,0:T(2,128)S(1)} %get-tuple-element.86), channel_id=1, source_target_pairs={{0,1},{1,0},{2,3},{3,2},{4,5},{5,4},{6,7},{7,6},{8,9},{9,8},{10,11... | collective-permute-start | bytes 6152 | tf_op jit(solution)/shard_map/ppermute | solution.py:441
  25.4 3.6 %collective-permute-start.9 = (f32[2,256]{1,0:T(2,128)S(1)}, f32[2,256]{1,0:T(2,128)S(1)}, u32[]{:S(2)}, u32[]{:S(2)}) collective-permute-start(f32[2,256]{1,0:T(2,128)S(1)} %get-tuple-element.86), channel_id=1, source_target_pairs={{0,2},{1,3},{2,0},{3,1},{4,6},{5,7},{6,4},{7,5},{8,10},{9,11},{10,... | collective-permute-start | bytes 6152 | tf_op jit(solution)/shard_map/ppermute | solution.py:441
  29.0 8.8 %collective-permute-start.11 = (f32[2,256]{1,0:T(2,128)S(1)}, f32[2,256]{1,0:T(2,128)S(1)}, u32[]{:S(2)}, u32[]{:S(2)}) collective-permute-start(f32[2,256]{1,0:T(2,128)S(1)} %add_add_fusion), channel_id=1, source_target_pairs={{0,4},{4,8},{8,12},{12,16},{16,20},{20,24},{24,28},{1,5},{5,9},{9,... | collective-permute-start | bytes 6152 | tf_op jit(solution)/shard_map/ppermute | solution.py:488
  31.0 19.5 %collective-permute-start.21 = (f32[576,256]{1,0:T(8,128)S(1)}, f32[576,256]{1,0:T(8,128)S(1)}, u32[]{:S(2)}, u32[]{:S(2)}) collective-permute-start(f32[576,256]{1,0:T(8,128)S(1)} %shard_map.60), channel_id=1, source_target_pairs={{0,4},{4,0},{8,12},{12,8},{16,20},{20,16},{24,28},{28,24},{1,5},{5... | collective-permute-start | bytes 1769480 | tf_op jit(solution)/shard_map/ppermute | solution.py:483
  38.8 24.2 %collective-permute-start.22 = (f32[576,256]{1,0:T(8,128)S(1)}, f32[576,256]{1,0:T(8,128)S(1)}, u32[]{:S(2)}, u32[]{:S(2)}) collective-permute-start(f32[576,256]{1,0:T(8,128)S(1)} %shard_map.61), channel_id=1, source_target_pairs={{0,4},{4,0},{8,12},{12,8},{16,20},{20,16},{24,28},{28,24},{1,5},{5... | collective-permute-start | bytes 1769480 | tf_op jit(solution)/shard_map/ppermute | solution.py:495
  40.3 27.8 %collective-permute-start.12 = (f32[2,16,16,256]{3,2,1,0:T(8,128)S(1)}, f32[2,16,16,256]{3,2,1,0:T(8,128)S(1)}, u32[]{:S(2)}, u32[]{:S(2)}) collective-permute-start(f32[2,16,16,256]{3,2,1,0:T(8,128)S(1)} %get-tuple-element.87.refs_0_), channel_id=1, source_target_pairs={{0,1},{1,0},{2,3},{3,2},{4,5},{5,4},{6,7},{7,6},{8,9},{9,8},{10,11... | collective-permute-start | bytes 1572872 | tf_op jit(solution)/shard_map/ppermute | solution.py:494
  50.5 39.2 %collective-permute-start.23 = (f32[576,256]{1,0:T(8,128)S(1)}, f32[576,256]{1,0:T(8,128)S(1)}, u32[]{:S(2)}, u32[]{:S(2)}) collective-permute-start(f32[576,256]{1,0:T(8,128)S(1)} %collective-permute-done.21.near_upper), channel_id=1, source_target_pairs={{0,1},{1,0},{2,3},{3,2},{4,5},{5,4},{6,7},{7,6},{8,9},{9,8},{10,11... | collective-permute-start | bytes 1769480 | tf_op jit(solution)/shard_map/ppermute | solution.py:496
  63.0 26.6 %collective-permute-start.24 = (f32[576,256]{1,0:T(8,128)S(1)}, f32[576,256]{1,0:T(8,128)S(1)}, u32[]{:S(2)}, u32[]{:S(2)}) collective-permute-start(f32[576,256]{1,0:T(8,128)S(1)} %collective-permute-done.22.near_lower), channel_id=1, source_target_pairs={{0,1},{1,0},{2,3},{3,2},{4,5},{5,4},{6,7},{7,6},{8,9},{9,8},{10,11... | collective-permute-start | bytes 1769480 | tf_op jit(solution)/shard_map/ppermute | solution.py:502
  63.0 2.0 %collective-permute-start.13 = (f32[2,256]{1,0:T(2,128)S(1)}, f32[2,256]{1,0:T(2,128)S(1)}, u32[]{:S(2)}, u32[]{:S(2)}) collective-permute-start(f32[2,256]{1,0:T(2,128)S(1)} %get-tuple-element.88.refs_0_.after), channel_id=1, source_target_pairs={{0,1},{1,0},{2,3},{3,2},{4,5},{5,4},{6,7},{7,6},{8,9},{9,8},{10,11... | collective-permute-start | bytes 6152 | tf_op jit(solution)/shard_map/ppermute | solution.py:441
  63.5 3.6 %collective-permute-start.14 = (f32[2,256]{1,0:T(2,128)S(1)}, f32[2,256]{1,0:T(2,128)S(1)}, u32[]{:S(2)}, u32[]{:S(2)}) collective-permute-start(f32[2,256]{1,0:T(2,128)S(1)} %get-tuple-element.88.refs_0_.after), channel_id=1, source_target_pairs={{0,2},{1,3},{2,0},{3,1},{4,6},{5,7},{6,4},{7,5},{8,10},{9,11},{10,... | collective-permute-start | bytes 6152 | tf_op jit(solution)/shard_map/ppermute | solution.py:441
  65.0 3.0 %collective-permute-start.15 = (f32[2,256]{1,0:T(2,128)S(1)}, f32[2,256]{1,0:T(2,128)S(1)}, u32[]{:S(2)}, u32[]{:S(2)}) collective-permute-start(f32[2,256]{1,0:T(2,128)S(1)} %get-tuple-element.88.refs_0_.after), channel_id=1, source_target_pairs={{0,3},{1,2},{2,1},{3,0},{4,7},{5,6},{6,5},{7,4},{8,11},{9,10},{10,... | collective-permute-start | bytes 6152 | tf_op jit(solution)/shard_map/ppermute | solution.py:441
  69.6 3.1 %collective-permute-start.16 = (f32[2,256]{1,0:T(2,128)S(1)}, f32[2,256]{1,0:T(2,128)S(1)}, u32[]{:S(2)}, u32[]{:S(2)}) collective-permute-start(f32[2,256]{1,0:T(2,128)S(1)} %get-tuple-element.91.refs_5_), channel_id=1, source_target_pairs={{0,3},{1,2},{2,1},{3,0},{4,7},{5,6},{6,5},{7,4},{8,11},{9,10},{10,... | collective-permute-start | bytes 6152 | tf_op jit(solution)/shard_map/ppermute | solution.py:441
  74.2 3.1 %collective-permute-start.17 = (f32[2,256]{1,0:T(2,128)S(1)}, f32[2,256]{1,0:T(2,128)S(1)}, u32[]{:S(2)}, u32[]{:S(2)}) collective-permute-start(f32[2,256]{1,0:T(2,128)S(1)} %get-tuple-element.93.refs_0_), channel_id=1, source_target_pairs={{0,3},{1,2},{2,1},{3,0},{4,7},{5,6},{6,5},{7,4},{8,11},{9,10},{10,... | collective-permute-start | bytes 6152 | tf_op jit(solution)/shard_map/ppermute | solution.py:441
  78.3 5.7 %collective-permute-start.18 = (f32[136,256]{1,0:T(8,128)S(1)}, f32[136,256]{1,0:T(8,128)S(1)}, u32[]{:S(2)}, u32[]{:S(2)}) collective-permute-start(f32[136,256]{1,0:T(8,128)S(1)} %get-tuple-element.96), channel_id=1, source_target_pairs={{0,4},{1,5},{2,6},{3,7},{4,0},{5,1},{6,2},{7,3},{8,13},{9,12},{10,... | collective-permute-start | bytes 417800 | tf_op jit(solution)/shard_map/ppermute | solution.py:519
  78.7 11.2 %collective-permute-start.20 = (f32[1,256,256]{2,1,0:T(8,128)S(1)}, f32[1,256,256]{2,1,0:T(8,128)S(1)}, u32[]{:S(2)}, u32[]{:S(2)}) collective-permute-start(f32[1,256,256]{2,1,0:T(8,128)S(1)} %get-tuple-element.98.refs_2_.refs_5_.refs_6_), channel_id=1, source_target_pairs={{0,1},{1,0},{2,3},{3,2},{4,5},{5,4},{6,7},{7,6},{8,9},{9,8},{10,11... | collective-permute-start | bytes 786440 | tf_op jit(solution)/shard_map/ppermute | solution.py:520
  79.1 7.0 %collective-permute-start.26 = (f32[96,256]{1,0:T(8,128)S(1)}, f32[96,256]{1,0:T(8,128)S(1)}, u32[]{:S(2)}, u32[]{:S(2)}) collective-permute-start(f32[96,256]{1,0:T(8,128)S(1)} %get-tuple-element.100), channel_id=1, source_target_pairs={{0,4},{1,5},{2,6},{3,7},{4,0},{5,1},{6,2},{7,3},{8,13},{9,12},{10,... | collective-permute-start | bytes 294920 | tf_op jit(solution)/shard_map/ppermute | solution.py:519
  84.1 5.8 %collective-permute-start.19 = (f32[1,8,16,256]{3,2,1,0:T(8,128)S(1)}, f32[1,8,16,256]{3,2,1,0:T(8,128)S(1)}, u32[]{:S(2)}, u32[]{:S(2)}) collective-permute-start(f32[1,8,16,256]{3,2,1,0:T(8,128)S(1)} %shard_map.59), channel_id=1, source_target_pairs={{0,9},{1,8},{2,11},{3,10},{4,13},{5,12},{6,15},{7,14},{8,1},{9,0},... | collective-permute-start | bytes 393224 | tf_op jit(solution)/shard_map/ppermute | solution.py:542
  86.1 3.4 %collective-permute-start.28 = (f32[32,256]{1,0:T(8,128)S(1)}, f32[32,256]{1,0:T(8,128)S(1)}, u32[]{:S(2)}, u32[]{:S(2)}) collective-permute-start(f32[32,256]{1,0:T(8,128)S(1)} %get-tuple-element.101), channel_id=1, source_target_pairs={{0,4},{1,5},{2,6},{3,7},{4,0},{5,1},{6,2},{7,3},{8,13},{9,12},{10,... | collective-permute-start | bytes 98312 | tf_op jit(solution)/shard_map/ppermute | solution.py:519
  89.5 1.3 %collective-permute-start.27 = (f32[1,6,16,256]{3,2,1,0:T(8,128)S(1)}, f32[1,6,16,256]{3,2,1,0:T(8,128)S(1)}, u32[]{:S(2)}, u32[]{:S(2)}) collective-permute-start(f32[1,6,16,256]{3,2,1,0:T(8,128)S(1)} %shard_map.64), channel_id=1, source_target_pairs={{0,9},{1,8},{2,11},{3,10},{4,13},{5,12},{6,15},{7,14},{8,1},{9,0},... | collective-permute-start | bytes 294920 | tf_op jit(solution)/shard_map/ppermute | solution.py:542
  90.2 2.3 %collective-permute-start.25 = (f32[1,6,16,256]{3,2,1,0:T(8,128)S(1)}, f32[1,6,16,256]{3,2,1,0:T(8,128)S(1)}, u32[]{:S(2)}, u32[]{:S(2)}) collective-permute-start(f32[1,6,16,256]{3,2,1,0:T(8,128)S(1)} %get-tuple-element.99), channel_id=1, source_target_pairs={{0,1},{1,0},{2,3},{3,2},{4,5},{5,4},{6,7},{7,6},{8,17},{9,16},{10,... | collective-permute-start | bytes 294920 | tf_op jit(solution)/shard_map/ppermute | solution.py:542
  90.8 10.3 %collective-permute-start.31 = (f32[1,6,16,256]{3,2,1,0:T(8,128)S(1)}, f32[1,6,16,256]{3,2,1,0:T(8,128)S(1)}, u32[]{:S(2)}, u32[]{:S(2)}) collective-permute-start(f32[1,6,16,256]{3,2,1,0:T(8,128)S(1)} %get-tuple-element.117), channel_id=1, source_target_pairs={{0,1},{1,0},{2,3},{3,2},{4,5},{5,4},{6,7},{7,6},{8,17},{9,16},{10,... | collective-permute-start | bytes 294920 | tf_op jit(solution)/shard_map/ppermute | solution.py:542
  91.0 1.2 %collective-permute-start.29 = (f32[1,2,16,256]{3,2,1,0:T(8,128)S(1)}, f32[1,2,16,256]{3,2,1,0:T(8,128)S(1)}, u32[]{:S(2)}, u32[]{:S(2)}) collective-permute-start(f32[1,2,16,256]{3,2,1,0:T(8,128)S(1)} %shard_map.65), channel_id=1, source_target_pairs={{0,9},{1,8},{2,11},{3,10},{4,13},{5,12},{6,15},{7,14},{8,1},{9,0},... | collective-permute-start | bytes 98312 | tf_op jit(solution)/shard_map/ppermute | solution.py:542
  92.2 9.9 %collective-permute-start.32 = (f32[1,4,16,256]{3,2,1,0:T(8,128)S(1)}, f32[1,4,16,256]{3,2,1,0:T(8,128)S(1)}, u32[]{:S(2)}, u32[]{:S(2)}) collective-permute-start(f32[1,4,16,256]{3,2,1,0:T(8,128)S(1)} %get-tuple-element.118), channel_id=1, source_target_pairs={{0,1},{1,0},{2,3},{3,2},{4,5},{5,4},{6,7},{7,6},{8,17},{9,16},{10,... | collective-permute-start | bytes 196616 | tf_op jit(solution)/shard_map/ppermute | solution.py:542
  92.5 11.4 %collective-permute-start.30 = (f32[1,4,16,256]{3,2,1,0:T(8,128)S(1)}, f32[1,4,16,256]{3,2,1,0:T(8,128)S(1)}, u32[]{:S(2)}, u32[]{:S(2)}) collective-permute-start(f32[1,4,16,256]{3,2,1,0:T(8,128)S(1)} %get-tuple-element.116), channel_id=1, source_target_pairs={{0,1},{1,0},{2,3},{3,2},{4,5},{5,4},{6,7},{7,6},{8,9},{9,8},{10,11... | collective-permute-start | bytes 196616 | tf_op jit(solution)/shard_map/ppermute | solution.py:542
  101.1 4.5 %collective-permute-start.34 = (f32[1,6,16,256]{3,2,1,0:T(8,128)S(1)}, f32[1,6,16,256]{3,2,1,0:T(8,128)S(1)}, u32[]{:S(2)}, u32[]{:S(2)}) collective-permute-start(f32[1,6,16,256]{3,2,1,0:T(8,128)S(1)} %get-tuple-element.133), channel_id=1, source_target_pairs={{0,1},{1,0},{2,3},{3,2},{4,5},{5,4},{6,7},{7,6},{8,9},{9,8},{10,11... | collective-permute-start | bytes 294920 | tf_op jit(solution)/shard_map/ppermute | solution.py:542
  102.1 5.7 %collective-permute-start.36 = (f32[1,6,16,256]{3,2,1,0:T(8,128)S(1)}, f32[1,6,16,256]{3,2,1,0:T(8,128)S(1)}, u32[]{:S(2)}, u32[]{:S(2)}) collective-permute-start(f32[1,6,16,256]{3,2,1,0:T(8,128)S(1)} %get-tuple-element.139), channel_id=1, source_target_pairs={{0,1},{1,0},{2,3},{3,2},{4,5},{5,4},{6,7},{7,6},{8,9},{9,8},{10,11... | collective-permute-start | bytes 294920 | tf_op jit(solution)/shard_map/ppermute | solution.py:542
  108.6 2.6 %collective-permute-start.38 = (f32[1,16,16,256]{3,2,1,0:T(8,128)S(1)}, f32[1,16,16,256]{3,2,1,0:T(8,128)S(1)}, u32[]{:S(2)}, u32[]{:S(2)}) collective-permute-start(f32[1,16,16,256]{3,2,1,0:T(8,128)S(1)} %get-tuple-element.144.own), channel_id=1, source_target_pairs={{0,1},{1,0},{2,3},{3,2},{4,5},{5,4},{6,7},{7,6},{8,9},{9,8},{10,11... | collective-permute-start | bytes 786440 | tf_op jit(solution)/shard_map/ppermute | solution.py:577
  109.1 8.3 %collective-permute-start.37 = (f32[1,8,16,256]{3,2,1,0:T(8,128)S(1)}, f32[1,8,16,256]{3,2,1,0:T(8,128)S(1)}, u32[]{:S(2)}, u32[]{:S(2)}) collective-permute-start(f32[1,8,16,256]{3,2,1,0:T(8,128)S(1)} %get-tuple-element.143), channel_id=1, source_target_pairs={{0,1},{1,0},{2,3},{3,2},{4,5},{5,4},{6,7},{7,6},{8,13},{9,12},{10,... | collective-permute-start | bytes 393224 | tf_op jit(solution)/shard_map/ppermute | solution.py:570
  109.4 7.9 %collective-permute-start.35 = (f32[1,6,16,256]{3,2,1,0:T(8,128)S(1)}, f32[1,6,16,256]{3,2,1,0:T(8,128)S(1)}, u32[]{:S(2)}, u32[]{:S(2)}) collective-permute-start(f32[1,6,16,256]{3,2,1,0:T(8,128)S(1)} %get-tuple-element.138), channel_id=1, source_target_pairs={{0,1},{1,0},{2,3},{3,2},{4,5},{5,4},{6,7},{7,6},{8,13},{9,12},{10,... | collective-permute-start | bytes 294920 | tf_op jit(solution)/shard_map/ppermute | solution.py:570
  110.8 6.6 %collective-permute-start.33 = (f32[1,2,16,256]{3,2,1,0:T(8,128)S(1)}, f32[1,2,16,256]{3,2,1,0:T(8,128)S(1)}, u32[]{:S(2)}, u32[]{:S(2)}) collective-permute-start(f32[1,2,16,256]{3,2,1,0:T(8,128)S(1)} %get-tuple-element.132), channel_id=1, source_target_pairs={{0,1},{1,0},{2,3},{3,2},{4,5},{5,4},{6,7},{7,6},{8,13},{9,12},{10,... | collective-permute-start | bytes 98312 | tf_op jit(solution)/shard_map/ppermute | solution.py:570

commit v5 on v4

--- a/solution.py
+++ b/solution.py
@@ -95,7 +95,7 @@
     return center, lax.rsqrt(totals[1:2] * (1.0 / entries) - center * center + epsilon)
 
 
-def layer_kernel(number, count, keep, parts, batch_entries, kind, cut, *refs):
+def layer_kernel(number, slot, count, keep, parts, batch_entries, kind, cut, *refs):
     states, refs = refs[:count], refs[count:]
     weights, gains, offsets = refs[:3]
     totals = refs[3 : 3 + parts]
@@ -133,8 +133,14 @@
     for i in range(count * samples):
         lay_out(jnp.maximum((load(i) - center) * scale + offset, 0.0), taps.at[i], width)
     total = jnp.zeros((2, channels), jnp.float32)
+    changes = 0.0
+    for row in range(3):
+        rows_in = [taps[i, row * width : row * width + entries] for i in range(count * samples)]
+        changes += jnp.dot(
+            jnp.concatenate(rows_in, axis=0), weights[slot, row], preferred_element_type=jnp.float32
+        )
     for i in range(count * samples):
-        change = convolved(taps.at[i], lambda row: weights[number, row], width, entries)
+        change = changes[i * entries : (i + 1) * entries]
         values = load(i)
         made = values + fine_step * change
         if kind == "last":
@@ -168,8 +174,9 @@
         )
 
 
-def layer(number, states, weights, gains, offsets, totals, batch_entries, kind, extra=(), cut=None, keep=None):
+def layer(number, states, kernels, gains, offsets, totals, batch_entries, kind, extra=(), cut=None, keep=None):
     state, keep = states[0], keep or len(states)
+    weights, slot = (kernels[0], 0) if number == 0 else (kernels[1], number - 1)
     samples, rows, width, channels = state.shape
     entries = rows * width
     half = samples // 2
@@ -188,7 +195,7 @@
             outs += (f32(*state.shape), f32(8, channels))
     return call(
         functools.partial(
-            layer_kernel, number, len(states), keep, len(totals), batch_entries, kind, cut
+            layer_kernel, number, slot, len(states), keep, len(totals), batch_entries, kind, cut
         ),
         (*states, weights, gains, offsets, *totals, *extra),
         outs,
@@ -199,27 +206,47 @@
     )
 
 
-def widen_kernel(part, weights, after, out):
-    piece = out.shape[0] // 3
-    at = pl.multiple_of((lax.axis_index("batch") % 2) * 2 * piece + part * piece, piece)
+def weight_parts(inner):
+    half, cut = inner // 2, inner // 2 * 5 // 8 // 16 * 16
+    return half, ((0, cut), (cut, half))
+
+
+def widen_kernel(part, stored, weights, *refs):
+    out = refs[-3] if stored else refs[-1]
+    half, parts = weight_parts(weights.shape[2])
+    low, high = parts[part]
+    piece = high - low
+    at = pl.multiple_of((lax.axis_index("batch") % 2) * half + low, 16)
+    if stored:
+        held, done = refs[-2:]
+        copy = pltpu.make_async_copy(weights.at[0, :, pl.ds(at, piece)], held, done)
+        copy.start()
+        copy.wait()
     for row in range(3):
-        out[row * piece : (row + 1) * piece] = weights[0, row, pl.ds(at, piece)].astype(jnp.float32)
-
-
-def widen(part, weights, after):
+        values = held[row] if stored else weights[0, row, pl.ds(at, piece)]
+        out[row * piece : (row + 1) * piece] = values.astype(jnp.float32)
+
+
+def widen(part, weights, after, stored):
     inner, channels = weights.shape[2:]
-    piece = inner // 4
+    low, high = weight_parts(inner)[1][part]
+    piece = high - low
     return call(
-        functools.partial(widen_kernel, part),
+        functools.partial(widen_kernel, part, stored),
         (weights, after),
         f32(3 * piece, channels),
+        [pltpu.VMEM((3, piece, channels), jnp.bfloat16), pltpu.SemaphoreType.DMA] if stored else [],
+        specs=[in_place if stored else whole, whole],
         moved=3 * piece * channels * 6,
-    )
-
-
-def stage_kernel(weights, out, done):
+        limit=51 << 20 if stored else vmem_bytes,
+    )
+
+
+def stage_kernel(first, weights, *refs):
+    out, done = refs[-2:]
     copies = [
-        pltpu.make_async_copy(weights.at[n], out.at[n], done.at[n]) for n in range(out.shape[0])
+        pltpu.make_async_copy(weights.at[first + n], out.at[n], done.at[n])
+        for n in range(out.shape[0])
     ]
     for copy in copies:
         copy.start()
@@ -227,16 +254,28 @@
         copy.wait()
 
 
+def stage(first, count, weights, after, limit):
+    return call(
+        functools.partial(stage_kernel, first),
+        (weights, after),
+        jax.ShapeDtypeStruct((count, *weights.shape[1:]), weights.dtype),
+        [pltpu.SemaphoreType.DMA((count,))],
+        specs=[in_place, whole],
+        moved=weights.size,
+        limit=limit,
+    )
+
+
 def gather_kernel(weights, near_upper, near_lower, far_upper, far_lower, out):
     parity, core = lax.axis_index("depth") % 2, lax.axis_index("batch") % 2
-    piece = near_upper.shape[0] // 3
     out[parity] = weights[0]
-    for part, pieces in enumerate(((near_upper, far_upper), (near_lower, far_lower))):
+    half, parts = weight_parts(weights.shape[2])
+    for (low, high), pieces in zip(parts, ((near_upper, far_upper), (near_lower, far_lower))):
         for owner, source in ((core, pieces[0]), (1 - core, pieces[1])):
-            at = pl.multiple_of(owner * 2 * piece + part * piece, piece)
+            at = pl.multiple_of(owner * half + low, 16)
             for row in range(3):
-                values = source[row * piece : (row + 1) * piece]
-                out[1 - parity, row, pl.ds(at, piece)] = values.astype(jnp.bfloat16)
+                values = source[row * (high - low) : (row + 1) * (high - low)]
+                out[1 - parity, row, pl.ds(at, high - low)] = values.astype(jnp.bfloat16)
 
 
 def relay_kernel(low, high, received, early, out):
@@ -465,23 +504,19 @@
     )
     first_totals = gathered(sums)
     other = lax.ppermute(initial, "batch", cores)
-    weights = call(
-        stage_kernel,
-        (weights,),
-        jax.ShapeDtypeStruct(weights.shape, weights.dtype),
-        [pltpu.SemaphoreType.DMA((layers_of_block,))],
-        specs=[in_place],
-        moved=weights.size * 4,
-        limit=47 << 20,
-    )
-    norms = (weights, norm_scale, norm_shift)
+    near_upper = lax.ppermute(widen(0, weights, sums, True), "depth", partners)
+    head = stage(0, 1, weights, sums, 51 << 20)
+    norms = (norm_scale, norm_shift)
     states, totals = (initial, other), first_totals
     for number in range(layers_of_block - 1):
         keep = 2 if number < layers_of_block - 2 else 1
-        *states, sums = run(number, states, *norms, totals, kind="plain", keep=keep)
         if number == 0:
-            near_upper = lax.ppermute(widen(0, weights, sums), "depth", partners)
-        totals = gathered(sums, number == 0, True)
+            *states, sums = run(0, states, (head,), *norms, totals, kind="plain", keep=keep)
+            rest = stage(1, layers_of_block - 1, weights, sums, 48 << 20)
+            norms = ((head, rest), *norms)
+        else:
+            *states, sums = run(number, states, *norms, totals, kind="plain", keep=keep)
+        totals = gathered(sums, False, True)
     current, sums = run(layers_of_block - 1, states[:1], *norms, totals, kind="plain")
     totals = gathered(sums)
     arrived = lax.ppermute(current, "depth", onward)
@@ -492,7 +527,7 @@
         0, (arrived,), *norms, (arrived_totals,), kind="first", extra=(initial, *first_totals)
     )
     other = lax.ppermute(current, "batch", cores)
-    near_lower = lax.ppermute(widen(1, weights, sums), "depth", partners)
+    near_lower = lax.ppermute(widen(1, head, sums, False), "depth", partners)
     far_upper = lax.ppermute(near_upper, "batch", cores)
     states = (current, other)
     for number in range(1, layers_of_block - 1):
@@ -511,7 +546,7 @@
     )
     kernels = call(
         gather_kernel,
-        (weights, near_upper, near_lower, far_upper, far_lower),
+        (head, near_upper, near_lower, far_upper, far_lower),
         jax.ShapeDtypeStruct((2, 3, 3 * channels, channels), jnp.bfloat16),
         moved=9 * channels * channels * 8,
     )

time: 120 us -> 112 us (0.933)
  waiting for transfers between devices: 60 us -> 47.3 us
  starting transfers between devices: 39.2 us -> 43 us
  Pallas kernels: 17.5 us -> 18.9 us
    ppermute x2, waiting for transfers between devices: 22.8 us -> 2.57 us  [the longest x1 2.57 us: steps(): near_lower = lax.ppermute(widen(1, head, sums, False), 'depth', partners)]
    ppermute x1, waiting for transfers between devices: 6.75 us -> 17.6 us  [steps(): arrived_totals = lax.ppermute(sum(totals[1:], totals[0]), 'depth', onward)]
    ppermute x3, starting transfers between devices: 1.94 us -> 3.94 us  [steps(): exchange = [lax.ppermute(part, both, swaps) for part in sent]]
    ppermute x1, starting transfers between devices: 1.91 us -> 3.84 us  [steps(): arrived_totals = lax.ppermute(sum(totals[1:], totals[0]), 'depth', onward)]
    ppermute x3, waiting for transfers between devices: 8 us -> 6.07 us  [steps(): exchange = [lax.ppermute(part, both, swaps) for part in sent]]
    ppermute x14, starting transfers between devices: 13.7 us -> 12.1 us  [gathered(): lax.ppermute(sums, 'batch', [(i, i ^ m) for i in range(group)])]
    pallas_call x30, Pallas kernels: 17.5 us -> 18.9 us  [call(): pl.pallas_call(body, out_shape=outs, in_specs=[whole] * len(operands) if...]
  transfers between devices with their start and end apart: 39 -> 39, of which waited for: 21 -> 21; matrix products, arithmetic and copies ran while one was open for 0% -> 0% of each run, Pallas kernels for 9% -> 11%
where the time goes in v5:
time: 112 us; the launch traced here: 111 us
  waiting for transfers between devices  47.3 us (42%)
  starting transfers between devices  43 us (38%)
  Pallas kernels  18.9 us (17%)
    pallas_call x30, Pallas kernels, call(): pl.pallas_call(body, out_shape=outs, in_specs=[whole] * len(operands) if...  18.9 us
    ppermute x1, waiting for transfers between devices, steps(): arrived_totals = lax.ppermute(sum(totals[1:], totals[0]), 'depth', onward)  17.6 us
    ppermute x9, starting transfers between devices, steps(): arriving = [lax.ppermute(part, both, route) for part in passed]  13.1 us
    ppermute x14, waiting for transfers between devices, gathered(): lax.ppermute(sums, 'batch', [(i, i ^ m) for i in range(group)])  12.8 us
    ppermute x14, starting transfers between devices, gathered(): lax.ppermute(sums, 'batch', [(i, i ^ m) for i in range(group)])  12.1 us
    ppermute x3, waiting for transfers between devices, steps(): exchange = [lax.ppermute(part, both, swaps) for part in sent]  6.07 us
    ppermute x3, waiting for transfers between devices, steps(): back.append(lax.ppermute(gives[back_spans[n]], both, backs))  4.85 us
    ppermute x3, starting transfers between devices, steps(): exchange = [lax.ppermute(part, both, swaps) for part in sent]  3.94 us
  transfers between devices with their start and end apart: 39, of which 21 were waited for; matrix products, arithmetic and copies ran while one was open for 0% of the time, Pallas kernels for 11%

profile of v5, /device:TPU:24, one launch (start us, length us, event | category | flops | bytes accessed | tf_op | source)
XLA Modules:
  0.0 110.8 jit_solution(528064189284478022)
XLA Ops:
  0.0 1.0 copy-done
  1.7 1.5 %collective-permute-start.2 = (f32[2,256]{1,0:T(2,128)S(1)}, f32[2,256]{1,0:T(2,128)S(1)}, u32[]{:S(2)}, u32[]{:S(2)}) collective-permute-start(f32[2,256]{1,0:T(2,128)S(1)} %get-tuple-element.76.refs_0_.refs_5_.refs_6_), channel_id=1, source_target_pairs={{0,2},{1,3},{2,0},{3,1},{4,6},{5,7},{6,4},{7,5},{8,10},{9,11},{10,... | collective-permute-start | bytes 6152 | tf_op jit(solution)/shard_map/ppermute | solution.py:480
  3.2 1.3 %shard_map.47.refs_2_.refs_1_.weights = bf16[1,3,768,256]{3,2,1,0:T(8,128)(2,1)S(1)} custom-call(bf16[4,3,768,256]{3,2,1,0:T(8,128)(2,1)} %bitcast.4, f32[2,256]{1,0:T(2,128)S(1)} %get-tuple-element.76.refs_0_.refs_5_.refs_6_), custom_call_target="tpu_custom_call" | custom-call | bytes 2359296 | tf_op jit(solution)/shard_map/pallas_call | solution.py:24
  5.3 0.9 collective-permute-done.3.refs_8_.refs_9_
  6.3 1.5 %shard_map.48 = (f32[2,16,16,256]{3,2,1,0:T(8,128)S(1)}, f32[2,16,16,256]{3,2,1,0:T(8,128)S(1)}, f32[2,256]{1,0:T(2,128)S(1)}) custom-call(f32[2,16,16,256]{3,2,1,0:T(8,128)S(1)} %get-tuple-element.75.refs_0_.refs_5_, f32[2,16,16,256]{3,2,1,0:T(8,128)S(1)} %collective-permute-done.refs_1_, bf16[1,3,768,256]{3,2,1,0:T(8,128)(2,1)S(1)} %shard_map.47.refs_2_.refs_1_.weights, ...), custom_call_target="tpu_custom_call" | custom-call | flops 1207959552 | bytes 1048576 | tf_op jit(solution)/shard_map/pallas_call | solution.py:24
  8.1 2.0 %shard_map.49.refs_2_.refs_1_ = bf16[3,3,768,256]{3,2,1,0:T(8,128)(2,1)S(1)} custom-call(bf16[4,3,768,256]{3,2,1,0:T(8,128)(2,1)} %bitcast.5, f32[2,256]{1,0:T(2,128)S(1)} %get-tuple-element.79.refs_0_.refs_5_), custom_call_target="tpu_custom_call" | custom-call | bytes 2359296 | tf_op jit(solution)/shard_map/pallas_call | solution.py:24
  10.8 1.5 %shard_map.50 = (f32[2,16,16,256]{3,2,1,0:T(8,128)S(1)}, f32[2,16,16,256]{3,2,1,0:T(8,128)S(1)}, f32[2,256]{1,0:T(2,128)S(1)}) custom-call(f32[2,16,16,256]{3,2,1,0:T(8,128)S(1)} %get-tuple-element.77.refs_0_, f32[2,16,16,256]{3,2,1,0:T(8,128)S(1)} %get-tuple-element.78.refs_1_, bf16[3,3,768,256]{3,2,1,0:T(8,128)(2,1)S(1)} %shard_map.49.refs_2_.refs_1_, ...), custom_call_target="tpu_custom_call" | custom-call | flops 1207959552 | bytes 1048576 | tf_op jit(solution)/shard_map/pallas_call | solution.py:24
  13.1 2.3 %collective-permute-done.5.refs_6_ = f32[2,256]{1,0:T(2,128)S(1)} collective-permute-done((f32[2,256]{1,0:T(2,128)S(1)}, f32[2,256]{1,0:T(2,128)S(1)}, u32[]{:S(2)}, u32[]{:S(2)}) %collective-permute-start.5) | collective-permute-done | bytes 2080 | tf_op jit(solution)/shard_map/ppermute | solution.py:480
  15.4 1.5 %shard_map.51 = (f32[2,16,16,256]{3,2,1,0:T(8,128)S(1)}, f32[2,256]{1,0:T(2,128)S(1)}) custom-call(f32[2,16,16,256]{3,2,1,0:T(8,128)S(1)} %get-tuple-element.80.refs_0_, f32[2,16,16,256]{3,2,1,0:T(8,128)S(1)} %get-tuple-element.81.refs_1_, bf16[3,3,768,256]{3,2,1,0:T(8,128)(2,1)S(1)} %shard_map.49.refs_2_.refs_1_, f32[4,256]{1,0:T(4,128)S(1)} %copy-done.1, ...), custom_call_target="tpu_custom_call" | custom-call | flops 1207959552 | bytes 1048576 | tf_op jit(solution)/shard_map/pallas_call | solution.py:24
  16.8 0.8 collective-permute-start.6
  17.6 2.3 %collective-permute-done.6.refs_5_ = f32[2,256]{1,0:T(2,128)S(1)} collective-permute-done((f32[2,256]{1,0:T(2,128)S(1)}, f32[2,256]{1,0:T(2,128)S(1)}, u32[]{:S(2)}, u32[]{:S(2)}) %collective-permute-start.6) | collective-permute-done | bytes 2080 | tf_op jit(solution)/shard_map/ppermute | solution.py:480
  19.9 0.8 shard_map.52
  20.7 3.4 %collective-permute-start.7 = (f32[2,16,16,256]{3,2,1,0:T(8,128)S(1)}, f32[2,16,16,256]{3,2,1,0:T(8,128)S(1)}, u32[]{:S(2)}, u32[]{:S(2)}) collective-permute-start(f32[2,16,16,256]{3,2,1,0:T(8,128)S(1)} %get-tuple-element.85), channel_id=1, source_target_pairs={{0,4},{4,8},{8,12},{12,16},{16,20},{20,24},{24,28},{1,5},{5,9},{9,... | collective-permute-start | bytes 1572872 | tf_op jit(solution)/shard_map/ppermute | solution.py:522
  24.2 1.1 shard_map.60
  26.1 1.4 %collective-permute-start.9 = (f32[2,256]{1,0:T(2,128)S(1)}, f32[2,256]{1,0:T(2,128)S(1)}, u32[]{:S(2)}, u32[]{:S(2)}) collective-permute-start(f32[2,256]{1,0:T(2,128)S(1)} %get-tuple-element.86), channel_id=1, source_target_pairs={{0,2},{1,3},{2,0},{3,1},{4,6},{5,7},{6,4},{7,5},{8,10},{9,11},{10,... | collective-permute-start | bytes 6152 | tf_op jit(solution)/shard_map/ppermute | solution.py:480
  27.5 0.9 collective-permute-done.10
  28.4 1.3 %collective-permute-done.9 = f32[2,256]{1,0:T(2,128)S(1)} collective-permute-done((f32[2,256]{1,0:T(2,128)S(1)}, f32[2,256]{1,0:T(2,128)S(1)}, u32[]{:S(2)}, u32[]{:S(2)}) %collective-permute-start.9) | collective-permute-done | bytes 2080 | tf_op jit(solution)/shard_map/ppermute | solution.py:480
  29.7 3.8 %collective-permute-start.11 = (f32[2,256]{1,0:T(2,128)S(1)}, f32[2,256]{1,0:T(2,128)S(1)}, u32[]{:S(2)}, u32[]{:S(2)}) collective-permute-start(f32[2,256]{1,0:T(2,128)S(1)} %add_add_fusion), channel_id=1, source_target_pairs={{0,4},{4,8},{8,12},{12,16},{16,20},{20,24},{24,28},{1,5},{5,9},{9,... | collective-permute-start | bytes 6152 | tf_op jit(solution)/shard_map/ppermute | solution.py:523
  33.5 17.6 %collective-permute-done.11.refs_4_ = f32[2,256]{1,0:T(2,128)S(1)} collective-permute-done((f32[2,256]{1,0:T(2,128)S(1)}, f32[2,256]{1,0:T(2,128)S(1)}, u32[]{:S(2)}, u32[]{:S(2)}) %collective-permute-start.11) | collective-permute-done | bytes 2080 | tf_op jit(solution)/shard_map/ppermute | solution.py:523
  51.1 0.9 shard_map.53
  52.2 2.5 %collective-permute-start.22 = (f32[432,256]{1,0:T(8,128)S(1)}, f32[432,256]{1,0:T(8,128)S(1)}, u32[]{:S(2)}, u32[]{:S(2)}) collective-permute-start(f32[432,256]{1,0:T(8,128)S(1)} %shard_map.61), channel_id=1, source_target_pairs={{0,4},{4,0},{8,12},{12,8},{16,20},{20,16},{24,28},{28,24},{1,5},{5... | collective-permute-start | bytes 1327112 | tf_op jit(solution)/shard_map/ppermute | solution.py:530
  55.2 1.4 %collective-permute-start.14 = (f32[2,256]{1,0:T(2,128)S(1)}, f32[2,256]{1,0:T(2,128)S(1)}, u32[]{:S(2)}, u32[]{:S(2)}) collective-permute-start(f32[2,256]{1,0:T(2,128)S(1)} %get-tuple-element.88.refs_0_), channel_id=1, source_target_pairs={{0,2},{1,3},{2,0},{3,1},{4,6},{5,7},{6,4},{7,5},{8,10},{9,11},{10,... | collective-permute-start | bytes 6152 | tf_op jit(solution)/shard_map/ppermute | solution.py:480
  56.9 1.2 %collective-permute-start.15 = (f32[2,256]{1,0:T(2,128)S(1)}, f32[2,256]{1,0:T(2,128)S(1)}, u32[]{:S(2)}, u32[]{:S(2)}) collective-permute-start(f32[2,256]{1,0:T(2,128)S(1)} %get-tuple-element.88.refs_0_), channel_id=1, source_target_pairs={{0,3},{1,2},{2,1},{3,0},{4,7},{5,6},{6,5},{7,4},{8,11},{9,10},{10,... | collective-permute-start | bytes 6152 | tf_op jit(solution)/shard_map/ppermute | solution.py:480
  58.8 1.1 %collective-permute-done.15.refs_8_ = f32[2,256]{1,0:T(2,128)S(1)} collective-permute-done((f32[2,256]{1,0:T(2,128)S(1)}, f32[2,256]{1,0:T(2,128)S(1)}, u32[]{:S(2)}, u32[]{:S(2)}) %collective-permute-start.15) | collective-permute-done | bytes 2080 | tf_op jit(solution)/shard_map/ppermute | solution.py:480
  59.9 1.5 %shard_map.55 = (f32[2,16,16,256]{3,2,1,0:T(8,128)S(1)}, f32[2,16,16,256]{3,2,1,0:T(8,128)S(1)}, f32[2,256]{1,0:T(2,128)S(1)}) custom-call(f32[2,16,16,256]{3,2,1,0:T(8,128)S(1)} %get-tuple-element.87.refs_0_, f32[2,16,16,256]{3,2,1,0:T(8,128)S(1)} %collective-permute-done.12.refs_1_, bf16[3,3,768,256]{3,2,1,0:T(8,128)(2,1)S(1)} %shard_map.49.refs_2_.refs_1_, ...), custom_call_target="tpu_custom_call" | custom-call | flops 1207959552 | bytes 1048576 | tf_op jit(solution)/shard_map/pallas_call | solution.py:24
  61.4 1.5 %collective-permute-start.16 = (f32[2,256]{1,0:T(2,128)S(1)}, f32[2,256]{1,0:T(2,128)S(1)}, u32[]{:S(2)}, u32[]{:S(2)}) collective-permute-start(f32[2,256]{1,0:T(2,128)S(1)} %get-tuple-element.91.refs_5_), channel_id=1, source_target_pairs={{0,3},{1,2},{2,1},{3,0},{4,7},{5,6},{6,5},{7,4},{8,11},{9,10},{10,... | collective-permute-start | bytes 6152 | tf_op jit(solution)/shard_map/ppermute | solution.py:480
  62.9 2.6 %collective-permute-done.22.near_lower = f32[432,256]{1,0:T(8,128)S(1)} collective-permute-done((f32[432,256]{1,0:T(8,128)S(1)}, f32[432,256]{1,0:T(8,128)S(1)}, u32[]{:S(2)}, u32[]{:S(2)}) %collective-permute-start.22) | collective-permute-done | bytes 442400 | tf_op jit(solution)/shard_map/ppermute | solution.py:530
  65.5 1.5 %shard_map.56 = (f32[2,16,16,256]{3,2,1,0:T(8,128)S(1)}, f32[2,256]{1,0:T(2,128)S(1)}) custom-call(f32[2,16,16,256]{3,2,1,0:T(8,128)S(1)} %get-tuple-element.89.refs_0_, f32[2,16,16,256]{3,2,1,0:T(8,128)S(1)} %get-tuple-element.90.refs_1_, bf16[3,3,768,256]{3,2,1,0:T(8,128)(2,1)S(1)} %shard_map.49.refs_2_.refs_1_, f32[4,256]{1,0:T(4,128)S(1)} %copy-done.1, ...), custom_call_target="tpu_custom_call" | custom-call | flops 1207959552 | bytes 1048576 | tf_op jit(solution)/shard_map/pallas_call | solution.py:24
  67.0 1.5 %collective-permute-start.17 = (f32[2,256]{1,0:T(2,128)S(1)}, f32[2,256]{1,0:T(2,128)S(1)}, u32[]{:S(2)}, u32[]{:S(2)}) collective-permute-start(f32[2,256]{1,0:T(2,128)S(1)} %get-tuple-element.93.refs_0_), channel_id=1, source_target_pairs={{0,3},{1,2},{2,1},{3,0},{4,7},{5,6},{6,5},{7,4},{8,11},{9,10},{10,... | collective-permute-start | bytes 6152 | tf_op jit(solution)/shard_map/ppermute | solution.py:480
  68.5 1.5 %collective-permute-done.17.refs_5_ = f32[2,256]{1,0:T(2,128)S(1)} collective-permute-done((f32[2,256]{1,0:T(2,128)S(1)}, f32[2,256]{1,0:T(2,128)S(1)}, u32[]{:S(2)}, u32[]{:S(2)}) %collective-permute-start.17) | collective-permute-done | bytes 2080 | tf_op jit(solution)/shard_map/ppermute | solution.py:480
  70.1 1.0 shard_map.58
  71.0 1.9 %collective-permute-start.18 = (f32[136,256]{1,0:T(8,128)S(1)}, f32[136,256]{1,0:T(8,128)S(1)}, u32[]{:S(2)}, u32[]{:S(2)}) collective-permute-start(f32[136,256]{1,0:T(8,128)S(1)} %get-tuple-element.96), channel_id=1, source_target_pairs={{0,4},{1,5},{2,6},{3,7},{4,0},{5,1},{6,2},{7,3},{8,13},{9,12},{10,... | collective-permute-start | bytes 417800 | tf_op jit(solution)/shard_map/ppermute | solution.py:554
  73.3 3.7 %collective-permute-done.18.received.refs_1_.refs_3_ = f32[136,256]{1,0:T(8,128)S(1)} collective-permute-done((f32[136,256]{1,0:T(8,128)S(1)}, f32[136,256]{1,0:T(8,128)S(1)}, u32[]{:S(2)}, u32[]{:S(2)}) %collective-permute-start.18) | collective-permute-done | bytes 139296 | tf_op jit(solution)/shard_map/ppermute | solution.py:554
  77.0 0.9 collective-permute-start.19
  78.7 1.6 %collective-permute-start.28 = (f32[32,256]{1,0:T(8,128)S(1)}, f32[32,256]{1,0:T(8,128)S(1)}, u32[]{:S(2)}, u32[]{:S(2)}) collective-permute-start(f32[32,256]{1,0:T(8,128)S(1)} %get-tuple-element.101), channel_id=1, source_target_pairs={{0,4},{1,5},{2,6},{3,7},{4,0},{5,1},{6,2},{7,3},{8,13},{9,12},{10,... | collective-permute-start | bytes 98312 | tf_op jit(solution)/shard_map/ppermute | solution.py:554
  80.3 1.7 %collective-permute-done.28.received.refs_5_ = f32[32,256]{1,0:T(8,128)S(1)} collective-permute-done((f32[32,256]{1,0:T(8,128)S(1)}, f32[32,256]{1,0:T(8,128)S(1)}, u32[]{:S(2)}, u32[]{:S(2)}) %collective-permute-start.28) | collective-permute-done | bytes 32800 | tf_op jit(solution)/shard_map/ppermute | solution.py:554
  83.9 1.1 collective-permute-done.29.refs_1_
  85.1 8.3 %collective-permute-start.30 = (f32[1,4,16,256]{3,2,1,0:T(8,128)S(1)}, f32[1,4,16,256]{3,2,1,0:T(8,128)S(1)}, u32[]{:S(2)}, u32[]{:S(2)}) collective-permute-start(f32[1,4,16,256]{3,2,1,0:T(8,128)S(1)} %get-tuple-element.116), channel_id=1, source_target_pairs={{0,1},{1,0},{2,3},{3,2},{4,5},{5,4},{6,7},{7,6},{8,9},{9,8},{10,11... | collective-permute-start | bytes 196616 | tf_op jit(solution)/shard_map/ppermute | solution.py:577
  93.4 1.0 collective-permute-start.34
  94.4 1.7 %collective-permute-start.36 = (f32[1,6,16,256]{3,2,1,0:T(8,128)S(1)}, f32[1,6,16,256]{3,2,1,0:T(8,128)S(1)}, u32[]{:S(2)}, u32[]{:S(2)}) collective-permute-start(f32[1,6,16,256]{3,2,1,0:T(8,128)S(1)} %get-tuple-element.139), channel_id=1, source_target_pairs={{0,1},{1,0},{2,3},{3,2},{4,5},{5,4},{6,7},{7,6},{8,9},{9,8},{10,11... | collective-permute-start | bytes 294920 | tf_op jit(solution)/shard_map/ppermute | solution.py:577
  96.1 0.8 shard_map.71
  96.9 0.9 collective-permute-done.34.refs_1_.refs_0_
  97.8 0.8 shard_map.72
  98.6 1.3 %collective-permute-done.36.refs_1_ = f32[1,6,16,256]{3,2,1,0:T(8,128)S(1)} collective-permute-done((f32[1,6,16,256]{3,2,1,0:T(8,128)S(1)}, f32[1,6,16,256]{3,2,1,0:T(8,128)S(1)}, u32[]{:S(2)}, u32[]{:S(2)}) %collective-permute-start.36) | collective-permute-done | bytes 98336 | tf_op jit(solution)/shard_map/ppermute | solution.py:577
  99.9 0.9 shard_map.73
  101.5 1.0 collective-permute-start.37
  103.3 1.0 collective-permute-start.33
  105.0 4.8 %collective-permute-done.33.refs_0_ = f32[1,2,16,256]{3,2,1,0:T(8,128)S(1)} collective-permute-done((f32[1,2,16,256]{3,2,1,0:T(8,128)S(1)}, f32[1,2,16,256]{3,2,1,0:T(8,128)S(1)}, u32[]{:S(2)}, u32[]{:S(2)}) %collective-permute-start.33) | collective-permute-done | bytes 32800 | tf_op jit(solution)/shard_map/ppermute | solution.py:605
  (71 shorter events, 12.0 us)
Async XLA Ops:
  0.0 1.0 copy-start
  1.0 5.2 %copy-start.1 = (f32[4,256]{1,0:T(4,128)S(1)}, f32[4,256]{1,0:T(4,128)}, u32[]{:S(2)}) copy-start(f32[4,256]{1,0:T(4,128)} %refs_2_.5) | copy-start | bytes 12292
  1.0 5.2 %copy-start.2 = (f32[4,256]{1,0:T(4,128)S(1)}, f32[4,256]{1,0:T(4,128)}, u32[]{:S(2)}) copy-start(f32[4,256]{1,0:T(4,128)} %refs_3_.15) | copy-start | bytes 12292
  1.2 5.1 %collective-permute-start = (f32[2,16,16,256]{3,2,1,0:T(8,128)S(1)}, f32[2,16,16,256]{3,2,1,0:T(8,128)S(1)}, u32[]{:S(2)}, u32[]{:S(2)}) collective-permute-start(f32[2,16,16,256]{3,2,1,0:T(8,128)S(1)} %get-tuple-element.75.refs_0_.refs_5_), channel_id=1, source_target_pairs={{0,1},{1,0},{2,3},{3,2},{4,5},{5,4},{6,7},{7,6},{8,9},{9,8},{10,11... | collective-permute-start | bytes 1572872 | tf_op jit(solution)/shard_map/ppermute | solution.py:506
  1.2 3.3 %collective-permute-start.1 = (f32[2,256]{1,0:T(2,128)S(1)}, f32[2,256]{1,0:T(2,128)S(1)}, u32[]{:S(2)}, u32[]{:S(2)}) collective-permute-start(f32[2,256]{1,0:T(2,128)S(1)} %get-tuple-element.76.refs_0_.refs_5_.refs_6_), channel_id=1, source_target_pairs={{0,1},{1,0},{2,3},{3,2},{4,5},{5,4},{6,7},{7,6},{8,9},{9,8},{10,11... | collective-permute-start | bytes 6152 | tf_op jit(solution)/shard_map/ppermute | solution.py:480
  1.7 3.6 %collective-permute-start.2 = (f32[2,256]{1,0:T(2,128)S(1)}, f32[2,256]{1,0:T(2,128)S(1)}, u32[]{:S(2)}, u32[]{:S(2)}) collective-permute-start(f32[2,256]{1,0:T(2,128)S(1)} %get-tuple-element.76.refs_0_.refs_5_.refs_6_), channel_id=1, source_target_pairs={{0,2},{1,3},{2,0},{3,1},{4,6},{5,7},{6,4},{7,5},{8,10},{9,11},{10,... | collective-permute-start | bytes 6152 | tf_op jit(solution)/shard_map/ppermute | solution.py:480
  3.2 3.0 %collective-permute-start.3 = (f32[2,256]{1,0:T(2,128)S(1)}, f32[2,256]{1,0:T(2,128)S(1)}, u32[]{:S(2)}, u32[]{:S(2)}) collective-permute-start(f32[2,256]{1,0:T(2,128)S(1)} %get-tuple-element.76.refs_0_.refs_5_.refs_6_), channel_id=1, source_target_pairs={{0,3},{1,2},{2,1},{3,0},{4,7},{5,6},{6,5},{7,4},{8,11},{9,10},{10,... | collective-permute-start | bytes 6152 | tf_op jit(solution)/shard_map/ppermute | solution.py:480
  7.7 3.1 %collective-permute-start.4 = (f32[2,256]{1,0:T(2,128)S(1)}, f32[2,256]{1,0:T(2,128)S(1)}, u32[]{:S(2)}, u32[]{:S(2)}) collective-permute-start(f32[2,256]{1,0:T(2,128)S(1)} %get-tuple-element.79.refs_0_.refs_5_), channel_id=1, source_target_pairs={{0,3},{1,2},{2,1},{3,0},{4,7},{5,6},{6,5},{7,4},{8,11},{9,10},{10,... | collective-permute-start | bytes 6152 | tf_op jit(solution)/shard_map/ppermute | solution.py:480
  12.3 3.1 %collective-permute-start.5 = (f32[2,256]{1,0:T(2,128)S(1)}, f32[2,256]{1,0:T(2,128)S(1)}, u32[]{:S(2)}, u32[]{:S(2)}) collective-permute-start(f32[2,256]{1,0:T(2,128)S(1)} %get-tuple-element.82.refs_5_), channel_id=1, source_target_pairs={{0,3},{1,2},{2,1},{3,0},{4,7},{5,6},{6,5},{7,4},{8,11},{9,10},{10,... | collective-permute-start | bytes 6152 | tf_op jit(solution)/shard_map/ppermute | solution.py:480
  16.8 3.1 %collective-permute-start.6 = (f32[2,256]{1,0:T(2,128)S(1)}, f32[2,256]{1,0:T(2,128)S(1)}, u32[]{:S(2)}, u32[]{:S(2)}) collective-permute-start(f32[2,256]{1,0:T(2,128)S(1)} %get-tuple-element.84.refs_4_), channel_id=1, source_target_pairs={{0,3},{1,2},{2,1},{3,0},{4,7},{5,6},{6,5},{7,4},{8,11},{9,10},{10,... | collective-permute-start | bytes 6152 | tf_op jit(solution)/shard_map/ppermute | solution.py:480
  20.7 30.4 %collective-permute-start.7 = (f32[2,16,16,256]{3,2,1,0:T(8,128)S(1)}, f32[2,16,16,256]{3,2,1,0:T(8,128)S(1)}, u32[]{:S(2)}, u32[]{:S(2)}) collective-permute-start(f32[2,16,16,256]{3,2,1,0:T(8,128)S(1)} %get-tuple-element.85), channel_id=1, source_target_pairs={{0,4},{4,8},{8,12},{12,16},{16,20},{20,24},{24,28},{1,5},{5,9},{9,... | collective-permute-start | bytes 1572872 | tf_op jit(solution)/shard_map/ppermute | solution.py:522
  25.2 29.5 %collective-permute-start.21 = (f32[720,256]{1,0:T(8,128)S(1)}, f32[720,256]{1,0:T(8,128)S(1)}, u32[]{:S(2)}, u32[]{:S(2)}) collective-permute-start(f32[720,256]{1,0:T(8,128)S(1)} %shard_map.60), channel_id=1, source_target_pairs={{0,4},{4,0},{8,12},{12,8},{16,20},{20,16},{24,28},{28,24},{1,5},{5... | collective-permute-start | bytes 2211848 | tf_op jit(solution)/shard_map/ppermute | solution.py:507
  25.3 3.1 %collective-permute-start.10 = (f32[2,256]{1,0:T(2,128)S(1)}, f32[2,256]{1,0:T(2,128)S(1)}, u32[]{:S(2)}, u32[]{:S(2)}) collective-permute-start(f32[2,256]{1,0:T(2,128)S(1)} %get-tuple-element.86), channel_id=1, source_target_pairs={{0,3},{1,2},{2,1},{3,0},{4,7},{5,6},{6,5},{7,4},{8,11},{9,10},{10,... | collective-permute-start | bytes 6152 | tf_op jit(solution)/shard_map/ppermute | solution.py:480
  25.9 2.5 %collective-permute-start.8 = (f32[2,256]{1,0:T(2,128)S(1)}, f32[2,256]{1,0:T(2,128)S(1)}, u32[]{:S(2)}, u32[]{:S(2)}) collective-permute-start(f32[2,256]{1,0:T(2,128)S(1)} %get-tuple-element.86), channel_id=1, source_target_pairs={{0,1},{1,0},{2,3},{3,2},{4,5},{5,4},{6,7},{7,6},{8,9},{9,8},{10,11... | collective-permute-start | bytes 6152 | tf_op jit(solution)/shard_map/ppermute | solution.py:480
  26.1 3.6 %collective-permute-start.9 = (f32[2,256]{1,0:T(2,128)S(1)}, f32[2,256]{1,0:T(2,128)S(1)}, u32[]{:S(2)}, u32[]{:S(2)}) collective-permute-start(f32[2,256]{1,0:T(2,128)S(1)} %get-tuple-element.86), channel_id=1, source_target_pairs={{0,2},{1,3},{2,0},{3,1},{4,6},{5,7},{6,4},{7,5},{8,10},{9,11},{10,... | collective-permute-start | bytes 6152 | tf_op jit(solution)/shard_map/ppermute | solution.py:480
  29.7 21.5 %collective-permute-start.11 = (f32[2,256]{1,0:T(2,128)S(1)}, f32[2,256]{1,0:T(2,128)S(1)}, u32[]{:S(2)}, u32[]{:S(2)}) collective-permute-start(f32[2,256]{1,0:T(2,128)S(1)} %add_add_fusion), channel_id=1, source_target_pairs={{0,4},{4,8},{8,12},{12,16},{16,20},{20,24},{24,28},{1,5},{5,9},{9,... | collective-permute-start | bytes 6152 | tf_op jit(solution)/shard_map/ppermute | solution.py:523
  52.0 7.9 %collective-permute-start.12 = (f32[2,16,16,256]{3,2,1,0:T(8,128)S(1)}, f32[2,16,16,256]{3,2,1,0:T(8,128)S(1)}, u32[]{:S(2)}, u32[]{:S(2)}) collective-permute-start(f32[2,16,16,256]{3,2,1,0:T(8,128)S(1)} %get-tuple-element.87.refs_0_), channel_id=1, source_target_pairs={{0,1},{1,0},{2,3},{3,2},{4,5},{5,4},{6,7},{7,6},{8,9},{9,8},{10,11... | collective-permute-start | bytes 1572872 | tf_op jit(solution)/shard_map/ppermute | solution.py:529
  52.2 13.4 %collective-permute-start.22 = (f32[432,256]{1,0:T(8,128)S(1)}, f32[432,256]{1,0:T(8,128)S(1)}, u32[]{:S(2)}, u32[]{:S(2)}) collective-permute-start(f32[432,256]{1,0:T(8,128)S(1)} %shard_map.61), channel_id=1, source_target_pairs={{0,4},{4,0},{8,12},{12,8},{16,20},{20,16},{24,28},{28,24},{1,5},{5... | collective-permute-start | bytes 1327112 | tf_op jit(solution)/shard_map/ppermute | solution.py:530
  54.7 27.7 %collective-permute-start.23 = (f32[720,256]{1,0:T(8,128)S(1)}, f32[720,256]{1,0:T(8,128)S(1)}, u32[]{:S(2)}, u32[]{:S(2)}) collective-permute-start(f32[720,256]{1,0:T(8,128)S(1)} %collective-permute-done.21.near_upper), channel_id=1, source_target_pairs={{0,1},{1,0},{2,3},{3,2},{4,5},{5,4},{6,7},{7,6},{8,9},{9,8},{10,11... | collective-permute-start | bytes 2211848 | tf_op jit(solution)/shard_map/ppermute | solution.py:531
  54.9 2.0 %collective-permute-start.13 = (f32[2,256]{1,0:T(2,128)S(1)}, f32[2,256]{1,0:T(2,128)S(1)}, u32[]{:S(2)}, u32[]{:S(2)}) collective-permute-start(f32[2,256]{1,0:T(2,128)S(1)} %get-tuple-element.88.refs_0_), channel_id=1, source_target_pairs={{0,1},{1,0},{2,3},{3,2},{4,5},{5,4},{6,7},{7,6},{8,9},{9,8},{10,11... | collective-permute-start | bytes 6152 | tf_op jit(solution)/shard_map/ppermute | solution.py:480
  55.2 3.6 %collective-permute-start.14 = (f32[2,256]{1,0:T(2,128)S(1)}, f32[2,256]{1,0:T(2,128)S(1)}, u32[]{:S(2)}, u32[]{:S(2)}) collective-permute-start(f32[2,256]{1,0:T(2,128)S(1)} %get-tuple-element.88.refs_0_), channel_id=1, source_target_pairs={{0,2},{1,3},{2,0},{3,1},{4,6},{5,7},{6,4},{7,5},{8,10},{9,11},{10,... | collective-permute-start | bytes 6152 | tf_op jit(solution)/shard_map/ppermute | solution.py:480
  56.9 3.0 %collective-permute-start.15 = (f32[2,256]{1,0:T(2,128)S(1)}, f32[2,256]{1,0:T(2,128)S(1)}, u32[]{:S(2)}, u32[]{:S(2)}) collective-permute-start(f32[2,256]{1,0:T(2,128)S(1)} %get-tuple-element.88.refs_0_), channel_id=1, source_target_pairs={{0,3},{1,2},{2,1},{3,0},{4,7},{5,6},{6,5},{7,4},{8,11},{9,10},{10,... | collective-permute-start | bytes 6152 | tf_op jit(solution)/shard_map/ppermute | solution.py:480
  61.4 4.1 %collective-permute-start.16 = (f32[2,256]{1,0:T(2,128)S(1)}, f32[2,256]{1,0:T(2,128)S(1)}, u32[]{:S(2)}, u32[]{:S(2)}) collective-permute-start(f32[2,256]{1,0:T(2,128)S(1)} %get-tuple-element.91.refs_5_), channel_id=1, source_target_pairs={{0,3},{1,2},{2,1},{3,0},{4,7},{5,6},{6,5},{7,4},{8,11},{9,10},{10,... | collective-permute-start | bytes 6152 | tf_op jit(solution)/shard_map/ppermute | solution.py:480
  65.5 16.9 %collective-permute-start.24 = (f32[432,256]{1,0:T(8,128)S(1)}, f32[432,256]{1,0:T(8,128)S(1)}, u32[]{:S(2)}, u32[]{:S(2)}) collective-permute-start(f32[432,256]{1,0:T(8,128)S(1)} %collective-permute-done.22.near_lower), channel_id=1, source_target_pairs={{0,1},{1,0},{2,3},{3,2},{4,5},{5,4},{6,7},{7,6},{8,9},{9,8},{10,11... | collective-permute-start | bytes 1327112 | tf_op jit(solution)/shard_map/ppermute | solution.py:537
  67.0 3.1 %collective-permute-start.17 = (f32[2,256]{1,0:T(2,128)S(1)}, f32[2,256]{1,0:T(2,128)S(1)}, u32[]{:S(2)}, u32[]{:S(2)}) collective-permute-start(f32[2,256]{1,0:T(2,128)S(1)} %get-tuple-element.93.refs_0_), channel_id=1, source_target_pairs={{0,3},{1,2},{2,1},{3,0},{4,7},{5,6},{6,5},{7,4},{8,11},{9,10},{10,... | collective-permute-start | bytes 6152 | tf_op jit(solution)/shard_map/ppermute | solution.py:480
  71.0 6.0 %collective-permute-start.18 = (f32[136,256]{1,0:T(8,128)S(1)}, f32[136,256]{1,0:T(8,128)S(1)}, u32[]{:S(2)}, u32[]{:S(2)}) collective-permute-start(f32[136,256]{1,0:T(8,128)S(1)} %get-tuple-element.96), channel_id=1, source_target_pairs={{0,4},{1,5},{2,6},{3,7},{4,0},{5,1},{6,2},{7,3},{8,13},{9,12},{10,... | collective-permute-start | bytes 417800 | tf_op jit(solution)/shard_map/ppermute | solution.py:554
  72.9 9.7 %collective-permute-start.20 = (f32[1,256,256]{2,1,0:T(8,128)S(1)}, f32[1,256,256]{2,1,0:T(8,128)S(1)}, u32[]{:S(2)}, u32[]{:S(2)}) collective-permute-start(f32[1,256,256]{2,1,0:T(8,128)S(1)} %get-tuple-element.98.refs_2_.refs_5_.refs_6_), channel_id=1, source_target_pairs={{0,1},{1,0},{2,3},{3,2},{4,5},{5,4},{6,7},{7,6},{8,9},{9,8},{10,11... | collective-permute-start | bytes 786440 | tf_op jit(solution)/shard_map/ppermute | solution.py:555
  72.9 5.8 %collective-permute-start.26 = (f32[96,256]{1,0:T(8,128)S(1)}, f32[96,256]{1,0:T(8,128)S(1)}, u32[]{:S(2)}, u32[]{:S(2)}) collective-permute-start(f32[96,256]{1,0:T(8,128)S(1)} %get-tuple-element.100), channel_id=1, source_target_pairs={{0,4},{1,5},{2,6},{3,7},{4,0},{5,1},{6,2},{7,3},{8,13},{9,12},{10,... | collective-permute-start | bytes 294920 | tf_op jit(solution)/shard_map/ppermute | solution.py:554
  77.0 5.7 %collective-permute-start.19 = (f32[1,8,16,256]{3,2,1,0:T(8,128)S(1)}, f32[1,8,16,256]{3,2,1,0:T(8,128)S(1)}, u32[]{:S(2)}, u32[]{:S(2)}) collective-permute-start(f32[1,8,16,256]{3,2,1,0:T(8,128)S(1)} %shard_map.59), channel_id=1, source_target_pairs={{0,9},{1,8},{2,11},{3,10},{4,13},{5,12},{6,15},{7,14},{8,1},{9,0},... | collective-permute-start | bytes 393224 | tf_op jit(solution)/shard_map/ppermute | solution.py:577
  78.7 3.3 %collective-permute-start.28 = (f32[32,256]{1,0:T(8,128)S(1)}, f32[32,256]{1,0:T(8,128)S(1)}, u32[]{:S(2)}, u32[]{:S(2)}) collective-permute-start(f32[32,256]{1,0:T(8,128)S(1)} %get-tuple-element.101), channel_id=1, source_target_pairs={{0,4},{1,5},{2,6},{3,7},{4,0},{5,1},{6,2},{7,3},{8,13},{9,12},{10,... | collective-permute-start | bytes 98312 | tf_op jit(solution)/shard_map/ppermute | solution.py:554
  82.0 1.3 %collective-permute-start.27 = (f32[1,6,16,256]{3,2,1,0:T(8,128)S(1)}, f32[1,6,16,256]{3,2,1,0:T(8,128)S(1)}, u32[]{:S(2)}, u32[]{:S(2)}) collective-permute-start(f32[1,6,16,256]{3,2,1,0:T(8,128)S(1)} %shard_map.64), channel_id=1, source_target_pairs={{0,9},{1,8},{2,11},{3,10},{4,13},{5,12},{6,15},{7,14},{8,1},{9,0},... | collective-permute-start | bytes 294920 | tf_op jit(solution)/shard_map/ppermute | solution.py:577
  83.0 2.1 %collective-permute-start.25 = (f32[1,6,16,256]{3,2,1,0:T(8,128)S(1)}, f32[1,6,16,256]{3,2,1,0:T(8,128)S(1)}, u32[]{:S(2)}, u32[]{:S(2)}) collective-permute-start(f32[1,6,16,256]{3,2,1,0:T(8,128)S(1)} %get-tuple-element.99), channel_id=1, source_target_pairs={{0,1},{1,0},{2,3},{3,2},{4,5},{5,4},{6,7},{7,6},{8,17},{9,16},{10,... | collective-permute-start | bytes 294920 | tf_op jit(solution)/shard_map/ppermute | solution.py:577
  83.4 10.0 %collective-permute-start.31 = (f32[1,6,16,256]{3,2,1,0:T(8,128)S(1)}, f32[1,6,16,256]{3,2,1,0:T(8,128)S(1)}, u32[]{:S(2)}, u32[]{:S(2)}) collective-permute-start(f32[1,6,16,256]{3,2,1,0:T(8,128)S(1)} %get-tuple-element.117), channel_id=1, source_target_pairs={{0,1},{1,0},{2,3},{3,2},{4,5},{5,4},{6,7},{7,6},{8,17},{9,16},{10,... | collective-permute-start | bytes 294920 | tf_op jit(solution)/shard_map/ppermute | solution.py:577
  83.7 1.2 %collective-permute-start.29 = (f32[1,2,16,256]{3,2,1,0:T(8,128)S(1)}, f32[1,2,16,256]{3,2,1,0:T(8,128)S(1)}, u32[]{:S(2)}, u32[]{:S(2)}) collective-permute-start(f32[1,2,16,256]{3,2,1,0:T(8,128)S(1)} %shard_map.65), channel_id=1, source_target_pairs={{0,9},{1,8},{2,11},{3,10},{4,13},{5,12},{6,15},{7,14},{8,1},{9,0},... | collective-permute-start | bytes 98312 | tf_op jit(solution)/shard_map/ppermute | solution.py:577
  84.9 9.4 %collective-permute-start.32 = (f32[1,4,16,256]{3,2,1,0:T(8,128)S(1)}, f32[1,4,16,256]{3,2,1,0:T(8,128)S(1)}, u32[]{:S(2)}, u32[]{:S(2)}) collective-permute-start(f32[1,4,16,256]{3,2,1,0:T(8,128)S(1)} %get-tuple-element.118), channel_id=1, source_target_pairs={{0,1},{1,0},{2,3},{3,2},{4,5},{5,4},{6,7},{7,6},{8,17},{9,16},{10,... | collective-permute-start | bytes 196616 | tf_op jit(solution)/shard_map/ppermute | solution.py:577
  85.1 11.0 %collective-permute-start.30 = (f32[1,4,16,256]{3,2,1,0:T(8,128)S(1)}, f32[1,4,16,256]{3,2,1,0:T(8,128)S(1)}, u32[]{:S(2)}, u32[]{:S(2)}) collective-permute-start(f32[1,4,16,256]{3,2,1,0:T(8,128)S(1)} %get-tuple-element.116), channel_id=1, source_target_pairs={{0,1},{1,0},{2,3},{3,2},{4,5},{5,4},{6,7},{7,6},{8,9},{9,8},{10,11... | collective-permute-start | bytes 196616 | tf_op jit(solution)/shard_map/ppermute | solution.py:577
  93.4 4.4 %collective-permute-start.34 = (f32[1,6,16,256]{3,2,1,0:T(8,128)S(1)}, f32[1,6,16,256]{3,2,1,0:T(8,128)S(1)}, u32[]{:S(2)}, u32[]{:S(2)}) collective-permute-start(f32[1,6,16,256]{3,2,1,0:T(8,128)S(1)} %get-tuple-element.133), channel_id=1, source_target_pairs={{0,1},{1,0},{2,3},{3,2},{4,5},{5,4},{6,7},{7,6},{8,9},{9,8},{10,11... | collective-permute-start | bytes 294920 | tf_op jit(solution)/shard_map/ppermute | solution.py:577
  94.4 5.5 %collective-permute-start.36 = (f32[1,6,16,256]{3,2,1,0:T(8,128)S(1)}, f32[1,6,16,256]{3,2,1,0:T(8,128)S(1)}, u32[]{:S(2)}, u32[]{:S(2)}) collective-permute-start(f32[1,6,16,256]{3,2,1,0:T(8,128)S(1)} %get-tuple-element.139), channel_id=1, source_target_pairs={{0,1},{1,0},{2,3},{3,2},{4,5},{5,4},{6,7},{7,6},{8,9},{9,8},{10,11... | collective-permute-start | bytes 294920 | tf_op jit(solution)/shard_map/ppermute | solution.py:577
  100.7 3.6 %collective-permute-start.38 = (f32[1,16,16,256]{3,2,1,0:T(8,128)S(1)}, f32[1,16,16,256]{3,2,1,0:T(8,128)S(1)}, u32[]{:S(2)}, u32[]{:S(2)}) collective-permute-start(f32[1,16,16,256]{3,2,1,0:T(8,128)S(1)} %get-tuple-element.144.own), channel_id=1, source_target_pairs={{0,1},{1,0},{2,3},{3,2},{4,5},{5,4},{6,7},{7,6},{8,9},{9,8},{10,11... | collective-permute-start | bytes 786440 | tf_op jit(solution)/shard_map/ppermute | solution.py:612
  101.5 8.3 %collective-permute-start.37 = (f32[1,8,16,256]{3,2,1,0:T(8,128)S(1)}, f32[1,8,16,256]{3,2,1,0:T(8,128)S(1)}, u32[]{:S(2)}, u32[]{:S(2)}) collective-permute-start(f32[1,8,16,256]{3,2,1,0:T(8,128)S(1)} %get-tuple-element.143), channel_id=1, source_target_pairs={{0,1},{1,0},{2,3},{3,2},{4,5},{5,4},{6,7},{7,6},{8,13},{9,12},{10,... | collective-permute-start | bytes 393224 | tf_op jit(solution)/shard_map/ppermute | solution.py:605
  102.5 7.3 %collective-permute-start.35 = (f32[1,6,16,256]{3,2,1,0:T(8,128)S(1)}, f32[1,6,16,256]{3,2,1,0:T(8,128)S(1)}, u32[]{:S(2)}, u32[]{:S(2)}) collective-permute-start(f32[1,6,16,256]{3,2,1,0:T(8,128)S(1)} %get-tuple-element.138), channel_id=1, source_target_pairs={{0,1},{1,0},{2,3},{3,2},{4,5},{5,4},{6,7},{7,6},{8,13},{9,12},{10,... | collective-permute-start | bytes 294920 | tf_op jit(solution)/shard_map/ppermute | solution.py:605
  103.3 6.6 %collective-permute-start.33 = (f32[1,2,16,256]{3,2,1,0:T(8,128)S(1)}, f32[1,2,16,256]{3,2,1,0:T(8,128)S(1)}, u32[]{:S(2)}, u32[]{:S(2)}) collective-permute-start(f32[1,2,16,256]{3,2,1,0:T(8,128)S(1)} %get-tuple-element.132), channel_id=1, source_target_pairs={{0,1},{1,0},{2,3},{3,2},{4,5},{5,4},{6,7},{7,6},{8,13},{9,12},{10,... | collective-permute-start | bytes 98312 | tf_op jit(solution)/shard_map/ppermute | solution.py:605
